TPU v7x, 32 devices: a whole 2x2x4 slice. The times are simulated.
32 devices in a mesh: sweep: 4 (over x, core), bulk: 8 (over z, y).
Axes of the slice: x: 2, y: 2, z: 4, core: 2. Of those that a mesh axis runs over, the one named last changes fastest.
Arguments:
- source: float32 [128, 5, 128, 128], P('sweep', None, 'bulk'), may hold values from -6 to 6
- psi_old: float32 [128, 5, 128, 128], P('sweep', None, 'bulk'), may hold values from -6 to 6
- lateral: float32 [128, 2, 128, 128], P('sweep', None, 'bulk'), may hold values from 0.1 to 0.6
- lower_jac: float32 [128, 5, 5, 128, 128], P('sweep', None, None, 'bulk')
- upper_jac: float32 [128, 5, 5, 128, 128], P('sweep', None, None, 'bulk')
- diag_inv: float32 [128, 5, 5, 128, 128], P('sweep', None, None, 'bulk')
- face_weight: float32 [5, 65536], P(None, ('sweep', 'bulk')), may hold values from -6 to 6
- face_cell: int32 [65536], P(('sweep', 'bulk')), may hold values from 0 to 65535
- face_owner: int32 [65536, 1], P(('sweep', 'bulk')), may hold values from 0 to 7; in each aligned block of 2048 rows (0 to 2047, 2048 to 4095, ...) at most 512 rows name the same one
- face_node: int32 [65536], P(('sweep', 'bulk')), may hold values from 0 to 16383
- face_count: int32 [32], P(('sweep', 'bulk')), may hold values from 1 to 2048, as said below
Outputs:
- adjoint: float32 [128, 5, 128, 128], P('sweep', None, 'bulk')
- node_sens: float32 [131072], P('bulk')
Inputs may be any that keep to these rules, and one draw needn't show every extreme that they name: `face_owner`: among the 2048 faces of one device no owner appears more than 512 times; some device reaches 512. `face_count`: some device has all 2048 slots live.
All inputs are finite; a program needn't handle non-finite values.
Results may differ from a plain program's by a relative error of at most 0.00011.
Values sent between devices are 32-bit elements; how exact they have to be, the bound alone decides.
No kernel may reach another device: no remote copies, remote signals or barrier semaphores. Data moves between devices by JAX's collectives and lax.ppermute only.
A program may use at most 128 MiB of HBM per device.

v0:
```python
import jax
import jax.numpy as jnp
from jax import lax
from jax.sharding import PartitionSpec as P

NODES_DEV = 16384


def padded_2(value, sides, width):
    for axis, dim in sides:
        size, length = (lax.axis_size(axis), value.shape[dim])
        up = [(i, (i + 1) % size) for i in range(size - 1)]
        down = [(j, i) for i, j in up]
        last = lax.slice_in_dim(value, length - width, length, axis=dim)
        initial = lax.slice_in_dim(value, 0, width, axis=dim)
        before = lax.ppermute(last, axis, up)
        after = lax.ppermute(initial, axis, down)
        value = jnp.concatenate([before, value, after], axis=dim)
    return value


def from_behind(value, axis, by):
    length = lax.axis_size(axis)
    pairs = [(i, i + by) for i in range(length) if 0 <= i + by < length]
    return lax.ppermute(value, axis, pairs)


def matvec(matrix, vector):
    return jnp.sum(matrix * vector[None], axis=1)


def matmat(matrix, other):
    return jnp.sum(matrix[:, :, None] * other[None], axis=1)


def forward_sweep(right_side, lower_jac, diag_inv, start):

    def forward_advance(current, planes):
        rhs_plane, lower_plane, inv_plane = planes
        updated = matvec(inv_plane, rhs_plane - matvec(lower_plane, current))
        return (updated, updated)

    leaving, fields = lax.scan(
        forward_advance, start, (right_side, lower_jac, diag_inv), unroll=True
    )
    return fields


def backward_sweep(forward_field, upper_jac, diag_inv, start):

    def backward_advance(current, planes):
        fwd_plane, upper_plane, inv_plane = planes
        updated = fwd_plane - matvec(inv_plane, matvec(upper_plane, current))
        return (updated, updated)

    leaving, fields = lax.scan(
        backward_advance, start, (forward_field, upper_jac, diag_inv), reverse=True, unroll=True
    )
    return fields


def block_affine(given, coupled, diag_inv, identity, zero_state, backward):

    def block_advance(carry, planes):
        transfer, current = carry
        given_plane, coupled_plane, inv_plane = planes
        transfer = -matmat(inv_plane, matmat(coupled_plane, transfer))
        if backward:
            current = given_plane - matvec(inv_plane, matvec(coupled_plane, current))
        else:
            current = matvec(inv_plane, given_plane - matvec(coupled_plane, current))
        return ((transfer, current), 0)

    result, unused = lax.scan(
        block_advance,
        (identity, zero_state),
        (given, coupled, diag_inv),
        reverse=backward,
        unroll=True,
    )
    return result


def per_device(
    source,
    psi_old,
    lateral,
    lower_jac,
    upper_jac,
    diag_inv,
    face_weight,
    face_cell,
    face_owner,
    face_node,
    face_count,
):
    padded = padded_2(psi_old, (("bulk", 2),), 1)
    right_side = source - lateral[:, 0:1] * padded[:, :, :-2] - lateral[:, 1:2] * padded[:, :, 2:]
    zero_state = jnp.zeros(source.shape[1:], jnp.float32)
    identity = jnp.broadcast_to(
        jnp.eye(5, dtype=jnp.float32)[:, :, None, None], (5, 5) + source.shape[2:]
    )
    transfer, leaving = block_affine(right_side, lower_jac, diag_inv, identity, zero_state, False)
    boundary = zero_state
    for relay_step in range(lax.axis_size("sweep") - 1):
        boundary = from_behind(matvec(transfer, boundary) + leaving, "sweep", 1)
    forward_field = forward_sweep(right_side, lower_jac, diag_inv, boundary)
    transfer, leaving = block_affine(forward_field, upper_jac, diag_inv, identity, zero_state, True)
    boundary = zero_state
    for relay_step in range(lax.axis_size("sweep") - 1):
        boundary = from_behind(matvec(transfer, boundary) + leaving, "sweep", -1)
    adjoint = backward_sweep(forward_field, upper_jac, diag_inv, boundary)
    width_j = source.shape[2]
    width_k = source.shape[3]
    slots = face_cell.shape[0]
    plane_index = face_cell // (width_j * width_k)
    rest_index = face_cell % (width_j * width_k)
    column_index = rest_index // width_k
    depth_index = rest_index % width_k
    at_faces = adjoint[plane_index, :, column_index, depth_index]
    partial_value = jnp.sum(at_faces * face_weight.T, axis=1)
    active = jnp.arange(slots, dtype=jnp.int32) < face_count[0]
    partial_value = jnp.where(active, partial_value, jnp.float32(0.0))
    owner_dev = face_owner[:, 0]
    owners = lax.axis_size("bulk")
    dense_sums = jax.ops.segment_sum(
        partial_value, owner_dev * NODES_DEV + face_node, num_segments=NODES_DEV * owners
    )
    summed = lax.psum(dense_sums, ("sweep", "bulk"))
    node_sens = lax.dynamic_slice_in_dim(summed, lax.axis_index("bulk") * NODES_DEV, NODES_DEV)
    return (adjoint, node_sens)


def solution(mesh):
    placed = (
        P("sweep", None, "bulk", None),
        P("sweep", None, "bulk", None),
        P("sweep", None, "bulk", None),
        P("sweep", None, None, "bulk", None),
        P("sweep", None, None, "bulk", None),
        P("sweep", None, None, "bulk", None),
        P(None, ("sweep", "bulk")),
        P(("sweep", "bulk")),
        P(("sweep", "bulk"), None),
        P(("sweep", "bulk")),
        P(("sweep", "bulk")),
    )
    return jax.shard_map(
        per_device,
        mesh=mesh,
        in_specs=placed,
        out_specs=(P("sweep", None, "bulk", None), P("bulk")),
        check_vma=False,
    )
```

profile of v0, /device:TPU:0, one launch (start us, length us, event | category | flops | bytes accessed | tf_op | source)
XLA Modules:
  0.0 318.8 jit_solution(10096926136467632355)
XLA Ops:
  7.2 1.6 fusion.88
  8.8 5.0 %collective-permute-start = (f32[32,5,1,128]{3,0,2,1:T(8,128)S(1)}, f32[32,5,1,128]{3,0,2,1:T(8,128)S(1)}, u32[]{:S(2)}, u32[]{:S(2)}) collective-permute-start(f32[32,5,1,128]{3,0,2,1:T(8,128)S(1)} %copy.123), channel_id=1, source_target_pairs={{0,1},{1,2},{2,3},{3,4},{4,5},{5,6},{6,7},{8,9},{9,10},{10,11},{11... | collective-permute-start | bytes 245768 | tf_op jit(solution)/shard_map/ppermute | solution.py:16
  13.8 1.3 collective-permute-start.1
  16.1 2.0 slice_bitcast_fusion.92
  18.1 2.1 slice_bitcast_fusion.32
  21.2 1.0 slice-done.1
  22.7 1.6 slice-done.4
  41.3 1.5 collective-permute-start.2
  43.6 4.2 %collective-permute-start.3 = (f32[5,16,128]{2,1,0:T(8,128)S(1)}, f32[5,16,128]{2,1,0:T(8,128)S(1)}, u32[]{:S(2)}, u32[]{:S(2)}) collective-permute-start(f32[5,16,128]{2,1,0:T(8,128)S(1)} %add.57), channel_id=1, source_target_pairs={{0,8},{8,16},{16,24},{1,9},{9,17},{17,25},{2,10},{10,18},{18,26},{... | collective-permute-start | bytes 122888 | tf_op jit(solution)/shard_map/ppermute | solution.py:25
  48.7 4.5 %collective-permute-start.4 = (f32[5,16,128]{2,1,0:T(8,128)S(1)}, f32[5,16,128]{2,1,0:T(8,128)S(1)}, u32[]{:S(2)}, u32[]{:S(2)}) collective-permute-start(f32[5,16,128]{2,1,0:T(8,128)S(1)} %add.58), channel_id=1, source_target_pairs={{0,8},{8,16},{16,24},{1,9},{9,17},{17,25},{2,10},{10,18},{18,26},{... | collective-permute-start | bytes 122888 | tf_op jit(solution)/shard_map/ppermute | solution.py:25
  58.9 1.4 collective-permute-start.5
  60.4 3.9 %collective-permute-done.5 = f32[5,16,128]{2,1,0:T(8,128)S(1)} collective-permute-done((f32[5,16,128]{2,1,0:T(8,128)S(1)}, f32[5,16,128]{2,1,0:T(8,128)S(1)}, u32[]{:S(2)}, u32[]{:S(2)}) %collective-permute-start.5) | collective-permute-done | bytes 40992 | tf_op jit(solution)/shard_map/ppermute | solution.py:25
  64.3 1.3 collective-permute-start.6
  65.6 4.6 %collective-permute-done.6 = f32[5,16,128]{2,1,0:T(8,128)S(1)} collective-permute-done((f32[5,16,128]{2,1,0:T(8,128)S(1)}, f32[5,16,128]{2,1,0:T(8,128)S(1)}, u32[]{:S(2)}, u32[]{:S(2)}) %collective-permute-start.6) | collective-permute-done | bytes 40992 | tf_op jit(solution)/shard_map/ppermute | solution.py:25
  70.8 1.5 collective-permute-start.7
  72.4 1.2 copy.122
  75.0 1.5 collective-permute-done.7
  76.5 1.0 multiply_reduce_fusion.191
  77.5 1.1 multiply_reduce_fusion.190
  78.6 1.0 sub.1037
  79.6 1.0 multiply_reduce_fusion.189
  80.6 1.0 multiply_reduce_fusion.188
  82.3 1.0 multiply_reduce_fusion.187
  83.3 1.0 multiply_reduce_fusion.186
  85.1 1.0 multiply_reduce_fusion.185
  86.0 1.0 multiply_reduce_fusion.184
  87.8 1.0 multiply_reduce_fusion.183
  88.7 1.0 multiply_reduce_fusion.182
  90.5 1.0 multiply_reduce_fusion.181
  91.5 1.0 multiply_reduce_fusion.180
  93.2 1.0 multiply_reduce_fusion.179
  94.2 1.0 multiply_reduce_fusion.178
  95.9 1.0 multiply_reduce_fusion.177
  96.9 1.0 multiply_reduce_fusion.176
  98.7 1.0 multiply_reduce_fusion.175
  99.6 1.0 multiply_reduce_fusion.174
  101.4 1.0 multiply_reduce_fusion.173
  102.3 1.0 multiply_reduce_fusion.172
  103.3 1.0 multiply_reduce_fusion.171
  104.3 1.0 multiply_reduce_fusion.170
  105.3 1.0 multiply_reduce_fusion.169
  106.3 1.0 multiply_reduce_fusion.167
  107.3 1.0 multiply_reduce_fusion.165
  108.3 1.0 multiply_reduce_fusion.163
  109.3 1.0 multiply_reduce_fusion.161
  110.4 1.0 multiply_reduce_fusion.159
  111.4 1.0 multiply_reduce_fusion.157
  112.4 1.0 multiply_reduce_fusion.155
  113.4 1.0 multiply_reduce_fusion.153
  115.4 1.0 multiply_reduce_fusion.149
  116.4 1.0 multiply_reduce_fusion.147
  117.4 1.0 multiply_reduce_fusion.145
  118.4 1.0 multiply_reduce_fusion.143
  119.4 1.0 multiply_reduce_fusion.141
  120.4 1.0 multiply_reduce_fusion.139
  121.5 1.0 multiply_reduce_fusion.137
  122.5 1.0 multiply_reduce_fusion.135
  123.5 1.0 multiply_reduce_fusion.133
  124.5 1.0 multiply_reduce_fusion.131
  126.9 16.5 %copy.121 = f32[32,5,16,128]{1,3,2,0:T(8,128)} copy(f32[32,5,16,128]{3,2,1,0:T(8,128)S(1)} %constant_dynamic-update-slice_fusion) | data formatting | bytes 2621440 | tf_op jit(solution)/shard_map/concatenate | solution.py:56
  143.4 22.1 %gather_fusion = f32[2048,5]{1,0:T(8,128)S(1)} fusion(f32[32,5,16,128]{1,3,2,0:T(8,128)} %copy.121, s32[2048]{0:T(1024)S(1)} %fusion.74), kind=kCustom, calls=%fused_computation | custom fusion | bytes 106496 | tf_op jit(solution)/shard_map/gather | solution.py:120
  165.9 12.2 %scatter_custom_fusion = f32[131072]{0:T(1024)} fusion(s32[2048]{0:T(1024)} %add.62, f32[2048]{0:T(1024)S(1)} %fusion.81, f32[]{:T(128)} %constant.53.clone.1), kind=kCustom, calls=%fused_computation.138 | custom fusion | flops 2048 | bytes 524800 | tf_op jit(solution)/shard_map/scatter-add | solution.py:126
  178.1 132.3 %all-reduce.2.cloned.1.call-done = f32[131072]{0:T(1024)} async-done(((f32[131072]{0:T(1024)}), f32[131072]{0:T(1024)}) %all-reduce.2.cloned.1.call-update) | async-done | bytes 524304 | tf_op jit(solution)/shard_map/psum | solution.py:129
  310.4 1.5 dynamic_slice.3
  (720 shorter events, 34.4 us)
Async XLA Ops:
  7.2 303.3 %all-reduce.2.cloned.1.call-start = ((), (), s32[]{:S(2)}) async-start(), calls=%async_computation | async-start | bytes 1048576 | tf_op jit(solution)/shard_map/psum | solution.py:129
  7.2 13.0 %copy-start = (f32[32,5,5,16,128]{4,3,2,1,0:T(8,128)S(1)}, f32[32,5,5,16,128]{4,3,2,1,0:T(8,128)}, u32[]{:S(2)}) copy-start(f32[32,5,5,16,128]{4,3,2,1,0:T(8,128)} %param.15) | copy-start | bytes 19660804
  8.8 29.5 %collective-permute-start = (f32[32,5,1,128]{3,0,2,1:T(8,128)S(1)}, f32[32,5,1,128]{3,0,2,1:T(8,128)S(1)}, u32[]{:S(2)}, u32[]{:S(2)}) collective-permute-start(f32[32,5,1,128]{3,0,2,1:T(8,128)S(1)} %copy.123), channel_id=1, source_target_pairs={{0,1},{1,2},{2,3},{3,4},{4,5},{5,6},{6,7},{8,9},{9,10},{10,11},{11... | collective-permute-start | bytes 245768 | tf_op jit(solution)/shard_map/ppermute | solution.py:16
  13.8 24.5 %collective-permute-start.1 = (f32[32,5,1,128]{3,0,2,1:T(8,128)S(1)}, f32[32,5,1,128]{3,0,2,1:T(8,128)S(1)}, u32[]{:S(2)}, u32[]{:S(2)}) collective-permute-start(f32[32,5,1,128]{3,0,2,1:T(8,128)S(1)} %copy.124), channel_id=1, source_target_pairs={{1,0},{2,1},{3,2},{4,3},{5,4},{6,5},{7,6},{9,8},{10,9},{11,10},{12... | collective-permute-start | bytes 245768 | tf_op jit(solution)/shard_map/ppermute | solution.py:17
  18.1 3.1 slice-start
  20.3 1.9 slice-start.1
  22.2 2.2 slice-start.4
  22.4 2.8 slice-start.5
  22.4 3.1 copy-start.52
  36.5 2.0 copy-start.1
  36.5 2.0 copy-start.3
  41.3 2.3 collective-permute-start.2
  43.6 5.0 %collective-permute-start.3 = (f32[5,16,128]{2,1,0:T(8,128)S(1)}, f32[5,16,128]{2,1,0:T(8,128)S(1)}, u32[]{:S(2)}, u32[]{:S(2)}) collective-permute-start(f32[5,16,128]{2,1,0:T(8,128)S(1)} %add.57), channel_id=1, source_target_pairs={{0,8},{8,16},{16,24},{1,9},{9,17},{17,25},{2,10},{10,18},{18,26},{... | collective-permute-start | bytes 122888 | tf_op jit(solution)/shard_map/ppermute | solution.py:25
  48.7 5.3 %collective-permute-start.4 = (f32[5,16,128]{2,1,0:T(8,128)S(1)}, f32[5,16,128]{2,1,0:T(8,128)S(1)}, u32[]{:S(2)}, u32[]{:S(2)}) collective-permute-start(f32[5,16,128]{2,1,0:T(8,128)S(1)} %add.58), channel_id=1, source_target_pairs={{0,8},{8,16},{16,24},{1,9},{9,17},{17,25},{2,10},{10,18},{18,26},{... | collective-permute-start | bytes 122888 | tf_op jit(solution)/shard_map/ppermute | solution.py:25
  54.3 4.4 %copy-start.4 = (f32[5,16,128]{2,1,0:T(8,128)}, f32[5,16,128]{2,1,0:T(8,128)S(1)}, u32[]{:S(2)}) copy-start(f32[5,16,128]{2,1,0:T(8,128)S(1)} %multiply_reduce_fusion.315) | copy-start | bytes 122884
  54.4 4.2 %copy-start.6 = (f32[5,16,128]{2,1,0:T(8,128)}, f32[5,16,128]{2,1,0:T(8,128)S(1)}, u32[]{:S(2)}) copy-start(f32[5,16,128]{2,1,0:T(8,128)S(1)} %multiply_reduce_fusion.313) | copy-start | bytes 122884
  54.5 4.1 %copy-start.8 = (f32[5,16,128]{2,1,0:T(8,128)}, f32[5,16,128]{2,1,0:T(8,128)S(1)}, u32[]{:S(2)}) copy-start(f32[5,16,128]{2,1,0:T(8,128)S(1)} %multiply_reduce_fusion.311) | copy-start | bytes 122884
  54.5 3.9 %copy-start.10 = (f32[5,16,128]{2,1,0:T(8,128)}, f32[5,16,128]{2,1,0:T(8,128)S(1)}, u32[]{:S(2)}) copy-start(f32[5,16,128]{2,1,0:T(8,128)S(1)} %multiply_reduce_fusion.309) | copy-start | bytes 122884
  54.6 3.8 %copy-start.12 = (f32[5,16,128]{2,1,0:T(8,128)}, f32[5,16,128]{2,1,0:T(8,128)S(1)}, u32[]{:S(2)}) copy-start(f32[5,16,128]{2,1,0:T(8,128)S(1)} %multiply_reduce_fusion.307) | copy-start | bytes 122884
  54.7 3.6 %copy-start.14 = (f32[5,16,128]{2,1,0:T(8,128)}, f32[5,16,128]{2,1,0:T(8,128)S(1)}, u32[]{:S(2)}) copy-start(f32[5,16,128]{2,1,0:T(8,128)S(1)} %multiply_reduce_fusion.305) | copy-start | bytes 122884
  54.8 3.5 %copy-start.16 = (f32[5,16,128]{2,1,0:T(8,128)}, f32[5,16,128]{2,1,0:T(8,128)S(1)}, u32[]{:S(2)}) copy-start(f32[5,16,128]{2,1,0:T(8,128)S(1)} %multiply_reduce_fusion.303) | copy-start | bytes 122884
  54.9 3.3 %copy-start.18 = (f32[5,16,128]{2,1,0:T(8,128)}, f32[5,16,128]{2,1,0:T(8,128)S(1)}, u32[]{:S(2)}) copy-start(f32[5,16,128]{2,1,0:T(8,128)S(1)} %multiply_reduce_fusion.301) | copy-start | bytes 122884
  54.9 3.1 copy-start.20
  55.0 3.0 copy-start.22
  55.1 2.8 copy-start.24
  55.2 2.6 copy-start.26
  55.2 2.5 copy-start.28
  55.3 2.3 copy-start.30
  55.4 2.1 copy-start.32
  55.5 2.0 copy-start.34
  55.6 1.8 copy-start.36
  55.6 1.6 copy-start.38
  56.3 1.5 copy-start.50
  56.4 1.5 copy-start.51
  56.5 1.5 copy-start.53
  57.4 8.1 %copy-start.55 = (s32[2048,1]{0,1:T(1,128)S(1)}, s32[2048,1]{0,1:T(1,128)}, u32[]{:S(2)}) copy-start(s32[2048,1]{0,1:T(1,128)} %param.19) | copy-start | bytes 24580
  57.5 14.9 %copy-start.56 = (s32[2048]{0:T(1024)S(1)}, s32[2048]{0:T(1024)}, u32[]{:S(2)}) copy-start(s32[2048]{0:T(1024)} %param.18) | copy-start | bytes 24580
  57.7 16.8 %copy-start.54 = (s32[2048]{0:T(1024)S(1)}, s32[2048]{0:T(1024)}, u32[]{:S(2)}) copy-start(s32[2048]{0:T(1024)} %param.20) | copy-start | bytes 24580
  58.4 47.8 %slice-start.2 = ((s8[6553600]{0:T(1024)(128)(4,1)}), s8[2359296]{0:T(1024)(128)(4,1)S(1)}, s32[]{:S(2)}) async-start(s8[6553600]{0:T(1024)(128)(4,1)} %bitcast.1165), calls=%async_computation.3 | async-start | bytes 4718592
  58.9 5.3 %collective-permute-start.5 = (f32[5,16,128]{2,1,0:T(8,128)S(1)}, f32[5,16,128]{2,1,0:T(8,128)S(1)}, u32[]{:S(2)}, u32[]{:S(2)}) collective-permute-start(f32[5,16,128]{2,1,0:T(8,128)S(1)} %get-tuple-element.10), channel_id=1, source_target_pairs={{8,0},{16,8},{24,16},{9,1},{17,9},{25,17},{10,2},{18,10},{26,18},{... | collective-permute-start | bytes 122888 | tf_op jit(solution)/shard_map/ppermute | solution.py:25
  64.3 5.9 %collective-permute-start.6 = (f32[5,16,128]{2,1,0:T(8,128)S(1)}, f32[5,16,128]{2,1,0:T(8,128)S(1)}, u32[]{:S(2)}, u32[]{:S(2)}) collective-permute-start(f32[5,16,128]{2,1,0:T(8,128)S(1)} %add.60), channel_id=1, source_target_pairs={{8,0},{16,8},{24,16},{9,1},{17,9},{25,17},{10,2},{18,10},{26,18},{... | collective-permute-start | bytes 122888 | tf_op jit(solution)/shard_map/ppermute | solution.py:25
  70.8 5.7 %collective-permute-start.7 = (f32[5,16,128]{2,1,0:T(8,128)}, f32[5,16,128]{2,1,0:T(8,128)}, u32[]{:S(2)}, u32[]{:S(2)}) collective-permute-start(f32[5,16,128]{2,1,0:T(8,128)} %add.61), channel_id=1, source_target_pairs={{8,0},{16,8},{24,16},{9,1},{17,9},{25,17},{10,2},{18,10},{26,18},{... | collective-permute-start | bytes 122888 | tf_op jit(solution)/shard_map/ppermute | solution.py:25
  73.6 29.7 %copy-start.43 = (f32[5,16,128]{2,1,0:T(8,128)S(1)}, f32[5,16,128]{2,1,0:T(8,128)}, u32[]{:S(2)}) copy-start(f32[5,16,128]{2,1,0:T(8,128)} %copy-done.42) | copy-start | bytes 122884
  73.6 31.6 %copy-start.41 = (f32[5,16,128]{2,1,0:T(8,128)S(1)}, f32[5,16,128]{2,1,0:T(8,128)}, u32[]{:S(2)}) copy-start(f32[5,16,128]{2,1,0:T(8,128)} %copy-done.40) | copy-start | bytes 122884
  73.6 32.7 %copy-start.39 = (f32[5,16,128]{2,1,0:T(8,128)S(1)}, f32[5,16,128]{2,1,0:T(8,128)}, u32[]{:S(2)}) copy-start(f32[5,16,128]{2,1,0:T(8,128)} %copy-done.38) | copy-start | bytes 122884
  73.6 33.7 %copy-start.37 = (f32[5,16,128]{2,1,0:T(8,128)S(1)}, f32[5,16,128]{2,1,0:T(8,128)}, u32[]{:S(2)}) copy-start(f32[5,16,128]{2,1,0:T(8,128)} %copy-done.36) | copy-start | bytes 122884
  73.6 34.7 %copy-start.35 = (f32[5,16,128]{2,1,0:T(8,128)S(1)}, f32[5,16,128]{2,1,0:T(8,128)}, u32[]{:S(2)}) copy-start(f32[5,16,128]{2,1,0:T(8,128)} %copy-done.34) | copy-start | bytes 122884
  73.7 35.7 %copy-start.33 = (f32[5,16,128]{2,1,0:T(8,128)S(1)}, f32[5,16,128]{2,1,0:T(8,128)}, u32[]{:S(2)}) copy-start(f32[5,16,128]{2,1,0:T(8,128)} %copy-done.32) | copy-start | bytes 122884
  73.7 36.7 %copy-start.31 = (f32[5,16,128]{2,1,0:T(8,128)S(1)}, f32[5,16,128]{2,1,0:T(8,128)}, u32[]{:S(2)}) copy-start(f32[5,16,128]{2,1,0:T(8,128)} %copy-done.30) | copy-start | bytes 122884
  73.7 37.7 %copy-start.29 = (f32[5,16,128]{2,1,0:T(8,128)S(1)}, f32[5,16,128]{2,1,0:T(8,128)}, u32[]{:S(2)}) copy-start(f32[5,16,128]{2,1,0:T(8,128)} %copy-done.28) | copy-start | bytes 122884
  73.7 38.7 %copy-start.27 = (f32[5,16,128]{2,1,0:T(8,128)S(1)}, f32[5,16,128]{2,1,0:T(8,128)}, u32[]{:S(2)}) copy-start(f32[5,16,128]{2,1,0:T(8,128)} %copy-done.26) | copy-start | bytes 122884
  75.0 38.3 %copy-start.25 = (f32[5,16,128]{2,1,0:T(8,128)S(1)}, f32[5,16,128]{2,1,0:T(8,128)}, u32[]{:S(2)}) copy-start(f32[5,16,128]{2,1,0:T(8,128)} %copy-done.24) | copy-start | bytes 122884
  77.5 28.8 %slice-start.3 = ((s8[6553600]{0:T(1024)(128)(4,1)}), s8[4194304]{0:T(1024)(128)(4,1)S(1)}, s32[]{:S(2)}) async-start(s8[6553600]{0:T(1024)(128)(4,1)} %bitcast.1165), calls=%async_computation.4 | async-start | bytes 8388608
  79.6 34.7 %copy-start.23 = (f32[5,16,128]{2,1,0:T(8,128)S(1)}, f32[5,16,128]{2,1,0:T(8,128)}, u32[]{:S(2)}) copy-start(f32[5,16,128]{2,1,0:T(8,128)} %copy-done.22) | copy-start | bytes 122884
  82.3 33.0 %copy-start.21 = (f32[5,16,128]{2,1,0:T(8,128)S(1)}, f32[5,16,128]{2,1,0:T(8,128)}, u32[]{:S(2)}) copy-start(f32[5,16,128]{2,1,0:T(8,128)} %copy-done.20) | copy-start | bytes 122884
  85.1 31.3 %copy-start.19 = (f32[5,16,128]{2,1,0:T(8,128)S(1)}, f32[5,16,128]{2,1,0:T(8,128)}, u32[]{:S(2)}) copy-start(f32[5,16,128]{2,1,0:T(8,128)} %copy-done.18) | copy-start | bytes 122884
  87.8 29.6 %copy-start.17 = (f32[5,16,128]{2,1,0:T(8,128)S(1)}, f32[5,16,128]{2,1,0:T(8,128)}, u32[]{:S(2)}) copy-start(f32[5,16,128]{2,1,0:T(8,128)} %copy-done.16) | copy-start | bytes 122884
  90.5 27.9 %copy-start.15 = (f32[5,16,128]{2,1,0:T(8,128)S(1)}, f32[5,16,128]{2,1,0:T(8,128)}, u32[]{:S(2)}) copy-start(f32[5,16,128]{2,1,0:T(8,128)} %copy-done.14) | copy-start | bytes 122884
  93.2 26.2 %copy-start.13 = (f32[5,16,128]{2,1,0:T(8,128)S(1)}, f32[5,16,128]{2,1,0:T(8,128)}, u32[]{:S(2)}) copy-start(f32[5,16,128]{2,1,0:T(8,128)} %copy-done.12) | copy-start | bytes 122884
  95.9 24.5 %copy-start.11 = (f32[5,16,128]{2,1,0:T(8,128)S(1)}, f32[5,16,128]{2,1,0:T(8,128)}, u32[]{:S(2)}) copy-start(f32[5,16,128]{2,1,0:T(8,128)} %copy-done.10) | copy-start | bytes 122884
  98.7 22.8 %copy-start.9 = (f32[5,16,128]{2,1,0:T(8,128)S(1)}, f32[5,16,128]{2,1,0:T(8,128)}, u32[]{:S(2)}) copy-start(f32[5,16,128]{2,1,0:T(8,128)} %copy-done.8) | copy-start | bytes 122884
  101.4 21.1 %copy-start.7 = (f32[5,16,128]{2,1,0:T(8,128)S(1)}, f32[5,16,128]{2,1,0:T(8,128)}, u32[]{:S(2)}) copy-start(f32[5,16,128]{2,1,0:T(8,128)} %copy-done.6) | copy-start | bytes 122884
  103.3 20.1 %copy-start.5 = (f32[5,16,128]{2,1,0:T(8,128)S(1)}, f32[5,16,128]{2,1,0:T(8,128)}, u32[]{:S(2)}) copy-start(f32[5,16,128]{2,1,0:T(8,128)} %copy-done.4) | copy-start | bytes 122884
  126.9 16.5 %copy-start.2 = (f32[32,5,16,128]{3,2,1,0:T(8,128)}, f32[32,5,16,128]{3,2,1,0:T(8,128)S(1)}, u32[]{:S(2)}) copy-start(f32[32,5,16,128]{3,2,1,0:T(8,128)S(1)} %constant_dynamic-update-slice_fusion) | copy-start | bytes 3932164
  (8 other events, 11.5 us)
Sparse Core Ops, SparseCore 0:
  178.2 132.1 all-reduce.1
where the time goes:
time: 321 us; the launch traced here: 319 us
  waiting for transfers between devices  145 us (45%)
  other arithmetic  81.3 us (25%)
  local copies, waits for them, and re-layouts  52.8 us (16%)
  starting transfers between devices  20.7 us (6%)
  between operations  19.2 us (6%)
    psum x1, waiting for transfers between devices, per_device(): summed = lax.psum(dense_sums, ('sweep', 'bulk'))  132 us
    reduce_sum x260, other arithmetic, matvec(): return jnp.sum(matrix * vector[None], axis=1)  46.8 us
    gather x1, local copies, waits for them, and re-layouts, per_device(): at_faces = adjoint[plane_index, :, column_index, depth_index]  22.1 us
    concatenate x2, local copies, waits for them, and re-layouts, backward_sweep(): lax.scan(backward_advance, start, (forward_field, upper_jac, diag_inv), r...  16.5 us
    ppermute x6, starting transfers between devices, from_behind(): return lax.ppermute(value, axis, pairs)  14.3 us
    ppermute x6, waiting for transfers between devices, from_behind(): return lax.ppermute(value, axis, pairs)  12.4 us
    scatter-add x1, other arithmetic, per_device(): jax.ops.segment_sum(partial_value, owner_dev * NODES_DEV + face_node, num...  12.2 us
    reduce_sum x126, other arithmetic, matmat(): return jnp.sum(matrix[:, :, None] * other[None], axis=1)  10.7 us
  transfers between devices with their start and end apart: 9, of which 7 were waited for; matrix products, arithmetic and copies ran while one was open for 6% of the time, Pallas kernels for 0%

commit v1 on v0

v1 whole, which is shorter than its diff:
```python
import jax
import jax.numpy as jnp
from jax import lax
from jax.experimental import pallas as pl
from jax.experimental.pallas import tpu as pltpu
from jax.sharding import PartitionSpec as P

NODES_DEV = 16384
LANES = 128
F32 = jnp.float32
BF16 = jnp.bfloat16
VMEM = pltpu.VMEM


def dot5(a, b):
    p = [x * y for x, y in zip(a, b)]
    return ((p[0] + p[1]) + (p[2] + p[3])) + p[4]


def block(ref, at, rows):
    return [[ref[at, c, d, rows, :] for d in range(5)] for c in range(5)]


def halves(width):
    return [pl.ds(8 * h, 8) for h in range(width // 8)]


def in_vmem(value):
    return pltpu.with_memory_space_constraint(value, VMEM)


def in_hbm(value):
    return pltpu.with_memory_space_constraint(value, pltpu.HBM)


def vmem_specs(n):
    return [pl.BlockSpec(memory_space=VMEM)] * n


def ratio_and_total(coupled, inv, ratio_ref, total_ref, at, width):
    for rows in halves(width):
        j = block(coupled, at, rows)
        ratio = []
        for c in range(5):
            d = [inv[at, c, e, rows, :] for e in range(5)]
            ratio.append([dot5(d, [j[e][x] for e in range(5)]) for x in range(5)])
        old = [[total_ref[e, x, rows, :] for x in range(5)] for e in range(5)]
        new = [[dot5(ratio[c], [old[e][x] for e in range(5)]) for x in range(5)] for c in range(5)]
        for c in range(5):
            for x in range(5):
                ratio_ref[at, c, x, rows, :] = ratio[c][x]
                total_ref[c, x, rows, :] = new[c][x]


def set_identity(total_ref, planes):
    sign = 1.0 if planes % 2 == 0 else -1.0
    for c in range(5):
        for d in range(5):
            total_ref[c, d] = jnp.full(total_ref.shape[2:], sign if c == d else 0.0, F32)


def forward_matrices(coupled, inv):
    planes, width = coupled.shape[0], coupled.shape[3]

    def kernel(coupled_hbm, inv_hbm, ratio_ref, inv_ref, total_ref, buf, sems):
        def copies(i):
            return (
                pltpu.make_async_copy(inv_hbm.at[i], inv_ref.at[i], sems.at[0, i]),
                pltpu.make_async_copy(coupled_hbm.at[i], buf.at[i], sems.at[1, i]),
            )

        for i in range(planes):
            for copy in copies(i):
                copy.start()
        set_identity(total_ref, planes)

        def body(i, carry):
            for copy in copies(i):
                copy.wait()
            ratio_and_total(buf, inv_ref, ratio_ref, total_ref, i, width)
            return carry

        lax.fori_loop(0, planes, body, 0)

    return pl.pallas_call(
        kernel,
        out_shape=(
            VMEM(coupled.shape, F32),
            VMEM(inv.shape, F32),
            jax.ShapeDtypeStruct(coupled.shape[1:], F32),
        ),
        in_specs=[pl.BlockSpec(memory_space=pltpu.HBM)] * 2,
        out_specs=tuple(vmem_specs(3)),
        scratch_shapes=[VMEM(coupled.shape, F32), pltpu.SemaphoreType.DMA((2, planes))],
        compiler_params=pltpu.CompilerParams(vmem_limit_bytes=10 << 20),
        name="forward_matrices",
    )(in_hbm(coupled), in_hbm(inv))


def backward_matrices(coupled, inv):
    planes, width = coupled.shape[0], coupled.shape[3]

    def kernel(coupled_ref, inv_ref, ratio_ref, total_ref):
        set_identity(total_ref, planes)

        def body(t, carry):
            ratio_and_total(coupled_ref, inv_ref, ratio_ref, total_ref, planes - 1 - t, width)
            return carry

        lax.fori_loop(0, planes, body, 0)

    return pl.pallas_call(
        kernel,
        out_shape=(VMEM(coupled.shape, F32), jax.ShapeDtypeStruct(coupled.shape[1:], F32)),
        in_specs=vmem_specs(2),
        out_specs=tuple(vmem_specs(2)),
        compiler_params=pltpu.CompilerParams(vmem_limit_bytes=4 << 20),
        cost_estimate=pl.CostEstimate(flops=4_000_000, bytes_accessed=20_000_000, transcendentals=0),
        name="backward_matrices",
    )(in_vmem(coupled), in_vmem(inv))


def local_forward(odd, source, psi, lateral, first, second, ratio, inv):
    planes, width = source.shape[0], source.shape[2]

    def kernel(odd_ref, source_ref, psi_ref, lateral_ref, first_ref, second_ref, ratio_ref, inv_ref,
               scaled_ref, leaving_ref):
        is_odd = odd_ref[0] == 1

        def body(i, state):
            one, two = first_ref[i], second_ref[i]
            low = jnp.where(is_odd, one, two)
            high = jnp.where(is_odd, two, one)
            below, above = lateral_ref[i, 0], lateral_ref[i, 1]
            right = []
            for c in range(5):
                here = psi_ref[i, c]
                down = jnp.concatenate([low[c:c + 1], here[:width - 1]], axis=0)
                up = jnp.concatenate([here[1:], high[c:c + 1]], axis=0)
                right.append(source_ref[i, c] - below * down - above * up)
            out = []
            for h, rows in enumerate(halves(width)):
                r = [v[8 * h:8 * h + 8] for v in right]
                d = block(inv_ref, i, rows)
                e = block(ratio_ref, i, rows)
                g = [dot5(d[c], r) for c in range(5)]
                f = [g[c] - dot5(e[c], state[h]) for c in range(5)]
                out.append((g, f))
            for h, rows in enumerate(halves(width)):
                for c in range(5):
                    scaled_ref[i, c, rows, :] = out[h][0][c]
            return [f for _, f in out]

        zero = [[jnp.zeros((8, LANES), F32)] * 5 for _ in halves(width)]
        state = lax.fori_loop(0, planes, body, zero)
        for h, rows in enumerate(halves(width)):
            for c in range(5):
                leaving_ref[c, rows, :] = state[h][c]

    return pl.pallas_call(
        kernel,
        out_shape=(VMEM(source.shape, F32), jax.ShapeDtypeStruct(source.shape[1:], F32)),
        in_specs=[pl.BlockSpec(memory_space=pltpu.SMEM)] + vmem_specs(7),
        out_specs=tuple(vmem_specs(2)),
        compiler_params=pltpu.CompilerParams(vmem_limit_bytes=4 << 20),
        name="local_forward",
    )(odd, in_vmem(source), in_vmem(psi), in_vmem(lateral), in_vmem(first), in_vmem(second),
      in_vmem(ratio), in_vmem(inv))


def forward_then_back(scaled, entering, ratio, back_ratio):
    planes, width = scaled.shape[0], scaled.shape[2]

    def kernel(scaled_ref, entering_ref, ratio_ref, back_ref, field_ref, leaving_ref):
        def ahead(i, state):
            out = []
            for h, rows in enumerate(halves(width)):
                e = block(ratio_ref, i, rows)
                out.append([scaled_ref[i, c, rows, :] - dot5(e[c], state[h]) for c in range(5)])
            for h, rows in enumerate(halves(width)):
                for c in range(5):
                    field_ref[i, c, rows, :] = out[h][c]
            return out

        start = [[entering_ref[c, rows, :] for c in range(5)] for rows in halves(width)]
        lax.fori_loop(0, planes, ahead, start)

        def back(t, state):
            i = planes - 1 - t
            out = []
            for h, rows in enumerate(halves(width)):
                e = block(back_ref, i, rows)
                out.append([field_ref[i, c, rows, :] - dot5(e[c], state[h]) for c in range(5)])
            return out

        zero = [[jnp.zeros((8, LANES), F32)] * 5 for _ in halves(width)]
        state = lax.fori_loop(0, planes, back, zero)
        for h, rows in enumerate(halves(width)):
            for c in range(5):
                leaving_ref[c, rows, :] = state[h][c]

    return pl.pallas_call(
        kernel,
        out_shape=(VMEM(scaled.shape, F32), jax.ShapeDtypeStruct(scaled.shape[1:], F32)),
        in_specs=vmem_specs(4),
        out_specs=tuple(vmem_specs(2)),
        compiler_params=pltpu.CompilerParams(vmem_limit_bytes=4 << 20),
        name="forward_then_back",
    )(in_vmem(scaled), in_vmem(entering), in_vmem(ratio), in_vmem(back_ratio))


def face_tables(count, cell, owner, node, weight, rows_of_cells, owners):
    face_rows = cell.shape[0]
    slots = face_rows * LANES
    cap = 2 * slots // owners
    bucket_rows = 2 * face_rows

    def kernel(count_ref, cell_ref, owner_ref, node_ref, weight_ref,
               row_hot_ref, picked_ref, low_hot_ref, high_hot_ref, nodes_ref):
        lane = lax.broadcasted_iota(jnp.int32, (LANES, LANES), 1)
        sub = lax.broadcasted_iota(jnp.int32, (LANES, LANES), 0)
        strict = (sub < lane).astype(F32).astype(BF16)
        ones = jnp.ones((LANES, LANES), BF16)
        rank = jnp.zeros((face_rows, LANES), F32)
        own = owner_ref[...]
        for o in range(owners):
            mask = (own == o).astype(F32)
            before = jnp.dot(mask.astype(BF16), strict, preferred_element_type=F32)
            totals = jnp.dot(mask.astype(BF16), ones, preferred_element_type=F32)
            fs = lax.broadcasted_iota(jnp.int32, (face_rows, face_rows), 0)
            fl = lax.broadcasted_iota(jnp.int32, (face_rows, face_rows), 1)
            lower = (fl < fs).astype(F32).astype(BF16)
            offset = jnp.dot(lower, totals.astype(BF16), preferred_element_type=F32)
            rank = rank + mask * (before + offset + float(o * cap))
        slot = rank.astype(jnp.int32)
        slot_high, slot_low = slot // LANES, slot % LANES
        high_iota = lax.broadcasted_iota(jnp.int32, (bucket_rows, LANES), 0)
        nodes = jnp.zeros((bucket_rows, LANES), F32)
        cells = cell_ref[...]
        live = lax.broadcasted_iota(jnp.int32, (face_rows, LANES), 0) * LANES + lax.broadcasted_iota(
            jnp.int32, (face_rows, LANES), 1) < count_ref[0]
        nodes_all = node_ref[...]
        for f in range(face_rows):
            at = slice(f, f + 1)
            parts = [
                (cells[at] // LANES).astype(F32),
                (cells[at] % LANES).astype(F32),
                slot_low[at].astype(F32),
                (nodes_all[at] // LANES).astype(F32),
                (nodes_all[at] % LANES).astype(F32),
            ]
            for c in range(5):
                w = weight_ref[c:c + 1, f * LANES:(f + 1) * LANES]
                parts.append(jnp.where(live[at], w, 0.0))
            parts.append(jnp.zeros((LANES - len(parts), LANES), F32))
            columns = jnp.transpose(jnp.concatenate(parts, axis=0))

            def spread(k):
                return jnp.broadcast_to(columns[:, k:k + 1], (LANES, LANES))

            lane_f = lane.astype(F32)
            row = spread(0)
            here = pl.ds(f * LANES, LANES)
            for k in range(rows_of_cells // LANES):
                row_hot_ref[here, k * LANES:(k + 1) * LANES] = jnp.where(
                    row == lane_f + float(k * LANES), 1.0, 0.0).astype(BF16)
            picked = spread(1) == lane_f
            for c in range(5):
                picked_ref[here, c * LANES:(c + 1) * LANES] = jnp.where(picked, spread(5 + c), 0.0)
            low = jnp.where(spread(2) == lane_f, 1.0, 0.0)
            low_hot_ref[here, :] = low
            high = jnp.where(high_iota == slot_high[at], 1.0, 0.0).astype(BF16)
            high_hot_ref[:, f * LANES:(f + 1) * LANES] = high
            nodes = nodes + LANES * jnp.dot(high, (low * spread(3)).astype(BF16), preferred_element_type=F32)
            nodes = nodes + jnp.dot(high, (low * spread(4)).astype(BF16), preferred_element_type=F32)
        nodes_ref[...] = nodes

    return pl.pallas_call(
        kernel,
        out_shape=(
            VMEM((slots, rows_of_cells), BF16),
            VMEM((slots, 5 * LANES), F32),
            VMEM((slots, LANES), F32),
            VMEM((bucket_rows, slots), BF16),
            VMEM((bucket_rows, LANES), F32),
        ),
        in_specs=[pl.BlockSpec(memory_space=pltpu.SMEM)] + vmem_specs(4),
        out_specs=tuple(vmem_specs(5)),
        compiler_params=pltpu.CompilerParams(vmem_limit_bytes=8 << 20),
        cost_estimate=pl.CostEstimate(flops=4_000_000, bytes_accessed=20_000_000, transcendentals=0),
        name="face_tables",
    )(count, cell, owner, node, weight)


def split(value):
    high = value.astype(BF16)
    return high, (value - high.astype(F32)).astype(BF16)


def backward_and_faces(field, entering, back_ratio, tables, devices, owners):
    row_hot, picked, low_hot, high_hot, nodes = tables
    planes, width = field.shape[0], field.shape[2]
    cells = planes * width
    slots = row_hot.shape[0]
    bucket_rows = nodes.shape[0]
    rows_each = bucket_rows // owners
    chunk = 256

    def kernel(field_ref, entering_ref, back_ref, row_hot_ref, picked_ref, low_hot_ref, high_hot_ref,
               nodes_ref, adjoint_ref, send_ref, halves_ref):
        def back(t, state):
            i = planes - 1 - t
            out = []
            for h, rows in enumerate(halves(width)):
                e = block(back_ref, i, rows)
                out.append([field_ref[i, c, rows, :] - dot5(e[c], state[h]) for c in range(5)])
            for h, rows in enumerate(halves(width)):
                for c in range(5):
                    adjoint_ref[i, c, rows, :] = out[h][c]
            at = pl.multiple_of(i * width, width)
            for c in range(5):
                high, low = split(jnp.concatenate([o[c] for o in out], axis=0))
                halves_ref[pl.ds(at, width), c * LANES:(c + 1) * LANES] = high
                halves_ref[pl.ds(cells + at, width), c * LANES:(c + 1) * LANES] = low
            return out

        start = [[entering_ref[c, rows, :] for c in range(5)] for rows in halves(width)]
        lax.fori_loop(0, planes, back, start)
        ones = jnp.ones((LANES, LANES), BF16)
        values = jnp.zeros((bucket_rows, LANES), F32)
        for k in range(slots // chunk):
            here = slice(k * chunk, (k + 1) * chunk)
            hot = row_hot_ref[here, :]
            rows = jnp.dot(hot, halves_ref[:cells, :], preferred_element_type=F32)
            rows = rows + jnp.dot(hot, halves_ref[cells:, :], preferred_element_type=F32)
            scaled = rows * picked_ref[here, :]
            total = scaled[:, :LANES]
            for c in range(1, 5):
                total = total + scaled[:, c * LANES:(c + 1) * LANES]
            high, low = split(total)
            value = jnp.dot(high, ones, preferred_element_type=F32) + jnp.dot(
                low, ones, preferred_element_type=F32)
            high, low = split(value * low_hot_ref[here, :])
            place = high_hot_ref[:, here]
            values = values + (jnp.dot(place, high, preferred_element_type=F32)
                               + jnp.dot(place, low, preferred_element_type=F32))
        for d in range(devices):
            o = d % owners
            send_ref[d, :rows_each, :] = values[o * rows_each:(o + 1) * rows_each]
            send_ref[d, rows_each:, :] = nodes_ref[o * rows_each:(o + 1) * rows_each, :]

    return pl.pallas_call(
        kernel,
        out_shape=(
            jax.ShapeDtypeStruct(field.shape, F32),
            jax.ShapeDtypeStruct((devices, 2 * rows_each, LANES), F32),
        ),
        in_specs=vmem_specs(8),
        out_specs=tuple(vmem_specs(2)),
        scratch_shapes=[VMEM((2 * cells, 5 * LANES), BF16)],
        compiler_params=pltpu.CompilerParams(vmem_limit_bytes=16 << 20),
        name="backward_and_faces",
    )(in_vmem(field), in_vmem(entering), in_vmem(back_ratio), in_vmem(row_hot), in_vmem(picked),
      in_vmem(low_hot), in_vmem(high_hot), in_vmem(nodes))


def node_sums(got):
    devices, rows2, _ = got.shape
    rows_each = rows2 // 2
    side = NODES_DEV // LANES

    def kernel(got_ref, out_ref):
        sub = lax.broadcasted_iota(jnp.int32, (LANES, LANES), 0)
        side_iota = lax.broadcasted_iota(jnp.int32, (side, LANES), 0)

        def body(d, total):
            lefts, rights = [], []
            for r in range(rows_each):
                value = got_ref[d, r:r + 1, :]
                node = got_ref[d, rows_each + r:rows_each + r + 1, :].astype(jnp.int32)
                lefts.append(jnp.where(side_iota == node // LANES, 1.0, 0.0).astype(BF16))
                hot = sub == node % LANES
                high, low = split(value)
                rights.append(jnp.concatenate([
                    jnp.where(hot, high.astype(F32), 0.0).astype(BF16),
                    jnp.where(hot, low.astype(F32), 0.0).astype(BF16)], axis=0))
            left = jnp.concatenate(lefts, axis=1)
            right = jnp.concatenate(rights, axis=1)
            return total + lax.dot_general(left, right, (((1,), (1,)), ((), ())),
                                           preferred_element_type=F32)

        total = lax.fori_loop(0, devices, body, jnp.zeros((side, 2 * LANES), F32))
        out_ref[...] = total[:, :LANES] + total[:, LANES:]

    return pl.pallas_call(
        kernel,
        out_shape=jax.ShapeDtypeStruct((side, LANES), F32),
        in_specs=vmem_specs(1),
        out_specs=pl.BlockSpec(memory_space=VMEM),
        compiler_params=pltpu.CompilerParams(vmem_limit_bytes=8 << 20),
        name="node_sums",
    )(in_vmem(got))


def matvec(matrix, vector):
    return jnp.sum(matrix * vector[None], axis=1)


def matmat(matrix, other):
    return jnp.sum(matrix[:, :, None] * other[None], axis=1)


def relay(total, leaving, backward):
    size = lax.axis_size("sweep")
    index = lax.axis_index("sweep")
    stages = size.bit_length() - 1
    entering = jnp.zeros_like(leaving)
    reach = None
    for stage in range(stages):
        step = 1 << stage
        last = stage == stages - 1
        pairs = [(i, i ^ step) for i in range(size)]
        after = ((index // step) % 2) == (0 if backward else 1)
        other = lax.ppermute(leaving, "sweep", pairs)
        other_total = None if last else lax.ppermute(total, "sweep", pairs)
        gain = other if reach is None else matvec(reach, other)
        entering = jnp.where(after, entering + gain, entering)
        if not last:
            if reach is None:
                eye = jnp.eye(5, dtype=F32)[:, :, None, None]
                reach = jnp.where(after, other_total, jnp.broadcast_to(eye, total.shape))
            else:
                reach = jnp.where(after, matmat(reach, other_total), reach)
            near = jnp.where(after, total, other_total)
            far = jnp.where(after, other_total, total)
            leaving = jnp.where(after, leaving, other) + matvec(near, jnp.where(after, other, leaving))
            if stage + 1 < stages - 1:
                total = matmat(near, far)
    return entering


def per_device(source, psi_old, lateral, lower_jac, upper_jac, diag_inv, face_weight, face_cell,
               face_owner, face_node, face_count):
    bulk = lax.axis_size("bulk")
    devices = bulk * lax.axis_size("sweep")
    width = source.shape[2]
    odd = lax.axis_index("bulk") % 2
    low_pairs = [(i, i ^ 1) for i in range(bulk) if i ^ 1 < bulk]
    high_pairs = [(i, j) for i in range(bulk) for j in [i + 1 if i % 2 else i - 1] if 0 <= j < bulk]
    edge = lax.dynamic_index_in_dim(psi_old, jnp.where(odd == 1, 0, width - 1), 2, keepdims=False)
    first = lax.ppermute(edge, "bulk", low_pairs)
    edge = lax.dynamic_index_in_dim(psi_old, jnp.where(odd == 1, width - 1, 0), 2, keepdims=False)
    second = lax.ppermute(edge, "bulk", high_pairs)

    ratio, inv, total = forward_matrices(lower_jac, diag_inv)
    scaled, leaving = local_forward(odd.reshape(1), source, psi_old, lateral, first, second, ratio, inv)
    entering = relay(total, leaving, False)
    back_ratio, back_total = backward_matrices(upper_jac, inv)
    field, leaving = forward_then_back(scaled, entering, ratio, back_ratio)
    entering = relay(back_total, leaving, True)

    slots = face_cell.shape[0]
    rows = (slots // LANES, LANES)
    tables = face_tables(face_count, face_cell.reshape(rows), face_owner.reshape(rows),
                         face_node.reshape(rows), face_weight, source.shape[0] * width, bulk)
    adjoint, send = backward_and_faces(field, entering, back_ratio, tables, devices, bulk)
    got = lax.all_to_all(send, ("sweep", "bulk"), 0, 0, tiled=True)
    return adjoint, node_sums(got).reshape(NODES_DEV)


def solution(mesh):
    placed = (
        P("sweep", None, "bulk", None),
        P("sweep", None, "bulk", None),
        P("sweep", None, "bulk", None),
        P("sweep", None, None, "bulk", None),
        P("sweep", None, None, "bulk", None),
        P("sweep", None, None, "bulk", None),
        P(None, ("sweep", "bulk")),
        P(("sweep", "bulk")),
        P(("sweep", "bulk"), None),
        P(("sweep", "bulk")),
        P(("sweep", "bulk")),
    )
    return jax.shard_map(
        per_device,
        mesh=mesh,
        in_specs=placed,
        out_specs=(P("sweep", None, "bulk", None), P("bulk")),
        check_vma=False,
    )
```

time: 321 us -> 78.9 us (0.25)
  waiting for transfers between devices: 145 us -> 2.16 us
  other arithmetic: 81.3 us -> 0.32 us
  local copies, waits for them, and re-layouts: 52.8 us -> 17.7 us
  Pallas kernels: 0 us -> 34.6 us
  between operations: 19.2 us -> 1.62 us
  blocking collectives: 0 us -> 15.1 us
  starting transfers between devices: 20.7 us -> 7.14 us
    psum x1 -> x0, waiting for transfers between devices: 132 us -> none  [per_device(): summed = lax.psum(dense_sums, ('sweep', 'bulk'))]
    reduce_sum x260 -> x4, other arithmetic: 46.8 us -> 0.26 us  [matvec(): return jnp.sum(matrix * vector[None], axis=1)]
    pallas_call x0 -> x7, Pallas kernels: none -> 34.6 us  [the longest x1 8.62 us: node_sums(): pl.pallas_call(kernel, out_shape=jax.ShapeDtypeStruct((side, LANES), F32)...]
    gather x1 -> x0, local copies, waits for them, and re-layouts: 22.1 us -> none  [per_device(): at_faces = adjoint[plane_index, :, column_index, depth_index]]
    concatenate x2 -> x0, local copies, waits for them, and re-layouts: 16.5 us -> none  [backward_sweep(): lax.scan(backward_advance, start, (forward_field, upper_jac, diag_inv), r...]
    all_to_all x0 -> x1, blocking collectives: none -> 15.1 us  [per_device(): got = lax.all_to_all(send, ('sweep', 'bulk'), 0, 0, tiled=True)]
    ppermute x8, starting transfers between devices: 20.6 us -> 7.14 us  [the longest x1 3.03 us: per_device(): first = lax.ppermute(edge, 'bulk', low_pairs)]
    scatter-add x1 -> x0, other arithmetic: 12.2 us -> none  [per_device(): jax.ops.segment_sum(partial_value, owner_dev * NODES_DEV + face_node, num...]
  transfers between devices with their start and end apart: 9 -> 8, of which waited for: 7 -> 4; matrix products, arithmetic and copies ran while one was open for 6% -> 0% of each run, Pallas kernels for 0% -> 19%
where the time goes in v1:
time: 78.9 us; the launch traced here: 78.6 us
  Pallas kernels  34.6 us (44%)
  local copies, waits for them, and re-layouts  17.7 us (22%)
  blocking collectives  15.1 us (19%)
  starting transfers between devices  7.14 us (9%)
  waiting for transfers between devices  2.16 us (3%)
  between operations  1.62 us (2%)
    unnamed x38, local copies, waits for them, and re-layouts  16.3 us
    all_to_all x1, blocking collectives, per_device(): got = lax.all_to_all(send, ('sweep', 'bulk'), 0, 0, tiled=True)  15.1 us
    pallas_call x1, Pallas kernels, node_sums(): pl.pallas_call(kernel, out_shape=jax.ShapeDtypeStruct((side, LANES), F32)...  8.62 us
    pallas_call x1, Pallas kernels, backward_and_faces(): pl.pallas_call(kernel, out_shape=(jax.ShapeDtypeStruct(field.shape, F32),...  7.86 us
    pallas_call x1, Pallas kernels, forward_matrices(): pl.pallas_call(kernel, out_shape=(VMEM(coupled.shape, F32), VMEM(inv.shap...  6.17 us
    pallas_call x1, Pallas kernels, face_tables(): pl.pallas_call(kernel, out_shape=(VMEM((slots, rows_of_cells), BF16), VME...  4.61 us
    pallas_call x1, Pallas kernels, backward_matrices(): pl.pallas_call(kernel, out_shape=(VMEM(coupled.shape, F32), jax.ShapeDtyp...  4.33 us
    ppermute x1, starting transfers between devices, per_device(): first = lax.ppermute(edge, 'bulk', low_pairs)  3.03 us
  transfers between devices with their start and end apart: 8, of which 4 were waited for; matrix products, arithmetic and copies ran while one was open for 0% of the time, Pallas kernels for 19%

profile of v1, /device:TPU:0, one launch (start us, length us, event | category | flops | bytes accessed | tf_op | source)
XLA Modules:
  0.0 78.6 jit_solution(17724042705334033313)
XLA Ops:
  0.6 1.4 %constant_dynamic-slice_fusion = (f32[32,5,1,128]{3,2,1,0:T(1,128)S(1)}, f32[32,5,1,128]{3,2,1,0:T(1,128)S(1)}) fusion(f32[32,5,16,128]{3,2,1,0:T(8,128)} %psi_ref.1, s32[]{:T(128)S(6)} %select_n.102, s32[]{:T(128)S(6)} %select_n.101), kind=kLoop, calls=%fused_computation.14 | loop fusion | bytes 327688 | tf_op jit(solution)/shard_map/jit(dynamic_index_in_dim)/dynamic_slice | solution.py:452
  2.1 3.0 %collective-permute-start = (f32[32,5,128]{2,1,0:T(8,128)S(1)}, f32[32,5,128]{2,1,0:T(8,128)S(1)}, u32[]{:S(2)}, u32[]{:S(2)}) collective-permute-start(f32[32,5,128]{2,1,0:T(8,128)S(1)} %bitcast.18), channel_id=1, source_target_pairs={{0,1},{1,0},{2,3},{3,2},{4,5},{5,4},{6,7},{7,6},{8,9},{9,8},{10,11... | collective-permute-start | bytes 245768 | tf_op jit(solution)/shard_map/ppermute | solution.py:451
  5.1 0.0 copy-start.6
  5.1 0.0 copy-start.7
  5.1 0.0 copy-start.12
  5.2 0.8 %collective-permute-start.1 = (f32[32,5,128]{2,1,0:T(8,128)S(1)}, f32[32,5,128]{2,1,0:T(8,128)S(1)}, u32[]{:S(2)}, u32[]{:S(2)}) collective-permute-start(f32[32,5,128]{2,1,0:T(8,128)S(1)} %bitcast.19), channel_id=1, source_target_pairs={{1,2},{2,1},{3,4},{4,3},{5,6},{6,5},{9,10},{10,9},{11,12},{12,11},... | collective-permute-start | bytes 245768 | tf_op jit(solution)/shard_map/ppermute | solution.py:453
  6.0 6.2 %forward_matrices.1 = (f32[32,5,5,16,128]{4,3,2,1,0:T(8,128)S(1)}, f32[32,5,5,16,128]{4,3,2,1,0:T(8,128)S(1)}, f32[5,5,16,128]{3,2,1,0:T(8,128)S(1)}) custom-call(f32[32,5,5,16,128]{4,3,2,1,0:T(8,128)} %coupled_hbm.1, f32[32,5,5,16,128]{4,3,2,1,0:T(8,128)} %inv_hbm.1), custom_call_target="tpu_custom_call" | custom-call | tf_op jit(solution)/shard_map/forward_matrices/pallas_call | solution.py:85
  12.1 0.0 copy-start
  12.1 0.0 copy-start.1
  12.2 0.0 collective-permute-done.first_ref
  12.2 0.0 collective-permute-done.1.second_ref
  12.2 0.0 copy-done.6
  12.2 0.0 copy-done.7
  12.2 0.0 copy-done.12
  12.2 1.7 %local_forward.1 = (f32[32,5,16,128]{3,2,1,0:T(8,128)S(1)}, f32[5,16,128]{2,1,0:T(8,128)S(1)}) custom-call(s32[1]{0:T(128)} %bitcast.odd_ref, f32[32,5,16,128]{3,2,1,0:T(8,128)S(1)} %copy-done.7, f32[32,5,16,128]{3,2,1,0:T(8,128)S(1)} %copy-done.6, f32[32,2,16,128]{3,2,1,0:T(8,128)S(1)} %copy-done.12, f32[32,5,128]{2,1,0:T(8,128)S(1)} %collective-permute-done.first_ref, ...), custom_call_target="tpu_custom_call" | custom-call | tf_op jit(solution)/shard_map/local_forward/pallas_call | solution.py:160
  13.9 1.0 %copy-done = f32[32,5,5,16,128]{4,3,2,1,0:T(8,128)} copy-done((f32[32,5,5,16,128]{4,3,2,1,0:T(8,128)}, f32[32,5,5,16,128]{4,3,2,1,0:T(8,128)S(1)}, u32[]{:S(2)}) %copy-start) | copy-done | bytes 6553624
  14.9 2.0 %copy-done.1 = f32[32,5,5,16,128]{4,3,2,1,0:T(8,128)} copy-done((f32[32,5,5,16,128]{4,3,2,1,0:T(8,128)}, f32[32,5,5,16,128]{4,3,2,1,0:T(8,128)S(1)}, u32[]{:S(2)}) %copy-start.1) | copy-done | bytes 6553624
  16.9 0.0 copy-start.10
  16.9 1.1 %copy-done.10 = f32[32,5,16,128]{3,2,1,0:T(8,128)} copy-done((f32[32,5,16,128]{3,2,1,0:T(8,128)}, f32[32,5,16,128]{3,2,1,0:T(8,128)S(1)}, u32[]{:S(2)}) %copy-start.10) | copy-done | bytes 1310744
  17.9 0.0 collective-permute-start.2
  17.9 0.5 collective-permute-start.3
  18.4 0.7 collective-permute-done.2
  19.2 0.4 collective-permute-done.3
  19.6 0.0 slice-start
  19.6 1.6 %collective-permute-start.4 = (f32[5,16,128]{2,1,0:T(8,128)S(1)}, f32[5,16,128]{2,1,0:T(8,128)S(1)}, u32[]{:S(2)}, u32[]{:S(2)}) collective-permute-start(f32[5,16,128]{2,1,0:T(8,128)S(1)} %select_add_fusion.1), channel_id=1, source_target_pairs={{0,16},{8,24},{16,0},{24,8},{1,17},{9,25},{17,1},{25,9},{2,18},{10... | collective-permute-start | bytes 122888 | tf_op jit(solution)/shard_map/ppermute | solution.py:424
  21.2 0.0 copy-start.2
  21.2 2.9 %copy-done.2 = f32[32,5,5,16,128]{4,3,2,1,0:T(8,128)S(1)} copy-done((f32[32,5,5,16,128]{4,3,2,1,0:T(8,128)S(1)}, f32[32,5,5,16,128]{4,3,2,1,0:T(8,128)}, u32[]{:S(2)}) %copy-start.2) | copy-done | bytes 6553624
  24.0 0.0 copy-start.5
  24.0 2.9 %copy-done.5 = f32[32,5,5,16,128]{4,3,2,1,0:T(8,128)S(1)} copy-done((f32[32,5,5,16,128]{4,3,2,1,0:T(8,128)S(1)}, f32[32,5,5,16,128]{4,3,2,1,0:T(8,128)}, u32[]{:S(2)}) %copy-start.5) | copy-done | bytes 6553624
  26.9 0.0 slice-start.1
  26.9 0.0 copy-start.11
  26.9 4.3 %backward_matrices.1 = (f32[32,5,5,16,128]{4,3,2,1,0:T(8,128)S(1)}, f32[5,5,16,128]{3,2,1,0:T(8,128)S(1)}) custom-call(f32[32,5,5,16,128]{4,3,2,1,0:T(8,128)S(1)} %copy-done.5, f32[32,5,5,16,128]{4,3,2,1,0:T(8,128)S(1)} %copy-done.2), custom_call_target="tpu_custom_call" | custom-call | flops 4000000 | bytes 20000000 | tf_op jit(solution)/shard_map/backward_matrices/pallas_call | solution.py:112
  31.2 0.0 copy-start.3
  31.2 0.0 collective-permute-done.4
  31.2 0.1 multiply_reduce_fusion.2
  31.4 0.0 slice-done
  31.4 0.0 slice-done.1
  31.4 0.0 copy-done.11
  31.4 0.0 copy-start.13
  31.4 0.0 copy-start.14
  31.4 0.0 copy-start.15
  31.4 0.0 copy-start.16
  31.4 1.3 %forward_then_back.1 = (f32[32,5,16,128]{3,2,1,0:T(8,128)S(1)}, f32[5,16,128]{2,1,0:T(8,128)S(1)}) custom-call(f32[32,5,16,128]{3,2,1,0:T(8,128)S(1)} %copy-done.11, f32[5,16,128]{2,1,0:T(8,128)S(1)} %add_select_fusion.1.entering_ref, f32[32,5,5,16,128]{4,3,2,1,0:T(8,128)S(1)} %bitcast.14, f32[32,5,5,16,128]{4,3,2,1,0:T(8,128)S(1)} %get-tuple-element.23.back_ref), custom_call_target="tpu_custom_call" | custom-call | tf_op jit(solution)/shard_map/forward_then_back/pallas_call | solution.py:202
  32.8 1.2 %copy-done.3 = f32[32,5,5,16,128]{4,3,2,1,0:T(8,128)} copy-done((f32[32,5,5,16,128]{4,3,2,1,0:T(8,128)}, f32[32,5,5,16,128]{4,3,2,1,0:T(8,128)S(1)}, u32[]{:S(2)}) %copy-start.3) | copy-done | bytes 6553624
  34.0 0.0 copy-start.8
  34.0 1.1 %copy-done.8 = f32[32,5,16,128]{3,2,1,0:T(8,128)} copy-done((f32[32,5,16,128]{3,2,1,0:T(8,128)}, f32[32,5,16,128]{3,2,1,0:T(8,128)S(1)}, u32[]{:S(2)}) %copy-start.8) | copy-done | bytes 1310744
  35.1 0.1 collective-permute-start.5
  35.1 0.4 collective-permute-start.6
  35.6 0.7 collective-permute-done.5
  36.3 0.4 collective-permute-done.6
  36.7 0.7 collective-permute-start.7
  38.1 0.0 copy-done.13
  38.1 0.0 copy-done.14
  38.1 0.0 copy-done.15
  38.1 0.0 copy-done.16
  38.1 4.6 %face_tables.1 = (bf16[2048,512]{1,0:T(8,128)(2,1)S(1)}, f32[2048,640]{1,0:T(8,128)S(1)}, f32[2048,128]{1,0:T(8,128)S(1)}, bf16[32,2048]{1,0:T(8,128)(2,1)S(1)}, f32[32,128]{1,0:T(8,128)S(1)}) custom-call(s32[1]{0:T(128)S(6)} %copy.25.count_ref, s32[16,128]{1,0:T(8,128)S(1)} %bitcast.15, s32[16,128]{1,0:T(8,128)S(1)} %bitcast.16, s32[16,128]{1,0:T(8,128)S(1)} %bitcast.17, ...), custom_call_target="tpu_custom_call" | custom-call | flops 4000000 | bytes 20000000 | tf_op jit(solution)/shard_map/face_tables/pallas_call | solution.py:278
  42.7 0.0 collective-permute-done.7
  42.7 0.1 multiply_reduce_fusion
  42.8 0.0 copy-start.4
  42.9 2.9 %copy-done.4 = f32[32,5,5,16,128]{4,3,2,1,0:T(8,128)S(1)} copy-done((f32[32,5,5,16,128]{4,3,2,1,0:T(8,128)S(1)}, f32[32,5,5,16,128]{4,3,2,1,0:T(8,128)}, u32[]{:S(2)}) %copy-start.4) | copy-done | bytes 6553624
  45.7 1.3 %copy-done.9 = f32[32,5,16,128]{3,2,1,0:T(8,128)S(1)} copy-done((f32[32,5,16,128]{3,2,1,0:T(8,128)S(1)}, f32[32,5,16,128]{3,2,1,0:T(8,128)}, u32[]{:S(2)}) %copy-start.9) | copy-done | bytes 1310744
  47.0 7.9 %backward_and_faces.1 = (f32[32,5,16,128]{3,2,1,0:T(8,128)}, f32[32,8,128]{2,1,0:T(8,128)S(1)}) custom-call(f32[32,5,16,128]{3,2,1,0:T(8,128)S(1)} %copy-done.9, f32[5,16,128]{2,1,0:T(8,128)S(1)} %add_select_fusion.entering_ref, f32[32,5,5,16,128]{4,3,2,1,0:T(8,128)S(1)} %copy-done.4, bf16[2048,512]{1,0:T(8,128)(2,1)S(1)} %get-tuple-element.27.row_hot_ref, ...), custom_call_target="tpu_custom_call" | custom-call | tf_op jit(solution)/shard_map/backward_and_faces/pallas_call | solution.py:352
  54.9 15.1 %all_to_all.5.got_ref = f32[32,8,128]{2,1,0:T(8,128)S(1)} all-to-all(f32[32,8,128]{2,1,0:T(8,128)S(1)} %get-tuple-element.33), channel_id=1, replica_groups=mesh['sweep'=4,'bulk'=8] {'sweep','bulk'}, dimensions={0} | all-to-all | bytes 262144 | tf_op jit(solution)/shard_map/all_to_all | solution.py:467
  70.0 8.6 %node_sums.1 = f32[128,128]{1,0:T(8,128)} custom-call(f32[32,8,128]{2,1,0:T(8,128)S(1)} %all_to_all.5.got_ref), custom_call_target="tpu_custom_call" | custom-call | tf_op jit(solution)/shard_map/node_sums/pallas_call | solution.py:395
  (13 shorter events, 0.2 us)
Async XLA Ops:
  2.1 10.1 %collective-permute-start = (f32[32,5,128]{2,1,0:T(8,128)S(1)}, f32[32,5,128]{2,1,0:T(8,128)S(1)}, u32[]{:S(2)}, u32[]{:S(2)}) collective-permute-start(f32[32,5,128]{2,1,0:T(8,128)S(1)} %bitcast.18), channel_id=1, source_target_pairs={{0,1},{1,0},{2,3},{3,2},{4,5},{5,4},{6,7},{7,6},{8,9},{9,8},{10,11... | collective-permute-start | bytes 245768 | tf_op jit(solution)/shard_map/ppermute | solution.py:451
  5.1 7.1 %copy-start.6 = (f32[32,5,16,128]{3,2,1,0:T(8,128)S(1)}, f32[32,5,16,128]{3,2,1,0:T(8,128)}, u32[]{:S(2)}) copy-start(f32[32,5,16,128]{3,2,1,0:T(8,128)} %psi_ref.1) | copy-start | bytes 3932164
  5.1 7.1 %copy-start.7 = (f32[32,5,16,128]{3,2,1,0:T(8,128)S(1)}, f32[32,5,16,128]{3,2,1,0:T(8,128)}, u32[]{:S(2)}) copy-start(f32[32,5,16,128]{3,2,1,0:T(8,128)} %source_ref.1) | copy-start | bytes 3932164
  5.1 7.1 %copy-start.12 = (f32[32,2,16,128]{3,2,1,0:T(8,128)S(1)}, f32[32,2,16,128]{3,2,1,0:T(8,128)}, u32[]{:S(2)}) copy-start(f32[32,2,16,128]{3,2,1,0:T(8,128)} %lateral_ref.1) | copy-start | bytes 1572868
  5.2 7.0 %collective-permute-start.1 = (f32[32,5,128]{2,1,0:T(8,128)S(1)}, f32[32,5,128]{2,1,0:T(8,128)S(1)}, u32[]{:S(2)}, u32[]{:S(2)}) collective-permute-start(f32[32,5,128]{2,1,0:T(8,128)S(1)} %bitcast.19), channel_id=1, source_target_pairs={{1,2},{2,1},{3,4},{4,3},{5,6},{6,5},{9,10},{10,9},{11,12},{12,11},... | collective-permute-start | bytes 245768 | tf_op jit(solution)/shard_map/ppermute | solution.py:453
  12.1 2.7 %copy-start = (f32[32,5,5,16,128]{4,3,2,1,0:T(8,128)}, f32[32,5,5,16,128]{4,3,2,1,0:T(8,128)S(1)}, u32[]{:S(2)}) copy-start(f32[32,5,5,16,128]{4,3,2,1,0:T(8,128)S(1)} %get-tuple-element.18.ratio_ref) | copy-start | bytes 19660804
  12.1 4.7 %copy-start.1 = (f32[32,5,5,16,128]{4,3,2,1,0:T(8,128)}, f32[32,5,5,16,128]{4,3,2,1,0:T(8,128)S(1)}, u32[]{:S(2)}) copy-start(f32[32,5,5,16,128]{4,3,2,1,0:T(8,128)S(1)} %get-tuple-element.19.inv_ref) | copy-start | bytes 19660804
  16.9 1.1 %copy-start.10 = (f32[32,5,16,128]{3,2,1,0:T(8,128)}, f32[32,5,16,128]{3,2,1,0:T(8,128)S(1)}, u32[]{:S(2)}) copy-start(f32[32,5,16,128]{3,2,1,0:T(8,128)S(1)} %get-tuple-element.20.scaled_ref) | copy-start | bytes 3932164
  17.9 1.2 %collective-permute-start.2 = (f32[5,16,128]{2,1,0:T(8,128)S(1)}, f32[5,16,128]{2,1,0:T(8,128)S(1)}, u32[]{:S(2)}, u32[]{:S(2)}) collective-permute-start(f32[5,16,128]{2,1,0:T(8,128)S(1)} %get-tuple-element.21), channel_id=1, source_target_pairs={{0,8},{8,0},{16,24},{24,16},{1,9},{9,1},{17,25},{25,17},{2,10},{10... | collective-permute-start | bytes 122888 | tf_op jit(solution)/shard_map/ppermute | solution.py:424
  17.9 1.6 %collective-permute-start.3 = (f32[5,5,16,128]{3,2,1,0:T(8,128)S(1)}, f32[5,5,16,128]{3,2,1,0:T(8,128)S(1)}, u32[]{:S(2)}, u32[]{:S(2)}) collective-permute-start(f32[5,5,16,128]{3,2,1,0:T(8,128)S(1)} %get-tuple-element.22), channel_id=1, source_target_pairs={{0,8},{8,0},{16,24},{24,16},{1,9},{9,1},{17,25},{25,17},{2,10},{10... | collective-permute-start | bytes 614408 | tf_op jit(solution)/shard_map/ppermute | solution.py:425
  19.6 11.8 %slice-start = ((s8[6553600]{0:T(1024)(128)(4,1)}), s8[2359296]{0:T(1024)(128)(4,1)S(1)}, s32[]{:S(2)}) async-start(s8[6553600]{0:T(1024)(128)(4,1)} %bitcast.13), calls=%async_computation.1 | async-start | bytes 4718592
  19.6 11.7 %collective-permute-start.4 = (f32[5,16,128]{2,1,0:T(8,128)S(1)}, f32[5,16,128]{2,1,0:T(8,128)S(1)}, u32[]{:S(2)}, u32[]{:S(2)}) collective-permute-start(f32[5,16,128]{2,1,0:T(8,128)S(1)} %select_add_fusion.1), channel_id=1, source_target_pairs={{0,16},{8,24},{16,0},{24,8},{1,17},{9,25},{17,1},{25,9},{2,18},{10... | collective-permute-start | bytes 122888 | tf_op jit(solution)/shard_map/ppermute | solution.py:424
  21.2 2.9 %copy-start.2 = (f32[32,5,5,16,128]{4,3,2,1,0:T(8,128)S(1)}, f32[32,5,5,16,128]{4,3,2,1,0:T(8,128)}, u32[]{:S(2)}) copy-start(f32[32,5,5,16,128]{4,3,2,1,0:T(8,128)} %copy-done.1) | copy-start | bytes 19660804
  24.0 2.9 %copy-start.5 = (f32[32,5,5,16,128]{4,3,2,1,0:T(8,128)S(1)}, f32[32,5,5,16,128]{4,3,2,1,0:T(8,128)}, u32[]{:S(2)}) copy-start(f32[32,5,5,16,128]{4,3,2,1,0:T(8,128)} %coupled_ref.1) | copy-start | bytes 19660804
  26.9 4.5 %slice-start.1 = ((s8[6553600]{0:T(1024)(128)(4,1)}), s8[4194304]{0:T(1024)(128)(4,1)S(1)}, s32[]{:S(2)}) async-start(s8[6553600]{0:T(1024)(128)(4,1)} %bitcast.13), calls=%async_computation.2 | async-start | bytes 8388608
  26.9 4.5 %copy-start.11 = (f32[32,5,16,128]{3,2,1,0:T(8,128)S(1)}, f32[32,5,16,128]{3,2,1,0:T(8,128)}, u32[]{:S(2)}) copy-start(f32[32,5,16,128]{3,2,1,0:T(8,128)} %copy-done.10) | copy-start | bytes 3932164
  31.2 2.8 %copy-start.3 = (f32[32,5,5,16,128]{4,3,2,1,0:T(8,128)}, f32[32,5,5,16,128]{4,3,2,1,0:T(8,128)S(1)}, u32[]{:S(2)}) copy-start(f32[32,5,5,16,128]{4,3,2,1,0:T(8,128)S(1)} %get-tuple-element.23.back_ref) | copy-start | bytes 19660804
  31.4 6.7 %copy-start.13 = (f32[5,2048]{1,0:T(8,128)S(1)}, f32[5,2048]{1,0:T(8,128)}, u32[]{:S(2)}) copy-start(f32[5,2048]{1,0:T(8,128)} %weight_ref.1) | copy-start | bytes 122884
  31.4 6.7 %copy-start.14 = (s32[2048]{0:T(1024)S(1)}, s32[2048]{0:T(1024)}, u32[]{:S(2)}) copy-start(s32[2048]{0:T(1024)} %param.18) | copy-start | bytes 24580
  31.4 6.7 %copy-start.15 = (s32[2048,1]{0,1:T(1,128)S(1)}, s32[2048,1]{0,1:T(1,128)}, u32[]{:S(2)}) copy-start(s32[2048,1]{0,1:T(1,128)} %param.19) | copy-start | bytes 24580
  31.4 6.7 %copy-start.16 = (s32[2048]{0:T(1024)S(1)}, s32[2048]{0:T(1024)}, u32[]{:S(2)}) copy-start(s32[2048]{0:T(1024)} %param.20) | copy-start | bytes 24580
  34.0 1.1 %copy-start.8 = (f32[32,5,16,128]{3,2,1,0:T(8,128)}, f32[32,5,16,128]{3,2,1,0:T(8,128)S(1)}, u32[]{:S(2)}) copy-start(f32[32,5,16,128]{3,2,1,0:T(8,128)S(1)} %get-tuple-element.24.field_ref) | copy-start | bytes 3932164
  35.1 1.2 %collective-permute-start.5 = (f32[5,16,128]{2,1,0:T(8,128)S(1)}, f32[5,16,128]{2,1,0:T(8,128)S(1)}, u32[]{:S(2)}, u32[]{:S(2)}) collective-permute-start(f32[5,16,128]{2,1,0:T(8,128)S(1)} %get-tuple-element.25), channel_id=1, source_target_pairs={{0,8},{8,0},{16,24},{24,16},{1,9},{9,1},{17,25},{25,17},{2,10},{10... | collective-permute-start | bytes 122888 | tf_op jit(solution)/shard_map/ppermute | solution.py:424
  35.1 1.5 %collective-permute-start.6 = (f32[5,5,16,128]{3,2,1,0:T(8,128)S(1)}, f32[5,5,16,128]{3,2,1,0:T(8,128)S(1)}, u32[]{:S(2)}, u32[]{:S(2)}) collective-permute-start(f32[5,5,16,128]{3,2,1,0:T(8,128)S(1)} %get-tuple-element.26), channel_id=1, source_target_pairs={{0,8},{8,0},{16,24},{24,16},{1,9},{9,1},{17,25},{25,17},{2,10},{10... | collective-permute-start | bytes 614408 | tf_op jit(solution)/shard_map/ppermute | solution.py:425
  36.7 6.0 %collective-permute-start.7 = (f32[5,16,128]{2,1,0:T(8,128)S(1)}, f32[5,16,128]{2,1,0:T(8,128)S(1)}, u32[]{:S(2)}, u32[]{:S(2)}) collective-permute-start(f32[5,16,128]{2,1,0:T(8,128)S(1)} %select_add_fusion), channel_id=1, source_target_pairs={{0,16},{8,24},{16,0},{24,8},{1,17},{9,25},{17,1},{25,9},{2,18},{10... | collective-permute-start | bytes 122888 | tf_op jit(solution)/shard_map/ppermute | solution.py:424
  42.8 2.9 %copy-start.4 = (f32[32,5,5,16,128]{4,3,2,1,0:T(8,128)S(1)}, f32[32,5,5,16,128]{4,3,2,1,0:T(8,128)}, u32[]{:S(2)}) copy-start(f32[32,5,5,16,128]{4,3,2,1,0:T(8,128)} %copy-done.3) | copy-start | bytes 19660804
  45.7 1.3 %copy-start.9 = (f32[32,5,16,128]{3,2,1,0:T(8,128)S(1)}, f32[32,5,16,128]{3,2,1,0:T(8,128)}, u32[]{:S(2)}) copy-start(f32[32,5,16,128]{3,2,1,0:T(8,128)} %copy-done.8) | copy-start | bytes 3932164

commit v2 on v0

v2 whole, which is shorter than its diff:
```python
import jax
import jax.numpy as jnp
from jax import lax
from jax.experimental import pallas as pl
from jax.experimental.pallas import tpu as pltpu
from jax.sharding import PartitionSpec as P

NODES_DEV = 16384
LANES = 128
F32 = jnp.float32
BF16 = jnp.bfloat16
VMEM = pltpu.VMEM


def dot5(a, b):
    p = [x * y for x, y in zip(a, b)]
    return ((p[0] + p[1]) + (p[2] + p[3])) + p[4]


def block(ref, at, rows):
    return [[ref[at, c, d, rows, :] for d in range(5)] for c in range(5)]


def halves(width):
    return [pl.ds(8 * h, 8) for h in range(width // 8)]


def in_vmem(value):
    return pltpu.with_memory_space_constraint(value, VMEM)


def vmem_specs(n):
    return [pl.BlockSpec(memory_space=VMEM)] * n


def ratio_of(coupled, inv, at, rows):
    j = block(coupled, at, rows)
    d = block(inv, at, rows)
    return [[dot5(d[c], [j[e][x] for e in range(5)]) for x in range(5)] for c in range(5)], d


def next_total(ratio, total_ref, rows):
    old = [[total_ref[e, x, rows, :] for x in range(5)] for e in range(5)]
    return [[dot5(ratio[c], [old[e][x] for e in range(5)]) for x in range(5)] for c in range(5)]


def keep_matrices(ratio, total, ratio_ref, total_ref, at, rows):
    for c in range(5):
        for x in range(5):
            ratio_ref[at, c, x, rows, :] = ratio[c][x]
            total_ref[c, x, rows, :] = total[c][x]


def set_identity(total_ref, planes):
    sign = 1.0 if planes % 2 == 0 else -1.0
    for c in range(5):
        for d in range(5):
            total_ref[c, d] = jnp.full(total_ref.shape[2:], sign if c == d else 0.0, F32)


def edge_rows(psi):
    planes, fields, width, _ = psi.shape
    shape = (planes, fields, LANES)

    def kernel(psi_ref, low_ref, high_ref):
        is_odd = lax.rem(lax.axis_index("bulk"), 2) == 1
        for i in range(planes):
            head = psi_ref[i, :, 0, :]
            tail = psi_ref[i, :, width - 1, :]
            low_ref[i] = jnp.where(is_odd, head, tail)
            high_ref[i] = jnp.where(is_odd, tail, head)

    return pl.pallas_call(
        kernel,
        out_shape=(jax.ShapeDtypeStruct(shape, F32), jax.ShapeDtypeStruct(shape, F32)),
        in_specs=vmem_specs(1),
        out_specs=tuple(vmem_specs(2)),
        compiler_params=pltpu.CompilerParams(vmem_limit_bytes=4 << 20),
        cost_estimate=pl.CostEstimate(flops=4_000_000, bytes_accessed=60_000_000, transcendentals=0),
        name="edge_rows",
    )(in_vmem(psi))


def forward_local(source, psi, lateral, first, second, coupled, inv):
    planes, width = source.shape[0], source.shape[2]

    def kernel(source_ref, psi_ref, lateral_ref, first_ref, second_ref, coupled_ref, inv_ref,
               ratio_ref, total_ref, scaled_ref, leaving_ref):
        is_odd = lax.rem(lax.axis_index("bulk"), 2) == 1
        set_identity(total_ref, planes)

        def body(i, state):
            one, two = first_ref[i], second_ref[i]
            low = jnp.where(is_odd, one, two)
            high = jnp.where(is_odd, two, one)
            below, above = lateral_ref[i, 0], lateral_ref[i, 1]
            right = []
            for c in range(5):
                here = psi_ref[i, c]
                down = jnp.concatenate([low[c:c + 1], here[:width - 1]], axis=0)
                up = jnp.concatenate([here[1:], high[c:c + 1]], axis=0)
                right.append(source_ref[i, c] - below * down - above * up)
            out = []
            for h, rows in enumerate(halves(width)):
                r = [v[8 * h:8 * h + 8] for v in right]
                ratio, d = ratio_of(coupled_ref, inv_ref, i, rows)
                scaled = [dot5(d[c], r) for c in range(5)]
                out.append([scaled[c] - dot5(ratio[c], state[h]) for c in range(5)])
                total = next_total(ratio, total_ref, rows)
                keep_matrices(ratio, total, ratio_ref, total_ref, i, rows)
                for c in range(5):
                    scaled_ref[i, c, rows, :] = scaled[c]
            return out

        zero = [[jnp.zeros((8, LANES), F32)] * 5 for _ in halves(width)]
        state = lax.fori_loop(0, planes, body, zero)
        for h, rows in enumerate(halves(width)):
            for c in range(5):
                leaving_ref[c, rows, :] = state[h][c]

    return pl.pallas_call(
        kernel,
        out_shape=(
            VMEM(coupled.shape, F32),
            jax.ShapeDtypeStruct(coupled.shape[1:], F32),
            VMEM(source.shape, F32),
            jax.ShapeDtypeStruct(source.shape[1:], F32),
        ),
        in_specs=vmem_specs(7),
        out_specs=tuple(vmem_specs(4)),
        compiler_params=pltpu.CompilerParams(vmem_limit_bytes=4 << 20),
        name="forward_local",
    )(*[in_vmem(v) for v in (source, psi, lateral, first, second, coupled, inv)])


def backward_matrices(coupled, inv):
    planes, width = coupled.shape[0], coupled.shape[3]

    def kernel(coupled_ref, inv_ref, ratio_ref, total_ref):
        set_identity(total_ref, planes)

        def body(t, carry):
            at = planes - 1 - t
            for rows in halves(width):
                ratio, _ = ratio_of(coupled_ref, inv_ref, at, rows)
                keep_matrices(ratio, next_total(ratio, total_ref, rows), ratio_ref, total_ref, at, rows)
            return carry

        lax.fori_loop(0, planes, body, 0)

    return pl.pallas_call(
        kernel,
        out_shape=(VMEM(coupled.shape, F32), jax.ShapeDtypeStruct(coupled.shape[1:], F32)),
        in_specs=vmem_specs(2),
        out_specs=tuple(vmem_specs(2)),
        compiler_params=pltpu.CompilerParams(vmem_limit_bytes=4 << 20),
        cost_estimate=pl.CostEstimate(flops=4_000_000, bytes_accessed=20_000_000, transcendentals=0),
        name="backward_matrices",
    )(in_vmem(coupled), in_vmem(inv))


def forward_then_back(scaled, arriving, ratio, back_ratio):
    planes, width = scaled.shape[0], scaled.shape[2]

    def kernel(scaled_ref, near_ref, reach_ref, other_ref, ratio_ref, back_ref, field_ref, leaving_ref):
        def ahead(i, state):
            out = []
            for h, rows in enumerate(halves(width)):
                e = block(ratio_ref, i, rows)
                out.append([scaled_ref[i, c, rows, :] - dot5(e[c], state[h]) for c in range(5)])
            for h, rows in enumerate(halves(width)):
                for c in range(5):
                    field_ref[i, c, rows, :] = out[h][c]
            return out

        start = last_join(near_ref, reach_ref, other_ref, False, width)
        lax.fori_loop(0, planes, ahead, start)

        def back(t, state):
            i = planes - 1 - t
            out = []
            for h, rows in enumerate(halves(width)):
                e = block(back_ref, i, rows)
                out.append([field_ref[i, c, rows, :] - dot5(e[c], state[h]) for c in range(5)])
            return out

        zero = [[jnp.zeros((8, LANES), F32)] * 5 for _ in halves(width)]
        state = lax.fori_loop(0, planes, back, zero)
        for h, rows in enumerate(halves(width)):
            for c in range(5):
                leaving_ref[c, rows, :] = state[h][c]

    return pl.pallas_call(
        kernel,
        out_shape=(VMEM(scaled.shape, F32), jax.ShapeDtypeStruct(scaled.shape[1:], F32)),
        in_specs=vmem_specs(6),
        out_specs=tuple(vmem_specs(2)),
        compiler_params=pltpu.CompilerParams(vmem_limit_bytes=4 << 20),
        name="forward_then_back",
    )(in_vmem(scaled), *[in_vmem(v) for v in arriving], in_vmem(ratio), in_vmem(back_ratio))


def face_slots(owner, node, owners):
    face_rows = owner.shape[0]
    cap = 2 * face_rows * LANES // owners
    bucket_rows = 2 * face_rows

    def kernel(owner_ref, node_ref, slot_ref, nodes_ref):
        sub = lax.broadcasted_iota(jnp.int32, (LANES, LANES), 0)
        lane = lax.broadcasted_iota(jnp.int32, (LANES, LANES), 1)
        strict = (sub < lane).astype(F32).astype(BF16)
        ones = jnp.ones((LANES, LANES), BF16)
        fs = lax.broadcasted_iota(jnp.int32, (face_rows, face_rows), 0)
        fl = lax.broadcasted_iota(jnp.int32, (face_rows, face_rows), 1)
        lower = (fl < fs).astype(F32).astype(BF16)
        own = owner_ref[...]
        masks = [(own == o).astype(F32) for o in range(owners)]
        stacked = jnp.concatenate(masks, axis=0).astype(BF16)
        before = jnp.dot(stacked, strict, preferred_element_type=F32)
        totals = jnp.dot(stacked, ones, preferred_element_type=F32).astype(BF16)
        rank = jnp.zeros((face_rows, LANES), F32)
        for o in range(owners):
            here = slice(o * face_rows, (o + 1) * face_rows)
            offset = jnp.dot(lower, totals[here], preferred_element_type=F32)
            rank = rank + masks[o] * (before[here] + offset + float(o * cap))
        slot = rank.astype(jnp.int32)
        slot_ref[...] = slot
        nodes = node_ref[...]
        high = (nodes // LANES).astype(F32)
        low = (nodes % LANES).astype(F32)
        parts = place_in_slots(slot, [high, low], bucket_rows)
        nodes_ref[...] = float(LANES) * parts[0] + parts[1]

    return pl.pallas_call(
        kernel,
        out_shape=(VMEM((face_rows, LANES), jnp.int32), VMEM((bucket_rows, LANES), F32)),
        in_specs=vmem_specs(2),
        out_specs=tuple(vmem_specs(2)),
        compiler_params=pltpu.CompilerParams(vmem_limit_bytes=4 << 20),
        cost_estimate=pl.CostEstimate(flops=4_000_000, bytes_accessed=10_000_000, transcendentals=0),
        name="face_slots",
    )(in_vmem(owner), in_vmem(node))


def split(value):
    high = value.astype(BF16)
    return high, (value - high.astype(F32)).astype(BF16)


def place_in_slots(slot, parts, bucket_rows):
    face_rows = slot.shape[0]
    high = (slot // LANES).astype(F32).astype(BF16)
    low = (slot % LANES).astype(F32).astype(BF16)
    parts = [p.astype(BF16) for p in parts]
    high_iota = lax.broadcasted_iota(jnp.int32, (bucket_rows, LANES), 0).astype(F32).astype(BF16)
    low_iota = lax.broadcasted_iota(jnp.int32, (LANES, LANES), 0).astype(F32).astype(BF16)
    zero = jnp.zeros((bucket_rows, LANES), BF16)
    lefts, rights = [], []
    for f in range(face_rows):

        def spread(value, rows):
            return jnp.broadcast_to(value[f:f + 1], (rows, LANES))

        hot = high_iota == spread(high, bucket_rows)
        lefts.append(jnp.concatenate([jnp.where(hot, spread(p, bucket_rows), zero) for p in parts], axis=0))
        rights.append(jnp.where(low_iota == spread(low, LANES), jnp.ones((LANES, LANES), BF16),
                                jnp.zeros((LANES, LANES), BF16)))
    out = lax.dot_general(jnp.concatenate(lefts, axis=1), jnp.concatenate(rights, axis=1),
                          (((1,), (1,)), ((), ())), preferred_element_type=F32)
    return [out[k * bucket_rows:(k + 1) * bucket_rows] for k in range(len(parts))]


def backward_and_faces(field, arriving, back_ratio, count, cell, weight, slot, nodes, devices, owners):
    planes, width = field.shape[0], field.shape[2]
    face_rows = cell.shape[0]
    bucket_rows = nodes.shape[0]
    rows_each = bucket_rows // owners
    group = 2
    piece = 4
    batch = 8

    def kernel(count_ref, field_ref, near_ref, reach_ref, other_ref, back_ref, cell_ref, weight_ref,
               slot_ref, nodes_ref, adjoint_hbm, send_ref, adjoint_ref, parts_ref, value_ref, sems):
        def write(k):
            return pltpu.make_async_copy(adjoint_ref.at[pl.ds(k * batch, batch)],
                                         adjoint_hbm.at[pl.ds(k * batch, batch)], sems.at[k])

        def back(t, state):
            i = planes - 1 - t
            out = []
            for h, rows in enumerate(halves(width)):
                e = block(back_ref, i, rows)
                out.append([field_ref[i, c, rows, :] - dot5(e[c], state[h]) for c in range(5)])
            for h, rows in enumerate(halves(width)):
                for c in range(5):
                    adjoint_ref[i, c, rows, :] = out[h][c]
            for c in range(5):
                high, low = split(jnp.concatenate([o[c] for o in out], axis=0))
                at = pl.ds(pl.multiple_of((i * 5 + c) * width, width), width)
                parts_ref[at, :LANES] = high
                parts_ref[at, LANES:] = low
            return out

        state = last_join(near_ref, reach_ref, other_ref, True, width)
        for k in reversed(range(planes // batch)):
            first = planes - (k + 1) * batch
            state = lax.fori_loop(first, first + batch, back, state)
            write(k).start()

        lane_iota = lax.broadcasted_iota(jnp.int32, (LANES, LANES), 0).astype(F32).astype(BF16)
        sub8 = lax.broadcasted_iota(jnp.int32, (8, LANES), 0)

        def gather(g, carry):
            cells = [cell_ref[pl.ds(g * group + u, 1), :] for u in range(group)]
            hots, offs = [], []
            for at in cells:
                lanes = jnp.broadcast_to((at % LANES).astype(F32), (LANES, LANES)).astype(BF16)
                hots.append(jnp.where(lane_iota == lanes, jnp.ones((LANES, LANES), BF16),
                                      jnp.zeros((LANES, LANES), BF16)))
                offs.append(jnp.broadcast_to(at // LANES, (8, LANES)) - sub8)
            hot = jnp.concatenate(hots, axis=1)
            hot = jnp.concatenate([hot, hot], axis=0)
            found = [[jnp.zeros((8, LANES), F32)] * 5 for _ in range(group)]
            for p in range(0, planes, piece):
                got = jnp.dot(parts_ref[p * 5 * width:(p + piece) * 5 * width, :], hot,
                              preferred_element_type=F32)
                for i in range(piece):
                    for h in range(width // 8):
                        for u in range(group):
                            mask = offs[u] == (p + i) * width + 8 * h
                            for c in range(5):
                                row = (i * 5 + c) * width + 8 * h
                                found[u][c] = jnp.where(mask, got[row:row + 8, u * LANES:(u + 1) * LANES],
                                                        found[u][c])
            weights = weight_ref[:, pl.ds(pl.multiple_of(g * (group * LANES), group * LANES), group * LANES)]
            for u in range(group):
                w = [jnp.broadcast_to(weights[c:c + 1, u * LANES:(u + 1) * LANES], (8, LANES)) for c in range(5)]
                value_ref[pl.ds(g * group + u, 1), :] = jnp.sum(dot5(w, found[u]), axis=0, keepdims=True)
            return carry

        lax.fori_loop(0, face_rows // group, gather, 0)
        live = lax.broadcasted_iota(jnp.int32, (face_rows, LANES), 0) * LANES + lax.broadcasted_iota(
            jnp.int32, (face_rows, LANES), 1) < count_ref[0]
        high, low = split(jnp.where(live, value_ref[...], 0.0))
        placed = place_in_slots(slot_ref[...], [high, low], bucket_rows)
        values = placed[0] + placed[1]
        for o in range(owners):
            here = slice(o * rows_each, (o + 1) * rows_each)
            both = jnp.concatenate([values[here], nodes_ref[here, :]], axis=0)
            for d in range(o, devices, owners):
                send_ref[d] = both
        for k in range(planes // batch):
            write(k).wait()

    return pl.pallas_call(
        kernel,
        out_shape=(
            jax.ShapeDtypeStruct(field.shape, F32),
            jax.ShapeDtypeStruct((devices, 2 * rows_each, LANES), F32),
        ),
        in_specs=[pl.BlockSpec(memory_space=pltpu.SMEM)] + vmem_specs(9),
        out_specs=(pl.BlockSpec(memory_space=pltpu.HBM), pl.BlockSpec(memory_space=VMEM)),
        scratch_shapes=[
            VMEM(field.shape, F32),
            VMEM((planes * 5 * width, 2 * LANES), BF16),
            VMEM((face_rows, LANES), F32),
            pltpu.SemaphoreType.DMA((planes // batch,)),
        ],
        compiler_params=pltpu.CompilerParams(vmem_limit_bytes=12 << 20),
        name="backward_and_faces",
    )(count, in_vmem(field), *[in_vmem(v) for v in arriving], in_vmem(back_ratio), in_vmem(cell),
      in_vmem(weight), in_vmem(slot), in_vmem(nodes))


def node_sums(got):
    devices, rows2, _ = got.shape
    rows_each = rows2 // 2
    side = NODES_DEV // LANES
    batch = 32 // rows_each

    def kernel(got_ref, out_ref):
        iota = lax.broadcasted_iota(jnp.int32, (LANES, LANES), 0).astype(F32).astype(BF16)
        side_iota = lax.broadcasted_iota(jnp.int32, (side, LANES), 0).astype(F32).astype(BF16)
        ones, zero = jnp.ones((LANES, LANES), BF16), jnp.zeros((LANES, LANES), BF16)
        side_zero = jnp.zeros((side, LANES), BF16)

        def body(t, total):
            lefts, rights = [], []
            for u in range(batch):
                d = t * batch + u
                node = got_ref[d, rows_each:, :].astype(jnp.int32)
                node_high = (node // LANES).astype(F32).astype(BF16)
                node_low = (node % LANES).astype(F32).astype(BF16)
                high, low = split(got_ref[d, :rows_each, :])
                for r in range(rows_each):

                    def spread(value, rows):
                        return jnp.broadcast_to(value[r:r + 1], (rows, LANES))

                    hot = side_iota == spread(node_high, side)
                    lefts.append(jnp.concatenate([
                        jnp.where(hot, spread(high, side), side_zero),
                        jnp.where(hot, spread(low, side), side_zero)], axis=0))
                    rights.append(jnp.where(iota == spread(node_low, LANES), ones, zero))
            return total + lax.dot_general(
                jnp.concatenate(lefts, axis=1), jnp.concatenate(rights, axis=1),
                (((1,), (1,)), ((), ())), preferred_element_type=F32)

        total = lax.fori_loop(0, devices // batch, body, jnp.zeros((2 * side, LANES), F32))
        out_ref[...] = total[:side] + total[side:]

    return pl.pallas_call(
        kernel,
        out_shape=jax.ShapeDtypeStruct((side, LANES), F32),
        in_specs=vmem_specs(1),
        out_specs=pl.BlockSpec(memory_space=VMEM),
        compiler_params=pltpu.CompilerParams(vmem_limit_bytes=8 << 20),
        name="node_sums",
    )(in_vmem(got))


def comes_after(stage, backward):
    bit = lax.rem(lax.div(lax.axis_index("sweep"), 1 << stage), 2)
    return bit == (0 if backward else 1)


def matvec(matrix, vector):
    return [dot5(row, vector) for row in matrix]


def matmat(matrix, other):
    return [[dot5(row, [other[e][x] for e in range(5)]) for x in range(5)] for row in matrix]


def load_matrix(ref, rows):
    return [[ref[c, d, rows, :] for d in range(5)] for c in range(5)]


def load_vector(ref, rows):
    return [ref[c, rows, :] for c in range(5)]


def pick(flag, one, two):
    if isinstance(one, list):
        return [pick(flag, a, b) for a, b in zip(one, two)]
    return jnp.where(flag, one, two)


def last_join(near_ref, reach_ref, other_ref, backward, width):
    after = comes_after(lax.axis_size("sweep").bit_length() - 2, backward)
    start = []
    for rows in halves(width):
        near = load_vector(near_ref, rows)
        gain = matvec(load_matrix(reach_ref, rows), load_vector(other_ref, rows))
        start.append([n + jnp.where(after, g, 0.0) for n, g in zip(near, gain)])
    return start


def join(stage, backward, near, reach, leaving, total, other, other_total, carry_total):
    first = near is None
    width = leaving.shape[1]
    outs = [leaving.shape, total.shape, leaving.shape] + ([total.shape] if carry_total else [])

    def kernel(*refs):
        ins, out = refs[:len(operands)], refs[len(operands):]
        after = comes_after(stage, backward)
        for rows in halves(width):
            own, theirs = load_vector(ins[0], rows), load_vector(ins[2], rows)
            own_total, their_total = load_matrix(ins[1], rows), load_matrix(ins[3], rows)
            if first:
                entering = theirs
                through = their_total
                before = [jnp.zeros((8, LANES), F32)] * 5
                unit = [[jnp.full((8, LANES), 1.0 if c == d else 0.0, F32) for d in range(5)] for c in range(5)]
            else:
                before, unit = load_vector(ins[4], rows), load_matrix(ins[5], rows)
                entering = [a + b for a, b in zip(before, matvec(unit, theirs))]
                through = matmat(unit, their_total)
            entering, through = pick(after, entering, before), pick(after, through, unit)
            downstream = pick(after, own_total, their_total)
            sent = matvec(downstream, pick(after, theirs, own))
            sent = [a + b for a, b in zip(pick(after, own, theirs), sent)]
            for c in range(5):
                out[0][c, rows, :] = entering[c]
                out[2][c, rows, :] = sent[c]
                for d in range(5):
                    out[1][c, d, rows, :] = through[c][d]
            if carry_total:
                whole = matmat(downstream, pick(after, their_total, own_total))
                for c in range(5):
                    for d in range(5):
                        out[3][c, d, rows, :] = whole[c][d]

    operands = [leaving, total, other, other_total] + ([] if first else [near, reach])
    return pl.pallas_call(
        kernel,
        out_shape=tuple(jax.ShapeDtypeStruct(shape, F32) for shape in outs),
        in_specs=vmem_specs(len(operands)),
        out_specs=tuple(vmem_specs(len(outs))),
        compiler_params=pltpu.CompilerParams(vmem_limit_bytes=4 << 20),
        name="join",
    )(*[in_vmem(v) for v in operands])


def relay(total, leaving, backward):
    size = lax.axis_size("sweep")
    stages = size.bit_length() - 1
    near = reach = None
    for stage in range(stages):
        pairs = [(i, i ^ (1 << stage)) for i in range(size)]
        other = lax.ppermute(leaving, "sweep", pairs)
        if stage == stages - 1:
            return (near, reach, other), leaving
        other_total = lax.ppermute(total, "sweep", pairs)
        carry_total = stage + 2 < stages
        joined = join(stage, backward, near, reach, leaving, total, other, other_total, carry_total)
        near, reach, leaving = joined[:3]
        if carry_total:
            total = joined[3]


def per_device(source, psi_old, lateral, lower_jac, upper_jac, diag_inv, face_weight, face_cell,
               face_owner, face_node, face_count):
    bulk = lax.axis_size("bulk")
    devices = bulk * lax.axis_size("sweep")
    low_pairs = [(i, i ^ 1) for i in range(bulk) if i ^ 1 < bulk]
    high_pairs = [(i, j) for i in range(bulk) for j in [i + 1 if i % 2 else i - 1] if 0 <= j < bulk]
    low_edge, high_edge = edge_rows(psi_old)
    first = lax.ppermute(low_edge, "bulk", low_pairs)
    second = lax.ppermute(high_edge, "bulk", high_pairs)

    ratio, total, scaled, leaving = forward_local(source, psi_old, lateral, first, second, lower_jac, diag_inv)
    arriving, joined = relay(total, leaving, False)
    upper_jac, joined = lax.optimization_barrier((upper_jac, joined))
    back_ratio, back_total = backward_matrices(upper_jac, diag_inv)
    field, leaving = forward_then_back(scaled, arriving, ratio, back_ratio)
    back_total, leaving = lax.optimization_barrier((back_total, leaving))
    arriving, _ = relay(back_total, leaving, True)

    slots = face_cell.shape[0]
    rows = (slots // LANES, LANES)
    slot, nodes = face_slots(face_owner.reshape(rows), face_node.reshape(rows), bulk)
    adjoint, send = backward_and_faces(field, arriving, back_ratio, face_count, face_cell.reshape(rows),
                                       face_weight, slot, nodes, devices, bulk)
    got = lax.all_to_all(send, ("sweep", "bulk"), 0, 0, tiled=True)
    return adjoint, node_sums(got).reshape(NODES_DEV)


def solution(mesh):
    placed = (
        P("sweep", None, "bulk", None),
        P("sweep", None, "bulk", None),
        P("sweep", None, "bulk", None),
        P("sweep", None, None, "bulk", None),
        P("sweep", None, None, "bulk", None),
        P("sweep", None, None, "bulk", None),
        P(None, ("sweep", "bulk")),
        P(("sweep", "bulk")),
        P(("sweep", "bulk"), None),
        P(("sweep", "bulk")),
        P(("sweep", "bulk")),
    )
    return jax.shard_map(
        per_device,
        mesh=mesh,
        in_specs=placed,
        out_specs=(P("sweep", None, "bulk", None), P("bulk")),
        check_vma=False,
    )
```

time: 321 us -> 62.3 us (0.19)
  waiting for transfers between devices: 145 us -> 7.26 us
  other arithmetic: 81.3 us -> 0 us
  local copies, waits for them, and re-layouts: 52.8 us -> 9.42 us
  Pallas kernels: 0 us -> 21.4 us
  between operations: 19.2 us -> 1.42 us
  blocking collectives: 0 us -> 15.5 us
  starting transfers between devices: 20.7 us -> 6.98 us
    psum x1 -> x0, waiting for transfers between devices: 132 us -> none  [per_device(): summed = lax.psum(dense_sums, ('sweep', 'bulk'))]
    reduce_sum x387 -> x0, other arithmetic: 57.9 us -> none  [the longest x260 46.8 us: matvec(): return jnp.sum(matrix * vector[None], axis=1)]
    gather x1 -> x0, local copies, waits for them, and re-layouts: 22.1 us -> none  [per_device(): at_faces = adjoint[plane_index, :, column_index, depth_index]]
    pallas_call x0 -> x9, Pallas kernels: none -> 21.4 us  [the longest x1 5.73 us: forward_local(): pl.pallas_call(kernel, out_shape=(VMEM(coupled.shape, F32), jax.ShapeDtyp...]
    concatenate x2 -> x0, local copies, waits for them, and re-layouts: 16.5 us -> none  [backward_sweep(): lax.scan(backward_advance, start, (forward_field, upper_jac, diag_inv), r...]
    all_to_all x0 -> x1, blocking collectives: none -> 15.5 us  [per_device(): got = lax.all_to_all(send, ('sweep', 'bulk'), 0, 0, tiled=True)]
    ppermute x8, starting transfers between devices: 20.6 us -> 6.98 us  [the longest x4 3.15 us: relay(): other = lax.ppermute(leaving, 'sweep', pairs)]
    scatter-add x1 -> x0, other arithmetic: 12.2 us -> none  [per_device(): jax.ops.segment_sum(partial_value, owner_dev * NODES_DEV + face_node, num...]
  transfers between devices with their start and end apart: 9 -> 8, of which waited for: 7 -> 4; matrix products, arithmetic and copies ran while one was open for 6% -> 0% of each run, Pallas kernels for 0% -> 8%
where the time goes in v2:
time: 62.3 us; the launch traced here: 62 us
  Pallas kernels  21.4 us (34%)
  blocking collectives  15.5 us (25%)
  local copies, waits for them, and re-layouts  9.42 us (15%)
  waiting for transfers between devices  7.26 us (12%)
  starting transfers between devices  6.98 us (11%)
  between operations  1.42 us (2%)
    all_to_all x1, blocking collectives, per_device(): got = lax.all_to_all(send, ('sweep', 'bulk'), 0, 0, tiled=True)  15.5 us
    unnamed x22, local copies, waits for them, and re-layouts  9.42 us
    pallas_call x1, Pallas kernels, forward_local(): pl.pallas_call(kernel, out_shape=(VMEM(coupled.shape, F32), jax.ShapeDtyp...  5.73 us
    pallas_call x1, Pallas kernels, backward_and_faces(): pl.pallas_call(kernel, out_shape=(jax.ShapeDtypeStruct(field.shape, F32),...  5.54 us
    ppermute x4, waiting for transfers between devices, relay(): other = lax.ppermute(leaving, 'sweep', pairs)  4.42 us
    pallas_call x1, Pallas kernels, backward_matrices(): pl.pallas_call(kernel, out_shape=(VMEM(coupled.shape, F32), jax.ShapeDtyp...  4.33 us
    pallas_call x1, Pallas kernels, node_sums(): pl.pallas_call(kernel, out_shape=jax.ShapeDtypeStruct((side, LANES), F32)...  3.56 us
    ppermute x4, starting transfers between devices, relay(): other = lax.ppermute(leaving, 'sweep', pairs)  3.15 us
  transfers between devices with their start and end apart: 8, of which 4 were waited for; matrix products, arithmetic and copies ran while one was open for 0% of the time, Pallas kernels for 8%

profile of v2, /device:TPU:0, one launch (start us, length us, event | category | flops | bytes accessed | tf_op | source)
XLA Modules:
  0.0 62.0 jit_solution(1813834981577967307)
XLA Ops:
  0.6 0.0 copy-start.4
  0.6 1.3 %copy-done.4 = f32[32,5,16,128]{3,2,1,0:T(8,128)S(1)} copy-done((f32[32,5,16,128]{3,2,1,0:T(8,128)S(1)}, f32[32,5,16,128]{3,2,1,0:T(8,128)}, u32[]{:S(2)}) %copy-start.4) | copy-done | bytes 1310744
  1.9 0.1 edge_rows.1
  2.1 3.0 %collective-permute-start = (f32[32,5,128]{2,1,0:T(8,128)S(1)}, f32[32,5,128]{2,1,0:T(8,128)S(1)}, u32[]{:S(2)}, u32[]{:S(2)}) collective-permute-start(f32[32,5,128]{2,1,0:T(8,128)S(1)} %get-tuple-element.25), channel_id=1, source_target_pairs={{0,1},{1,0},{2,3},{3,2},{4,5},{5,4},{6,7},{7,6},{8,9},{9,8},{10,11... | collective-permute-start | bytes 245768 | tf_op jit(solution)/shard_map/ppermute | solution.py:529
  5.1 0.7 %collective-permute-start.1 = (f32[32,5,128]{2,1,0:T(8,128)S(1)}, f32[32,5,128]{2,1,0:T(8,128)S(1)}, u32[]{:S(2)}, u32[]{:S(2)}) collective-permute-start(f32[32,5,128]{2,1,0:T(8,128)S(1)} %get-tuple-element.26), channel_id=1, source_target_pairs={{1,2},{2,1},{3,4},{4,3},{5,6},{6,5},{9,10},{10,9},{11,12},{12,11},... | collective-permute-start | bytes 245768 | tf_op jit(solution)/shard_map/ppermute | solution.py:530
  5.8 2.8 %collective-permute-done.first_ref = f32[32,5,128]{2,1,0:T(8,128)S(1)} collective-permute-done((f32[32,5,128]{2,1,0:T(8,128)S(1)}, f32[32,5,128]{2,1,0:T(8,128)S(1)}, u32[]{:S(2)}, u32[]{:S(2)}) %collective-permute-start) | collective-permute-done | bytes 81952 | tf_op jit(solution)/shard_map/ppermute | solution.py:529
  8.6 0.0 collective-permute-done.1.second_ref
  8.6 0.0 copy-start
  8.6 2.9 %copy-done = f32[32,5,5,16,128]{4,3,2,1,0:T(8,128)S(1)} copy-done((f32[32,5,5,16,128]{4,3,2,1,0:T(8,128)S(1)}, f32[32,5,5,16,128]{4,3,2,1,0:T(8,128)}, u32[]{:S(2)}) %copy-start) | copy-done | bytes 6553624
  11.5 0.0 copy-start.3
  11.5 2.9 %copy-done.3 = f32[32,5,5,16,128]{4,3,2,1,0:T(8,128)S(1)} copy-done((f32[32,5,5,16,128]{4,3,2,1,0:T(8,128)S(1)}, f32[32,5,5,16,128]{4,3,2,1,0:T(8,128)}, u32[]{:S(2)}) %copy-start.3) | copy-done | bytes 6553624
  14.3 0.0 copy-start.5
  14.3 1.3 %copy-done.5 = f32[32,5,16,128]{3,2,1,0:T(8,128)S(1)} copy-done((f32[32,5,16,128]{3,2,1,0:T(8,128)S(1)}, f32[32,5,16,128]{3,2,1,0:T(8,128)}, u32[]{:S(2)}) %copy-start.5) | copy-done | bytes 1310744
  15.6 0.0 copy-start.6
  15.6 1.0 %copy-done.6 = f32[32,2,16,128]{3,2,1,0:T(8,128)S(1)} copy-done((f32[32,2,16,128]{3,2,1,0:T(8,128)S(1)}, f32[32,2,16,128]{3,2,1,0:T(8,128)}, u32[]{:S(2)}) %copy-start.6) | copy-done | bytes 524312
  16.7 0.0 copy-start.1
  16.7 0.0 copy-start.2
  16.7 5.7 %forward_local.1 = (f32[32,5,5,16,128]{4,3,2,1,0:T(8,128)S(1)}, f32[5,5,16,128]{3,2,1,0:T(8,128)S(1)}, f32[32,5,16,128]{3,2,1,0:T(8,128)S(1)}, f32[5,16,128]{2,1,0:T(8,128)S(1)}) custom-call(f32[32,5,16,128]{3,2,1,0:T(8,128)S(1)} %copy-done.5, f32[32,5,16,128]{3,2,1,0:T(8,128)S(1)} %copy-done.4, f32[32,2,16,128]{3,2,1,0:T(8,128)S(1)} %copy-done.6, ...), custom_call_target="tpu_custom_call" | custom-call | tf_op jit(solution)/shard_map/forward_local/pallas_call | solution.py:121
  22.4 0.1 collective-permute-start.3
  22.5 0.5 collective-permute-start.2
  23.0 1.0 %collective-permute-done.2.refs_2_ = f32[5,16,128]{2,1,0:T(8,128)S(1)} collective-permute-done((f32[5,16,128]{2,1,0:T(8,128)S(1)}, f32[5,16,128]{2,1,0:T(8,128)S(1)}, u32[]{:S(2)}, u32[]{:S(2)}) %collective-permute-start.2) | collective-permute-done | bytes 40992 | tf_op jit(solution)/shard_map/ppermute | solution.py:511
  24.0 0.0 collective-permute-done.3.refs_3_
  24.0 0.1 join.2
  24.1 1.8 %collective-permute-start.4 = (f32[5,16,128]{2,1,0:T(8,128)S(1)}, f32[5,16,128]{2,1,0:T(8,128)S(1)}, u32[]{:S(2)}, u32[]{:S(2)}) collective-permute-start(f32[5,16,128]{2,1,0:T(8,128)S(1)} %get-tuple-element.32), channel_id=1, source_target_pairs={{0,16},{8,24},{16,0},{24,8},{1,17},{9,25},{17,1},{25,9},{2,18},{10... | collective-permute-start | bytes 122888 | tf_op jit(solution)/shard_map/ppermute | solution.py:511
  25.8 0.0 copy-done.1
  25.8 0.0 copy-done.2
  25.8 4.3 %backward_matrices.1 = (f32[32,5,5,16,128]{4,3,2,1,0:T(8,128)S(1)}, f32[5,5,16,128]{3,2,1,0:T(8,128)S(1)}) custom-call(f32[32,5,5,16,128]{4,3,2,1,0:T(8,128)S(1)} %copy-done.2, f32[32,5,5,16,128]{4,3,2,1,0:T(8,128)S(1)} %copy-done.1), custom_call_target="tpu_custom_call" | custom-call | flops 4000000 | bytes 20000000 | tf_op jit(solution)/shard_map/backward_matrices/pallas_call | solution.py:151
  30.2 0.0 collective-permute-done.4.other_ref
  30.2 0.0 copy-start.9
  30.2 0.0 copy-start.10
  30.2 0.0 copy-start.7
  30.2 0.0 copy-start.8
  30.2 1.4 %forward_then_back.1 = (f32[32,5,16,128]{3,2,1,0:T(8,128)S(1)}, f32[5,16,128]{2,1,0:T(8,128)S(1)}) custom-call(f32[32,5,16,128]{3,2,1,0:T(8,128)S(1)} %get-tuple-element.27.scaled_ref, f32[5,16,128]{2,1,0:T(8,128)S(1)} %get-tuple-element.30.near_ref, f32[5,5,16,128]{3,2,1,0:T(8,128)S(1)} %get-tuple-element.31.reach_ref, ...), custom_call_target="tpu_custom_call" | custom-call | tf_op jit(solution)/shard_map/forward_then_back/pallas_call | solution.py:193
  31.6 0.1 collective-permute-start.6
  31.7 0.5 collective-permute-start.5
  32.2 1.0 %collective-permute-done.5.refs_2_ = f32[5,16,128]{2,1,0:T(8,128)S(1)} collective-permute-done((f32[5,16,128]{2,1,0:T(8,128)S(1)}, f32[5,16,128]{2,1,0:T(8,128)S(1)}, u32[]{:S(2)}, u32[]{:S(2)}) %collective-permute-start.5) | collective-permute-done | bytes 40992 | tf_op jit(solution)/shard_map/ppermute | solution.py:511
  33.2 0.0 collective-permute-done.6.refs_3_
  33.2 0.1 join.3
  33.3 0.4 collective-permute-start.7
  34.3 0.0 copy-done.9
  34.3 0.0 copy-done.10
  34.3 0.6 face_slots.1
  34.9 2.4 %collective-permute-done.7.other_ref = f32[5,16,128]{2,1,0:T(8,128)S(1)} collective-permute-done((f32[5,16,128]{2,1,0:T(8,128)S(1)}, f32[5,16,128]{2,1,0:T(8,128)S(1)}, u32[]{:S(2)}, u32[]{:S(2)}) %collective-permute-start.7) | collective-permute-done | bytes 40992 | tf_op jit(solution)/shard_map/ppermute | solution.py:511
  37.3 0.0 copy-done.7
  37.3 0.0 copy-done.8
  37.3 5.5 %backward_and_faces.1 = (f32[32,5,16,128]{3,2,1,0:T(8,128)}, f32[32,8,128]{2,1,0:T(8,128)S(1)}) custom-call(s32[1]{0:T(128)S(6)} %copy.13.count_ref, f32[32,5,16,128]{3,2,1,0:T(8,128)S(1)} %get-tuple-element.36.field_ref, f32[5,16,128]{2,1,0:T(8,128)S(1)} %get-tuple-element.41.near_ref, f32[5,5,16,128]{3,2,1,0:T(8,128)S(1)} %get-tuple-element.42.reach_ref, ...), custom_call_target="tpu_custom_call" | custom-call | tf_op jit(solution)/shard_map/backward_and_faces/pallas_call | solution.py:355
  42.9 15.5 %all_to_all.5.got_ref = f32[32,8,128]{2,1,0:T(8,128)S(1)} all-to-all(f32[32,8,128]{2,1,0:T(8,128)S(1)} %get-tuple-element.47), channel_id=1, replica_groups=mesh['sweep'=4,'bulk'=8] {'sweep','bulk'}, dimensions={0} | all-to-all | bytes 262144 | tf_op jit(solution)/shard_map/all_to_all | solution.py:545
  58.4 3.6 %node_sums.1 = f32[128,128]{1,0:T(8,128)} custom-call(f32[32,8,128]{2,1,0:T(8,128)S(1)} %all_to_all.5.got_ref), custom_call_target="tpu_custom_call" | custom-call | tf_op jit(solution)/shard_map/node_sums/pallas_call | solution.py:412
Async XLA Ops:
  0.6 1.3 %copy-start.4 = (f32[32,5,16,128]{3,2,1,0:T(8,128)S(1)}, f32[32,5,16,128]{3,2,1,0:T(8,128)}, u32[]{:S(2)}) copy-start(f32[32,5,16,128]{3,2,1,0:T(8,128)} %psi_ref.3) | copy-start | bytes 3932164
  2.1 6.5 %collective-permute-start = (f32[32,5,128]{2,1,0:T(8,128)S(1)}, f32[32,5,128]{2,1,0:T(8,128)S(1)}, u32[]{:S(2)}, u32[]{:S(2)}) collective-permute-start(f32[32,5,128]{2,1,0:T(8,128)S(1)} %get-tuple-element.25), channel_id=1, source_target_pairs={{0,1},{1,0},{2,3},{3,2},{4,5},{5,4},{6,7},{7,6},{8,9},{9,8},{10,11... | collective-permute-start | bytes 245768 | tf_op jit(solution)/shard_map/ppermute | solution.py:529
  5.1 3.5 %collective-permute-start.1 = (f32[32,5,128]{2,1,0:T(8,128)S(1)}, f32[32,5,128]{2,1,0:T(8,128)S(1)}, u32[]{:S(2)}, u32[]{:S(2)}) collective-permute-start(f32[32,5,128]{2,1,0:T(8,128)S(1)} %get-tuple-element.26), channel_id=1, source_target_pairs={{1,2},{2,1},{3,4},{4,3},{5,6},{6,5},{9,10},{10,9},{11,12},{12,11},... | collective-permute-start | bytes 245768 | tf_op jit(solution)/shard_map/ppermute | solution.py:530
  8.6 2.9 %copy-start = (f32[32,5,5,16,128]{4,3,2,1,0:T(8,128)S(1)}, f32[32,5,5,16,128]{4,3,2,1,0:T(8,128)}, u32[]{:S(2)}) copy-start(f32[32,5,5,16,128]{4,3,2,1,0:T(8,128)} %inv_ref.3) | copy-start | bytes 19660804
  11.5 2.9 %copy-start.3 = (f32[32,5,5,16,128]{4,3,2,1,0:T(8,128)S(1)}, f32[32,5,5,16,128]{4,3,2,1,0:T(8,128)}, u32[]{:S(2)}) copy-start(f32[32,5,5,16,128]{4,3,2,1,0:T(8,128)} %coupled_ref.1) | copy-start | bytes 19660804
  14.3 1.3 %copy-start.5 = (f32[32,5,16,128]{3,2,1,0:T(8,128)S(1)}, f32[32,5,16,128]{3,2,1,0:T(8,128)}, u32[]{:S(2)}) copy-start(f32[32,5,16,128]{3,2,1,0:T(8,128)} %source_ref.1) | copy-start | bytes 3932164
  15.6 1.0 %copy-start.6 = (f32[32,2,16,128]{3,2,1,0:T(8,128)S(1)}, f32[32,2,16,128]{3,2,1,0:T(8,128)}, u32[]{:S(2)}) copy-start(f32[32,2,16,128]{3,2,1,0:T(8,128)} %lateral_ref.1) | copy-start | bytes 1572868
  16.7 9.2 %copy-start.1 = (f32[32,5,5,16,128]{4,3,2,1,0:T(8,128)S(1)}, f32[32,5,5,16,128]{4,3,2,1,0:T(8,128)}, u32[]{:S(2)}) copy-start(f32[32,5,5,16,128]{4,3,2,1,0:T(8,128)} %inv_ref.3) | copy-start | bytes 19660804
  16.7 9.2 %copy-start.2 = (f32[32,5,5,16,128]{4,3,2,1,0:T(8,128)S(1)}, f32[32,5,5,16,128]{4,3,2,1,0:T(8,128)}, u32[]{:S(2)}) copy-start(f32[32,5,5,16,128]{4,3,2,1,0:T(8,128)} %coupled_ref.2) | copy-start | bytes 19660804
  22.4 1.6 %collective-permute-start.3 = (f32[5,5,16,128]{3,2,1,0:T(8,128)S(1)}, f32[5,5,16,128]{3,2,1,0:T(8,128)S(1)}, u32[]{:S(2)}, u32[]{:S(2)}) collective-permute-start(f32[5,5,16,128]{3,2,1,0:T(8,128)S(1)} %get-tuple-element.29.refs_1_), channel_id=1, source_target_pairs={{0,8},{8,0},{16,24},{24,16},{1,9},{9,1},{17,25},{25,17},{2,10},{10... | collective-permute-start | bytes 614408 | tf_op jit(solution)/shard_map/ppermute | solution.py:514
  22.5 1.5 %collective-permute-start.2 = (f32[5,16,128]{2,1,0:T(8,128)S(1)}, f32[5,16,128]{2,1,0:T(8,128)S(1)}, u32[]{:S(2)}, u32[]{:S(2)}) collective-permute-start(f32[5,16,128]{2,1,0:T(8,128)S(1)} %get-tuple-element.28.refs_0_), channel_id=1, source_target_pairs={{0,8},{8,0},{16,24},{24,16},{1,9},{9,1},{17,25},{25,17},{2,10},{10... | collective-permute-start | bytes 122888 | tf_op jit(solution)/shard_map/ppermute | solution.py:511
  24.1 6.1 %collective-permute-start.4 = (f32[5,16,128]{2,1,0:T(8,128)S(1)}, f32[5,16,128]{2,1,0:T(8,128)S(1)}, u32[]{:S(2)}, u32[]{:S(2)}) collective-permute-start(f32[5,16,128]{2,1,0:T(8,128)S(1)} %get-tuple-element.32), channel_id=1, source_target_pairs={{0,16},{8,24},{16,0},{24,8},{1,17},{9,25},{17,1},{25,9},{2,18},{10... | collective-permute-start | bytes 122888 | tf_op jit(solution)/shard_map/ppermute | solution.py:511
  30.2 4.1 %copy-start.9 = (s32[2048,1]{0,1:T(1,128)S(1)}, s32[2048,1]{0,1:T(1,128)}, u32[]{:S(2)}) copy-start(s32[2048,1]{0,1:T(1,128)} %param.19) | copy-start | bytes 24580
  30.2 4.1 %copy-start.10 = (s32[2048]{0:T(1024)S(1)}, s32[2048]{0:T(1024)}, u32[]{:S(2)}) copy-start(s32[2048]{0:T(1024)} %param.20) | copy-start | bytes 24580
  30.2 7.1 %copy-start.7 = (f32[5,2048]{1,0:T(8,128)S(1)}, f32[5,2048]{1,0:T(8,128)}, u32[]{:S(2)}) copy-start(f32[5,2048]{1,0:T(8,128)} %weight_ref.1) | copy-start | bytes 122884
  30.2 7.1 %copy-start.8 = (s32[2048]{0:T(1024)S(1)}, s32[2048]{0:T(1024)}, u32[]{:S(2)}) copy-start(s32[2048]{0:T(1024)} %param.18) | copy-start | bytes 24580
  31.6 1.6 %collective-permute-start.6 = (f32[5,5,16,128]{3,2,1,0:T(8,128)S(1)}, f32[5,5,16,128]{3,2,1,0:T(8,128)S(1)}, u32[]{:S(2)}, u32[]{:S(2)}) collective-permute-start(f32[5,5,16,128]{3,2,1,0:T(8,128)S(1)} %get-tuple-element.40.refs_1_), channel_id=1, source_target_pairs={{0,8},{8,0},{16,24},{24,16},{1,9},{9,1},{17,25},{25,17},{2,10},{10... | collective-permute-start | bytes 614408 | tf_op jit(solution)/shard_map/ppermute | solution.py:514
  31.7 1.5 %collective-permute-start.5 = (f32[5,16,128]{2,1,0:T(8,128)S(1)}, f32[5,16,128]{2,1,0:T(8,128)S(1)}, u32[]{:S(2)}, u32[]{:S(2)}) collective-permute-start(f32[5,16,128]{2,1,0:T(8,128)S(1)} %get-tuple-element.39.refs_0_), channel_id=1, source_target_pairs={{0,8},{8,0},{16,24},{24,16},{1,9},{9,1},{17,25},{25,17},{2,10},{10... | collective-permute-start | bytes 122888 | tf_op jit(solution)/shard_map/ppermute | solution.py:511
  33.3 4.1 %collective-permute-start.7 = (f32[5,16,128]{2,1,0:T(8,128)S(1)}, f32[5,16,128]{2,1,0:T(8,128)S(1)}, u32[]{:S(2)}, u32[]{:S(2)}) collective-permute-start(f32[5,16,128]{2,1,0:T(8,128)S(1)} %get-tuple-element.43), channel_id=1, source_target_pairs={{0,16},{8,24},{16,0},{24,8},{1,17},{9,25},{17,1},{25,9},{2,18},{10... | collective-permute-start | bytes 122888 | tf_op jit(solution)/shard_map/ppermute | solution.py:511

commit v3 on v2

--- a/solution.py
+++ b/solution.py
@@ -29,6 +29,10 @@
     return pltpu.with_memory_space_constraint(value, VMEM)
 
 
+def in_hbm(value):
+    return pltpu.with_memory_space_constraint(value, pltpu.HBM)
+
+
 def vmem_specs(n):
     return [pl.BlockSpec(memory_space=VMEM)] * n
 
@@ -62,23 +66,31 @@
     planes, fields, width, _ = psi.shape
     shape = (planes, fields, LANES)
 
-    def kernel(psi_ref, low_ref, high_ref):
+    def kernel(psi_hbm, low_ref, high_ref, head_ref, tail_ref, sems):
+        copies = [
+            pltpu.make_async_copy(psi_hbm.at[:, :, 0, :], head_ref, sems.at[0]),
+            pltpu.make_async_copy(psi_hbm.at[:, :, width - 1, :], tail_ref, sems.at[1]),
+        ]
+        for copy in copies:
+            copy.start()
         is_odd = lax.rem(lax.axis_index("bulk"), 2) == 1
+        for copy in copies:
+            copy.wait()
         for i in range(planes):
-            head = psi_ref[i, :, 0, :]
-            tail = psi_ref[i, :, width - 1, :]
+            head, tail = head_ref[i], tail_ref[i]
             low_ref[i] = jnp.where(is_odd, head, tail)
             high_ref[i] = jnp.where(is_odd, tail, head)
 
     return pl.pallas_call(
         kernel,
         out_shape=(jax.ShapeDtypeStruct(shape, F32), jax.ShapeDtypeStruct(shape, F32)),
-        in_specs=vmem_specs(1),
+        in_specs=[pl.BlockSpec(memory_space=pltpu.HBM)],
         out_specs=tuple(vmem_specs(2)),
+        scratch_shapes=[VMEM(shape, F32), VMEM(shape, F32), pltpu.SemaphoreType.DMA((2,))],
         compiler_params=pltpu.CompilerParams(vmem_limit_bytes=4 << 20),
-        cost_estimate=pl.CostEstimate(flops=4_000_000, bytes_accessed=60_000_000, transcendentals=0),
+        cost_estimate=pl.CostEstimate(flops=10_000_000_000, bytes_accessed=20_000_000, transcendentals=0),
         name="edge_rows",
-    )(in_vmem(psi))
+    )(in_hbm(psi))
 
 
 def forward_local(source, psi, lateral, first, second, coupled, inv):

time: 62.3 us -> 54.3 us (0.87)
  local copies, waits for them, and re-layouts: 9.42 us -> 0.05 us
  Pallas kernels: 21.4 us -> 22.4 us
    unnamed x22, local copies, waits for them, and re-layouts: 9.42 us -> 0.05 us
    pallas_call x1, Pallas kernels: 0.12 us -> 1.15 us  [edge_rows(): pl.pallas_call(kernel, out_shape=(jax.ShapeDtypeStruct(shape, F32), jax.S...]
  transfers between devices with their start and end apart: 8 -> 8, of which waited for: 4 -> 4; matrix products, arithmetic and copies ran while one was open for 0% -> 0% of each run, Pallas kernels for 8% -> 9%
where the time goes in v3:
time: 54.3 us; the launch traced here: 54.1 us
  Pallas kernels  22.4 us (41%)
  blocking collectives  15.9 us (29%)
  waiting for transfers between devices  7.13 us (13%)
  starting transfers between devices  7.11 us (13%)
  between operations  1.48 us (3%)
    all_to_all x1, blocking collectives, per_device(): got = lax.all_to_all(send, ('sweep', 'bulk'), 0, 0, tiled=True)  15.9 us
    pallas_call x1, Pallas kernels, forward_local(): pl.pallas_call(kernel, out_shape=(VMEM(coupled.shape, F32), jax.ShapeDtyp...  5.75 us
    pallas_call x1, Pallas kernels, backward_and_faces(): pl.pallas_call(kernel, out_shape=(jax.ShapeDtypeStruct(field.shape, F32),...  5.54 us
    ppermute x4, waiting for transfers between devices, relay(): other = lax.ppermute(leaving, 'sweep', pairs)  4.43 us
    pallas_call x1, Pallas kernels, backward_matrices(): pl.pallas_call(kernel, out_shape=(VMEM(coupled.shape, F32), jax.ShapeDtyp...  4.33 us
    pallas_call x1, Pallas kernels, node_sums(): pl.pallas_call(kernel, out_shape=jax.ShapeDtypeStruct((side, LANES), F32)...  3.55 us
    ppermute x4, starting transfers between devices, relay(): other = lax.ppermute(leaving, 'sweep', pairs)  3.15 us
    ppermute x1, starting transfers between devices, per_device(): first = lax.ppermute(low_edge, 'bulk', low_pairs)  3.03 us
  transfers between devices with their start and end apart: 8, of which 4 were waited for; matrix products, arithmetic and copies ran while one was open for 0% of the time, Pallas kernels for 9%

profile of v3, /device:TPU:0, one launch (start us, length us, event | category | flops | bytes accessed | tf_op | source)
XLA Modules:
  0.0 54.1 jit_solution(4622817944821403720)
XLA Ops:
  0.6 0.0 copy-start.3
  0.6 0.0 copy-start.2
  0.7 0.0 copy-start.4
  0.7 0.0 copy-start.1
  0.7 0.0 copy-start
  0.7 1.2 %edge_rows.1 = (f32[32,5,128]{2,1,0:T(8,128)S(1)}, f32[32,5,128]{2,1,0:T(8,128)S(1)}) custom-call(f32[32,5,16,128]{3,2,1,0:T(8,128)} %psi_ref.1), custom_call_target="tpu_custom_call" | custom-call | flops 10000000000 | bytes 20000000 | tf_op jit(solution)/shard_map/edge_rows/pallas_call | solution.py:84
  1.8 3.0 %collective-permute-start = (f32[32,5,128]{2,1,0:T(8,128)S(1)}, f32[32,5,128]{2,1,0:T(8,128)S(1)}, u32[]{:S(2)}, u32[]{:S(2)}) collective-permute-start(f32[32,5,128]{2,1,0:T(8,128)S(1)} %get-tuple-element.25), channel_id=1, source_target_pairs={{0,1},{1,0},{2,3},{3,2},{4,5},{5,4},{6,7},{7,6},{8,9},{9,8},{10,11... | collective-permute-start | bytes 245768 | tf_op jit(solution)/shard_map/ppermute | solution.py:541
  4.9 0.0 slice-start
  4.9 0.0 slice-start.1
  4.9 0.8 %collective-permute-start.1 = (f32[32,5,128]{2,1,0:T(8,128)S(1)}, f32[32,5,128]{2,1,0:T(8,128)S(1)}, u32[]{:S(2)}, u32[]{:S(2)}) collective-permute-start(f32[32,5,128]{2,1,0:T(8,128)S(1)} %get-tuple-element.26), channel_id=1, source_target_pairs={{1,2},{2,1},{3,4},{4,3},{5,6},{6,5},{9,10},{10,9},{11,12},{12,11},... | collective-permute-start | bytes 245768 | tf_op jit(solution)/shard_map/ppermute | solution.py:542
  5.7 2.7 %collective-permute-done.first_ref = f32[32,5,128]{2,1,0:T(8,128)S(1)} collective-permute-done((f32[32,5,128]{2,1,0:T(8,128)S(1)}, f32[32,5,128]{2,1,0:T(8,128)S(1)}, u32[]{:S(2)}, u32[]{:S(2)}) %collective-permute-start) | collective-permute-done | bytes 81952 | tf_op jit(solution)/shard_map/ppermute | solution.py:541
  8.4 0.0 collective-permute-done.1.second_ref
  8.4 0.0 copy-done.3
  8.4 0.0 copy-done.2
  8.4 0.0 copy-done.4
  8.4 0.0 copy-done.1
  8.4 0.0 copy-done
  8.4 5.7 %forward_local.1 = (f32[32,5,5,16,128]{4,3,2,1,0:T(8,128)S(1)}, f32[5,5,16,128]{3,2,1,0:T(8,128)S(1)}, f32[32,5,16,128]{3,2,1,0:T(8,128)S(1)}, f32[5,16,128]{2,1,0:T(8,128)S(1)}) custom-call(f32[32,5,16,128]{3,2,1,0:T(8,128)S(1)} %copy-done.2, f32[32,5,16,128]{3,2,1,0:T(8,128)S(1)} %copy-done.3, f32[32,2,16,128]{3,2,1,0:T(8,128)S(1)} %copy-done.4, ...), custom_call_target="tpu_custom_call" | custom-call | tf_op jit(solution)/shard_map/forward_local/pallas_call | solution.py:133
  14.2 0.1 collective-permute-start.3
  14.2 0.5 collective-permute-start.2
  14.7 1.0 %collective-permute-done.2.refs_2_ = f32[5,16,128]{2,1,0:T(8,128)S(1)} collective-permute-done((f32[5,16,128]{2,1,0:T(8,128)S(1)}, f32[5,16,128]{2,1,0:T(8,128)S(1)}, u32[]{:S(2)}, u32[]{:S(2)}) %collective-permute-start.2) | collective-permute-done | bytes 40992 | tf_op jit(solution)/shard_map/ppermute | solution.py:523
  15.7 0.0 collective-permute-done.3.refs_3_
  15.7 0.1 join.2
  15.8 1.8 %collective-permute-start.4 = (f32[5,16,128]{2,1,0:T(8,128)S(1)}, f32[5,16,128]{2,1,0:T(8,128)S(1)}, u32[]{:S(2)}, u32[]{:S(2)}) collective-permute-start(f32[5,16,128]{2,1,0:T(8,128)S(1)} %get-tuple-element.32), channel_id=1, source_target_pairs={{0,16},{8,24},{16,0},{24,8},{1,17},{9,25},{17,1},{25,9},{2,18},{10... | collective-permute-start | bytes 122888 | tf_op jit(solution)/shard_map/ppermute | solution.py:523
  17.6 0.0 slice-done
  17.6 0.0 slice-done.1
  17.6 4.3 %backward_matrices.1 = (f32[32,5,5,16,128]{4,3,2,1,0:T(8,128)S(1)}, f32[5,5,16,128]{3,2,1,0:T(8,128)S(1)}) custom-call(f32[32,5,5,16,128]{4,3,2,1,0:T(8,128)S(1)} %bitcast.5, f32[32,5,5,16,128]{4,3,2,1,0:T(8,128)S(1)} %copy-done), custom_call_target="tpu_custom_call" | custom-call | flops 4000000 | bytes 20000000 | tf_op jit(solution)/shard_map/backward_matrices/pallas_call | solution.py:163
  21.9 0.0 collective-permute-done.4.other_ref
  21.9 0.0 copy-start.7
  22.0 0.0 copy-start.8
  22.0 0.0 copy-start.5
  22.0 0.0 copy-start.6
  22.0 1.4 %forward_then_back.1 = (f32[32,5,16,128]{3,2,1,0:T(8,128)S(1)}, f32[5,16,128]{2,1,0:T(8,128)S(1)}) custom-call(f32[32,5,16,128]{3,2,1,0:T(8,128)S(1)} %get-tuple-element.27.scaled_ref, f32[5,16,128]{2,1,0:T(8,128)S(1)} %get-tuple-element.30.near_ref, f32[5,5,16,128]{3,2,1,0:T(8,128)S(1)} %get-tuple-element.31.reach_ref, ...), custom_call_target="tpu_custom_call" | custom-call | tf_op jit(solution)/shard_map/forward_then_back/pallas_call | solution.py:205
  23.4 0.1 collective-permute-start.6
  23.5 0.5 collective-permute-start.5
  24.0 1.0 %collective-permute-done.5.refs_2_ = f32[5,16,128]{2,1,0:T(8,128)S(1)} collective-permute-done((f32[5,16,128]{2,1,0:T(8,128)S(1)}, f32[5,16,128]{2,1,0:T(8,128)S(1)}, u32[]{:S(2)}, u32[]{:S(2)}) %collective-permute-start.5) | collective-permute-done | bytes 40992 | tf_op jit(solution)/shard_map/ppermute | solution.py:523
  25.0 0.0 collective-permute-done.6.refs_3_
  25.0 0.1 join.3
  25.0 0.4 collective-permute-start.7
  26.1 0.0 copy-done.7
  26.1 0.0 copy-done.8
  26.1 0.6 %face_slots.1 = (s32[16,128]{1,0:T(8,128)S(1)}, f32[32,128]{1,0:T(8,128)S(1)}) custom-call(s32[16,128]{1,0:T(8,128)S(1)} %bitcast.7, s32[16,128]{1,0:T(8,128)S(1)} %bitcast.8), custom_call_target="tpu_custom_call" | custom-call | flops 4000000 | bytes 10000000 | tf_op jit(solution)/shard_map/face_slots/pallas_call | solution.py:246
  26.7 2.4 %collective-permute-done.7.other_ref = f32[5,16,128]{2,1,0:T(8,128)S(1)} collective-permute-done((f32[5,16,128]{2,1,0:T(8,128)S(1)}, f32[5,16,128]{2,1,0:T(8,128)S(1)}, u32[]{:S(2)}, u32[]{:S(2)}) %collective-permute-start.7) | collective-permute-done | bytes 40992 | tf_op jit(solution)/shard_map/ppermute | solution.py:523
  29.1 0.0 copy-done.5
  29.1 0.0 copy-done.6
  29.1 5.5 %backward_and_faces.1 = (f32[32,5,16,128]{3,2,1,0:T(8,128)}, f32[32,8,128]{2,1,0:T(8,128)S(1)}) custom-call(s32[1]{0:T(128)S(6)} %copy.13.count_ref, f32[32,5,16,128]{3,2,1,0:T(8,128)S(1)} %get-tuple-element.36.field_ref, f32[5,16,128]{2,1,0:T(8,128)S(1)} %get-tuple-element.41.near_ref, f32[5,5,16,128]{3,2,1,0:T(8,128)S(1)} %get-tuple-element.42.reach_ref, ...), custom_call_target="tpu_custom_call" | custom-call | tf_op jit(solution)/shard_map/backward_and_faces/pallas_call | solution.py:367
  34.6 15.9 %all_to_all.5.got_ref = f32[32,8,128]{2,1,0:T(8,128)S(1)} all-to-all(f32[32,8,128]{2,1,0:T(8,128)S(1)} %get-tuple-element.47), channel_id=1, replica_groups=mesh['sweep'=4,'bulk'=8] {'sweep','bulk'}, dimensions={0} | all-to-all | bytes 262144 | tf_op jit(solution)/shard_map/all_to_all | solution.py:557
  50.6 3.5 %node_sums.1 = f32[128,128]{1,0:T(8,128)} custom-call(f32[32,8,128]{2,1,0:T(8,128)S(1)} %all_to_all.5.got_ref), custom_call_target="tpu_custom_call" | custom-call | tf_op jit(solution)/shard_map/node_sums/pallas_call | solution.py:424
  (1 shorter events, 0.0 us)
Async XLA Ops:
  0.6 7.7 %copy-start.3 = (f32[32,5,16,128]{3,2,1,0:T(8,128)S(1)}, f32[32,5,16,128]{3,2,1,0:T(8,128)}, u32[]{:S(2)}) copy-start(f32[32,5,16,128]{3,2,1,0:T(8,128)} %psi_ref.1) | copy-start | bytes 3932164
  0.6 7.7 %copy-start.2 = (f32[32,5,16,128]{3,2,1,0:T(8,128)S(1)}, f32[32,5,16,128]{3,2,1,0:T(8,128)}, u32[]{:S(2)}) copy-start(f32[32,5,16,128]{3,2,1,0:T(8,128)} %source_ref.1) | copy-start | bytes 3932164
  0.7 7.7 %copy-start.4 = (f32[32,2,16,128]{3,2,1,0:T(8,128)S(1)}, f32[32,2,16,128]{3,2,1,0:T(8,128)}, u32[]{:S(2)}) copy-start(f32[32,2,16,128]{3,2,1,0:T(8,128)} %lateral_ref.1) | copy-start | bytes 1572868
  0.7 7.7 %copy-start.1 = (f32[32,5,5,16,128]{4,3,2,1,0:T(8,128)S(1)}, f32[32,5,5,16,128]{4,3,2,1,0:T(8,128)}, u32[]{:S(2)}) copy-start(f32[32,5,5,16,128]{4,3,2,1,0:T(8,128)} %coupled_ref.1) | copy-start | bytes 19660804
  0.7 7.7 %copy-start = (f32[32,5,5,16,128]{4,3,2,1,0:T(8,128)S(1)}, f32[32,5,5,16,128]{4,3,2,1,0:T(8,128)}, u32[]{:S(2)}) copy-start(f32[32,5,5,16,128]{4,3,2,1,0:T(8,128)} %inv_ref.3) | copy-start | bytes 19660804
  1.8 6.5 %collective-permute-start = (f32[32,5,128]{2,1,0:T(8,128)S(1)}, f32[32,5,128]{2,1,0:T(8,128)S(1)}, u32[]{:S(2)}, u32[]{:S(2)}) collective-permute-start(f32[32,5,128]{2,1,0:T(8,128)S(1)} %get-tuple-element.25), channel_id=1, source_target_pairs={{0,1},{1,0},{2,3},{3,2},{4,5},{5,4},{6,7},{7,6},{8,9},{9,8},{10,11... | collective-permute-start | bytes 245768 | tf_op jit(solution)/shard_map/ppermute | solution.py:541
  4.9 12.7 %slice-start = ((s8[6553600]{0:T(1024)(128)(4,1)}), s8[4194304]{0:T(1024)(128)(4,1)S(1)}, s32[]{:S(2)}) async-start(s8[6553600]{0:T(1024)(128)(4,1)} %bitcast.4), calls=%async_computation.1 | async-start | bytes 8388608
  4.9 12.7 %slice-start.1 = ((s8[6553600]{0:T(1024)(128)(4,1)}), s8[2359296]{0:T(1024)(128)(4,1)S(1)}, s32[]{:S(2)}) async-start(s8[6553600]{0:T(1024)(128)(4,1)} %bitcast.4), calls=%async_computation.2 | async-start | bytes 4718592
  4.9 3.5 %collective-permute-start.1 = (f32[32,5,128]{2,1,0:T(8,128)S(1)}, f32[32,5,128]{2,1,0:T(8,128)S(1)}, u32[]{:S(2)}, u32[]{:S(2)}) collective-permute-start(f32[32,5,128]{2,1,0:T(8,128)S(1)} %get-tuple-element.26), channel_id=1, source_target_pairs={{1,2},{2,1},{3,4},{4,3},{5,6},{6,5},{9,10},{10,9},{11,12},{12,11},... | collective-permute-start | bytes 245768 | tf_op jit(solution)/shard_map/ppermute | solution.py:542
  14.2 1.6 %collective-permute-start.3 = (f32[5,5,16,128]{3,2,1,0:T(8,128)S(1)}, f32[5,5,16,128]{3,2,1,0:T(8,128)S(1)}, u32[]{:S(2)}, u32[]{:S(2)}) collective-permute-start(f32[5,5,16,128]{3,2,1,0:T(8,128)S(1)} %get-tuple-element.29.refs_1_), channel_id=1, source_target_pairs={{0,8},{8,0},{16,24},{24,16},{1,9},{9,1},{17,25},{25,17},{2,10},{10... | collective-permute-start | bytes 614408 | tf_op jit(solution)/shard_map/ppermute | solution.py:526
  14.2 1.5 %collective-permute-start.2 = (f32[5,16,128]{2,1,0:T(8,128)S(1)}, f32[5,16,128]{2,1,0:T(8,128)S(1)}, u32[]{:S(2)}, u32[]{:S(2)}) collective-permute-start(f32[5,16,128]{2,1,0:T(8,128)S(1)} %get-tuple-element.28.refs_0_), channel_id=1, source_target_pairs={{0,8},{8,0},{16,24},{24,16},{1,9},{9,1},{17,25},{25,17},{2,10},{10... | collective-permute-start | bytes 122888 | tf_op jit(solution)/shard_map/ppermute | solution.py:523
  15.8 6.1 %collective-permute-start.4 = (f32[5,16,128]{2,1,0:T(8,128)S(1)}, f32[5,16,128]{2,1,0:T(8,128)S(1)}, u32[]{:S(2)}, u32[]{:S(2)}) collective-permute-start(f32[5,16,128]{2,1,0:T(8,128)S(1)} %get-tuple-element.32), channel_id=1, source_target_pairs={{0,16},{8,24},{16,0},{24,8},{1,17},{9,25},{17,1},{25,9},{2,18},{10... | collective-permute-start | bytes 122888 | tf_op jit(solution)/shard_map/ppermute | solution.py:523
  21.9 4.1 %copy-start.7 = (s32[2048,1]{0,1:T(1,128)S(1)}, s32[2048,1]{0,1:T(1,128)}, u32[]{:S(2)}) copy-start(s32[2048,1]{0,1:T(1,128)} %param.19) | copy-start | bytes 24580
  22.0 4.1 %copy-start.8 = (s32[2048]{0:T(1024)S(1)}, s32[2048]{0:T(1024)}, u32[]{:S(2)}) copy-start(s32[2048]{0:T(1024)} %param.20) | copy-start | bytes 24580
  22.0 7.1 %copy-start.5 = (f32[5,2048]{1,0:T(8,128)S(1)}, f32[5,2048]{1,0:T(8,128)}, u32[]{:S(2)}) copy-start(f32[5,2048]{1,0:T(8,128)} %weight_ref.1) | copy-start | bytes 122884
  22.0 7.1 %copy-start.6 = (s32[2048]{0:T(1024)S(1)}, s32[2048]{0:T(1024)}, u32[]{:S(2)}) copy-start(s32[2048]{0:T(1024)} %param.18) | copy-start | bytes 24580
  23.4 1.6 %collective-permute-start.6 = (f32[5,5,16,128]{3,2,1,0:T(8,128)S(1)}, f32[5,5,16,128]{3,2,1,0:T(8,128)S(1)}, u32[]{:S(2)}, u32[]{:S(2)}) collective-permute-start(f32[5,5,16,128]{3,2,1,0:T(8,128)S(1)} %get-tuple-element.40.refs_1_), channel_id=1, source_target_pairs={{0,8},{8,0},{16,24},{24,16},{1,9},{9,1},{17,25},{25,17},{2,10},{10... | collective-permute-start | bytes 614408 | tf_op jit(solution)/shard_map/ppermute | solution.py:526
  23.5 1.5 %collective-permute-start.5 = (f32[5,16,128]{2,1,0:T(8,128)S(1)}, f32[5,16,128]{2,1,0:T(8,128)S(1)}, u32[]{:S(2)}, u32[]{:S(2)}) collective-permute-start(f32[5,16,128]{2,1,0:T(8,128)S(1)} %get-tuple-element.39.refs_0_), channel_id=1, source_target_pairs={{0,8},{8,0},{16,24},{24,16},{1,9},{9,1},{17,25},{25,17},{2,10},{10... | collective-permute-start | bytes 122888 | tf_op jit(solution)/shard_map/ppermute | solution.py:523
  25.0 4.1 %collective-permute-start.7 = (f32[5,16,128]{2,1,0:T(8,128)S(1)}, f32[5,16,128]{2,1,0:T(8,128)S(1)}, u32[]{:S(2)}, u32[]{:S(2)}) collective-permute-start(f32[5,16,128]{2,1,0:T(8,128)S(1)} %get-tuple-element.43), channel_id=1, source_target_pairs={{0,16},{8,24},{16,0},{24,8},{1,17},{9,25},{17,1},{25,9},{2,18},{10... | collective-permute-start | bytes 122888 | tf_op jit(solution)/shard_map/ppermute | solution.py:523

commit v4 on v3

--- a/solution.py
+++ b/solution.py
@@ -40,7 +40,7 @@
 def ratio_of(coupled, inv, at, rows):
     j = block(coupled, at, rows)
     d = block(inv, at, rows)
-    return [[dot5(d[c], [j[e][x] for e in range(5)]) for x in range(5)] for c in range(5)], d
+    return [[dot5(d[c], [j[e][x] for e in range(5)]) for x in range(5)] for c in range(5)]
 
 
 def next_total(ratio, total_ref, rows):
@@ -64,65 +64,63 @@
 
 def edge_rows(psi):
     planes, fields, width, _ = psi.shape
-    shape = (planes, fields, LANES)
+    shape = (fields * planes, LANES)
 
     def kernel(psi_hbm, low_ref, high_ref, head_ref, tail_ref, sems):
-        copies = [
-            pltpu.make_async_copy(psi_hbm.at[:, :, 0, :], head_ref, sems.at[0]),
-            pltpu.make_async_copy(psi_hbm.at[:, :, width - 1, :], tail_ref, sems.at[1]),
-        ]
+        copies = []
+        for c in range(fields):
+            rows = pl.ds(c * planes, planes)
+            copies.append(pltpu.make_async_copy(psi_hbm.at[:, c, 0, :], head_ref.at[rows], sems.at[0, c]))
+            copies.append(pltpu.make_async_copy(psi_hbm.at[:, c, width - 1, :], tail_ref.at[rows], sems.at[1, c]))
         for copy in copies:
             copy.start()
         is_odd = lax.rem(lax.axis_index("bulk"), 2) == 1
         for copy in copies:
             copy.wait()
-        for i in range(planes):
-            head, tail = head_ref[i], tail_ref[i]
-            low_ref[i] = jnp.where(is_odd, head, tail)
-            high_ref[i] = jnp.where(is_odd, tail, head)
+        head, tail = head_ref[...], tail_ref[...]
+        low_ref[...] = jnp.where(is_odd, head, tail)
+        high_ref[...] = jnp.where(is_odd, tail, head)
 
     return pl.pallas_call(
         kernel,
         out_shape=(jax.ShapeDtypeStruct(shape, F32), jax.ShapeDtypeStruct(shape, F32)),
         in_specs=[pl.BlockSpec(memory_space=pltpu.HBM)],
         out_specs=tuple(vmem_specs(2)),
-        scratch_shapes=[VMEM(shape, F32), VMEM(shape, F32), pltpu.SemaphoreType.DMA((2,))],
+        scratch_shapes=[VMEM(shape, F32), VMEM(shape, F32), pltpu.SemaphoreType.DMA((2, fields))],
         compiler_params=pltpu.CompilerParams(vmem_limit_bytes=4 << 20),
         cost_estimate=pl.CostEstimate(flops=10_000_000_000, bytes_accessed=20_000_000, transcendentals=0),
         name="edge_rows",
     )(in_hbm(psi))
 
 
-def forward_local(source, psi, lateral, first, second, coupled, inv):
+def forward_local(source, psi, lateral, first, second, ratio, inv):
     planes, width = source.shape[0], source.shape[2]
 
-    def kernel(source_ref, psi_ref, lateral_ref, first_ref, second_ref, coupled_ref, inv_ref,
-               ratio_ref, total_ref, scaled_ref, leaving_ref):
+    def kernel(source_ref, psi_ref, lateral_ref, first_ref, second_ref, ratio_ref, inv_ref,
+               scaled_ref, leaving_ref):
         is_odd = lax.rem(lax.axis_index("bulk"), 2) == 1
-        set_identity(total_ref, planes)
 
         def body(i, state):
-            one, two = first_ref[i], second_ref[i]
-            low = jnp.where(is_odd, one, two)
-            high = jnp.where(is_odd, two, one)
             below, above = lateral_ref[i, 0], lateral_ref[i, 1]
             right = []
             for c in range(5):
+                one = first_ref[pl.ds(c * planes + i, 1), :]
+                two = second_ref[pl.ds(c * planes + i, 1), :]
                 here = psi_ref[i, c]
-                down = jnp.concatenate([low[c:c + 1], here[:width - 1]], axis=0)
-                up = jnp.concatenate([here[1:], high[c:c + 1]], axis=0)
+                down = jnp.concatenate([jnp.where(is_odd, one, two), here[:width - 1]], axis=0)
+                up = jnp.concatenate([here[1:], jnp.where(is_odd, two, one)], axis=0)
                 right.append(source_ref[i, c] - below * down - above * up)
             out = []
             for h, rows in enumerate(halves(width)):
                 r = [v[8 * h:8 * h + 8] for v in right]
-                ratio, d = ratio_of(coupled_ref, inv_ref, i, rows)
-                scaled = [dot5(d[c], r) for c in range(5)]
-                out.append([scaled[c] - dot5(ratio[c], state[h]) for c in range(5)])
-                total = next_total(ratio, total_ref, rows)
-                keep_matrices(ratio, total, ratio_ref, total_ref, i, rows)
+                d = block(inv_ref, i, rows)
+                e = block(ratio_ref, i, rows)
+                g = [dot5(d[c], r) for c in range(5)]
+                out.append((g, [g[c] - dot5(e[c], state[h]) for c in range(5)]))
+            for h, rows in enumerate(halves(width)):
                 for c in range(5):
-                    scaled_ref[i, c, rows, :] = scaled[c]
-            return out
+                    scaled_ref[i, c, rows, :] = out[h][0][c]
+            return [f for _, f in out]
 
         zero = [[jnp.zeros((8, LANES), F32)] * 5 for _ in halves(width)]
         state = lax.fori_loop(0, planes, body, zero)
@@ -132,33 +130,28 @@
 
     return pl.pallas_call(
         kernel,
-        out_shape=(
-            VMEM(coupled.shape, F32),
-            jax.ShapeDtypeStruct(coupled.shape[1:], F32),
-            VMEM(source.shape, F32),
-            jax.ShapeDtypeStruct(source.shape[1:], F32),
-        ),
+        out_shape=(VMEM(source.shape, F32), jax.ShapeDtypeStruct(source.shape[1:], F32)),
         in_specs=vmem_specs(7),
-        out_specs=tuple(vmem_specs(4)),
+        out_specs=tuple(vmem_specs(2)),
         compiler_params=pltpu.CompilerParams(vmem_limit_bytes=4 << 20),
         name="forward_local",
-    )(*[in_vmem(v) for v in (source, psi, lateral, first, second, coupled, inv)])
-
-
-def backward_matrices(coupled, inv):
+    )(*[in_vmem(v) for v in (source, psi, lateral, first, second, ratio, inv)])
+
+
+def matrices(coupled, inv, backward, name):
     planes, width = coupled.shape[0], coupled.shape[3]
 
     def kernel(coupled_ref, inv_ref, ratio_ref, total_ref):
         set_identity(total_ref, planes)
 
         def body(t, carry):
-            at = planes - 1 - t
+            at = planes - 1 - t if backward else t
             for rows in halves(width):
-                ratio, _ = ratio_of(coupled_ref, inv_ref, at, rows)
+                ratio = ratio_of(coupled_ref, inv_ref, at, rows)
                 keep_matrices(ratio, next_total(ratio, total_ref, rows), ratio_ref, total_ref, at, rows)
             return carry
 
-        lax.fori_loop(0, planes, body, 0)
+        lax.fori_loop(0, planes, body, 0, unroll=2)
 
     return pl.pallas_call(
         kernel,
@@ -166,8 +159,8 @@
         in_specs=vmem_specs(2),
         out_specs=tuple(vmem_specs(2)),
         compiler_params=pltpu.CompilerParams(vmem_limit_bytes=4 << 20),
-        cost_estimate=pl.CostEstimate(flops=4_000_000, bytes_accessed=20_000_000, transcendentals=0),
-        name="backward_matrices",
+        cost_estimate=pl.CostEstimate(flops=5_000_000_000, bytes_accessed=20_000_000, transcendentals=0),
+        name=name,
     )(in_vmem(coupled), in_vmem(inv))
 
 
@@ -538,13 +531,16 @@
     low_pairs = [(i, i ^ 1) for i in range(bulk) if i ^ 1 < bulk]
     high_pairs = [(i, j) for i in range(bulk) for j in [i + 1 if i % 2 else i - 1] if 0 <= j < bulk]
     low_edge, high_edge = edge_rows(psi_old)
+    low_edge, high_edge, lower_jac = lax.optimization_barrier((low_edge, high_edge, lower_jac))
     first = lax.ppermute(low_edge, "bulk", low_pairs)
     second = lax.ppermute(high_edge, "bulk", high_pairs)
 
-    ratio, total, scaled, leaving = forward_local(source, psi_old, lateral, first, second, lower_jac, diag_inv)
+    ratio, total = matrices(lower_jac, diag_inv, False, "forward_matrices")
+    scaled, leaving = forward_local(source, psi_old, lateral, first, second, ratio, diag_inv)
+    total, leaving = lax.optimization_barrier((total, leaving))
     arriving, joined = relay(total, leaving, False)
     upper_jac, joined = lax.optimization_barrier((upper_jac, joined))
-    back_ratio, back_total = backward_matrices(upper_jac, diag_inv)
+    back_ratio, back_total = matrices(upper_jac, diag_inv, True, "backward_matrices")
     field, leaving = forward_then_back(scaled, arriving, ratio, back_ratio)
     back_total, leaving = lax.optimization_barrier((back_total, leaving))
     arriving, _ = relay(back_total, leaving, True)

time: 54.3 us -> 49.3 us (0.908)
  blocking collectives: 15.9 us -> 13 us
  waiting for transfers between devices: 7.13 us -> 4.75 us
  starting transfers between devices: 7.11 us -> 7.89 us
    all_to_all x1, blocking collectives: 15.9 us -> 13 us  [per_device(): got = lax.all_to_all(send, ('sweep', 'bulk'), 0, 0, tiled=True)]
    ppermute x1, waiting for transfers between devices: 2.7 us -> 0.01 us  [per_device(): first = lax.ppermute(low_edge, 'bulk', low_pairs)]
    pallas_call x2 -> x3, Pallas kernels: 10.1 us -> 9.63 us  [the longest x2 8.03 us: matrices(): pl.pallas_call(kernel, out_shape=(VMEM(coupled.shape, F32), jax.ShapeDtyp...]
  transfers between devices with their start and end apart: 8 -> 8, of which waited for: 4 -> 3; matrix products, arithmetic and copies ran while one was open for 0% -> 0% of each run, Pallas kernels for 9% -> 18%
where the time goes in v4:
time: 49.3 us; the launch traced here: 49.2 us
  Pallas kernels  21.9 us (44%)
  blocking collectives  13 us (26%)
  starting transfers between devices  7.89 us (16%)
  waiting for transfers between devices  4.75 us (10%)
  between operations  1.52 us (3%)
    all_to_all x1, blocking collectives, per_device(): got = lax.all_to_all(send, ('sweep', 'bulk'), 0, 0, tiled=True)  13 us
    pallas_call x2, Pallas kernels, matrices(): pl.pallas_call(kernel, out_shape=(VMEM(coupled.shape, F32), jax.ShapeDtyp...  8.03 us
    pallas_call x1, Pallas kernels, backward_and_faces(): pl.pallas_call(kernel, out_shape=(jax.ShapeDtypeStruct(field.shape, F32),...  5.53 us
    ppermute x4, waiting for transfers between devices, relay(): other = lax.ppermute(leaving, 'sweep', pairs)  4.74 us
    ppermute x4, starting transfers between devices, relay(): other = lax.ppermute(leaving, 'sweep', pairs)  3.62 us
    pallas_call x1, Pallas kernels, node_sums(): pl.pallas_call(kernel, out_shape=jax.ShapeDtypeStruct((side, LANES), F32)...  3.56 us
    ppermute x1, starting transfers between devices, per_device(): first = lax.ppermute(low_edge, 'bulk', low_pairs)  3.03 us
    pallas_call x1, Pallas kernels, forward_local(): pl.pallas_call(kernel, out_shape=(VMEM(source.shape, F32), jax.ShapeDtype...  1.6 us
  transfers between devices with their start and end apart: 8, of which 3 were waited for; matrix products, arithmetic and copies ran while one was open for 0% of the time, Pallas kernels for 18%

profile of v4, /device:TPU:0, one launch (start us, length us, event | category | flops | bytes accessed | tf_op | source)
XLA Modules:
  0.0 49.2 jit_solution(14165136107703848657)
XLA Ops:
  0.6 0.0 copy-start.8
  0.6 0.0 copy-start
  0.6 1.1 %edge_rows.1 = (f32[160,128]{1,0:T(8,128)S(1)}, f32[160,128]{1,0:T(8,128)S(1)}) custom-call(f32[32,5,16,128]{3,2,1,0:T(8,128)} %psi_ref.1), custom_call_target="tpu_custom_call" | custom-call | flops 10000000000 | bytes 20000000 | tf_op jit(solution)/shard_map/edge_rows/pallas_call | solution.py:84
  1.7 0.0 copy-start.1
  1.8 0.0 copy-start.2
  1.8 0.0 copy-start.3
  1.8 3.0 %collective-permute-start = (f32[160,128]{1,0:T(8,128)S(1)}, f32[160,128]{1,0:T(8,128)S(1)}, u32[]{:S(2)}, u32[]{:S(2)}) collective-permute-start(f32[160,128]{1,0:T(8,128)S(1)} %get-tuple-element.32), channel_id=1, source_target_pairs={{0,1},{1,0},{2,3},{3,2},{4,5},{5,4},{6,7},{7,6},{8,9},{9,8},{10,11... | collective-permute-start | bytes 245768 | tf_op jit(solution)/shard_map/ppermute | solution.py:535
  4.8 0.8 %collective-permute-start.1 = (f32[160,128]{1,0:T(8,128)S(1)}, f32[160,128]{1,0:T(8,128)S(1)}, u32[]{:S(2)}, u32[]{:S(2)}) collective-permute-start(f32[160,128]{1,0:T(8,128)S(1)} %get-tuple-element.33), channel_id=1, source_target_pairs={{1,2},{2,1},{3,4},{4,3},{5,6},{6,5},{9,10},{10,9},{11,12},{12,11},... | collective-permute-start | bytes 245768 | tf_op jit(solution)/shard_map/ppermute | solution.py:536
  5.6 0.0 copy-done.8
  5.6 0.0 copy-done
  5.6 4.1 %forward_matrices.1 = (f32[32,5,5,16,128]{4,3,2,1,0:T(8,128)S(1)}, f32[5,5,16,128]{3,2,1,0:T(8,128)S(1)}) custom-call(f32[32,5,5,16,128]{4,3,2,1,0:T(8,128)S(1)} %copy-done.8, f32[32,5,5,16,128]{4,3,2,1,0:T(8,128)S(1)} %copy-done), custom_call_target="tpu_custom_call" | custom-call | flops 5000000000 | bytes 20000000 | tf_op jit(solution)/shard_map/forward_matrices/pallas_call | solution.py:156
  9.7 0.0 collective-permute-done.first_ref
  9.7 0.0 collective-permute-done.1.second_ref
  9.7 0.0 copy-done.1
  9.7 0.0 copy-done.2
  9.7 0.0 copy-done.3
  9.8 0.0 copy-start.9
  9.8 1.6 %forward_local.1 = (f32[32,5,16,128]{3,2,1,0:T(8,128)S(1)}, f32[5,16,128]{2,1,0:T(8,128)S(1)}) custom-call(f32[32,5,16,128]{3,2,1,0:T(8,128)S(1)} %copy-done.1, f32[32,5,16,128]{3,2,1,0:T(8,128)S(1)} %copy-done.2, f32[32,2,16,128]{3,2,1,0:T(8,128)S(1)} %copy-done.3, f32[160,128]{1,0:T(8,128)S(1)} %collective-permute-done.first_ref, ...), custom_call_target="tpu_custom_call" | custom-call | tf_op jit(solution)/shard_map/forward_local/pallas_call | solution.py:131
  11.4 0.4 collective-permute-start.3
  11.8 0.2 collective-permute-start.2
  12.0 1.0 %collective-permute-done.2.refs_2_ = f32[5,16,128]{2,1,0:T(8,128)S(1)} collective-permute-done((f32[5,16,128]{2,1,0:T(8,128)S(1)}, f32[5,16,128]{2,1,0:T(8,128)S(1)}, u32[]{:S(2)}, u32[]{:S(2)}) %collective-permute-start.2) | collective-permute-done | bytes 40992 | tf_op jit(solution)/shard_map/ppermute | solution.py:516
  13.0 0.0 collective-permute-done.3.refs_3_
  13.0 0.1 join.2
  13.0 2.8 %collective-permute-start.4 = (f32[5,16,128]{2,1,0:T(8,128)S(1)}, f32[5,16,128]{2,1,0:T(8,128)S(1)}, u32[]{:S(2)}, u32[]{:S(2)}) collective-permute-start(f32[5,16,128]{2,1,0:T(8,128)S(1)} %get-tuple-element.43), channel_id=1, source_target_pairs={{0,16},{8,24},{16,0},{24,8},{1,17},{9,25},{17,1},{25,9},{2,18},{10... | collective-permute-start | bytes 122888 | tf_op jit(solution)/shard_map/ppermute | solution.py:516
  15.9 0.0 copy-done.9
  15.9 4.0 %backward_matrices.1 = (f32[32,5,5,16,128]{4,3,2,1,0:T(8,128)S(1)}, f32[5,5,16,128]{3,2,1,0:T(8,128)S(1)}) custom-call(f32[32,5,5,16,128]{4,3,2,1,0:T(8,128)S(1)} %copy-done.9, f32[32,5,5,16,128]{4,3,2,1,0:T(8,128)S(1)} %copy-done), custom_call_target="tpu_custom_call" | custom-call | flops 5000000000 | bytes 20000000 | tf_op jit(solution)/shard_map/backward_matrices/pallas_call | solution.py:156
  19.9 0.0 collective-permute-done.4.other_ref
  19.9 0.0 copy-start.6
  19.9 0.0 copy-start.7
  19.9 0.0 copy-start.4
  19.9 0.0 copy-start.5
  19.9 1.4 %forward_then_back.1 = (f32[32,5,16,128]{3,2,1,0:T(8,128)S(1)}, f32[5,16,128]{2,1,0:T(8,128)S(1)}) custom-call(f32[32,5,16,128]{3,2,1,0:T(8,128)S(1)} %get-tuple-element.36.scaled_ref, f32[5,16,128]{2,1,0:T(8,128)S(1)} %get-tuple-element.41.near_ref, f32[5,5,16,128]{3,2,1,0:T(8,128)S(1)} %get-tuple-element.42.reach_ref, ...), custom_call_target="tpu_custom_call" | custom-call | tf_op jit(solution)/shard_map/forward_then_back/pallas_call | solution.py:198
  21.3 0.1 collective-permute-start.6
  21.4 0.5 %collective-permute-start.5 = (f32[5,16,128]{2,1,0:T(8,128)S(1)}, f32[5,16,128]{2,1,0:T(8,128)S(1)}, u32[]{:S(2)}, u32[]{:S(2)}) collective-permute-start(f32[5,16,128]{2,1,0:T(8,128)S(1)} %get-tuple-element.49.refs_0_), channel_id=1, source_target_pairs={{0,8},{8,0},{16,24},{24,16},{1,9},{9,1},{17,25},{25,17},{2,10},{10... | collective-permute-start | bytes 122888 | tf_op jit(solution)/shard_map/ppermute | solution.py:516
  21.9 1.0 %collective-permute-done.5.refs_2_ = f32[5,16,128]{2,1,0:T(8,128)S(1)} collective-permute-done((f32[5,16,128]{2,1,0:T(8,128)S(1)}, f32[5,16,128]{2,1,0:T(8,128)S(1)}, u32[]{:S(2)}, u32[]{:S(2)}) %collective-permute-start.5) | collective-permute-done | bytes 40992 | tf_op jit(solution)/shard_map/ppermute | solution.py:516
  22.9 0.0 collective-permute-done.6.refs_3_
  22.9 0.1 join.3
  22.9 0.1 collective-permute-start.7
  23.7 0.0 copy-done.6
  23.7 0.0 copy-done.7
  23.7 0.6 %face_slots.1 = (s32[16,128]{1,0:T(8,128)S(1)}, f32[32,128]{1,0:T(8,128)S(1)}) custom-call(s32[16,128]{1,0:T(8,128)S(1)} %bitcast.5, s32[16,128]{1,0:T(8,128)S(1)} %bitcast.6), custom_call_target="tpu_custom_call" | custom-call | flops 4000000 | bytes 10000000 | tf_op jit(solution)/shard_map/face_slots/pallas_call | solution.py:239
  24.3 2.7 %collective-permute-done.7.other_ref = f32[5,16,128]{2,1,0:T(8,128)S(1)} collective-permute-done((f32[5,16,128]{2,1,0:T(8,128)S(1)}, f32[5,16,128]{2,1,0:T(8,128)S(1)}, u32[]{:S(2)}, u32[]{:S(2)}) %collective-permute-start.7) | collective-permute-done | bytes 40992 | tf_op jit(solution)/shard_map/ppermute | solution.py:516
  27.0 0.0 copy-done.4
  27.0 0.0 copy-done.5
  27.0 5.5 %backward_and_faces.1 = (f32[32,5,16,128]{3,2,1,0:T(8,128)}, f32[32,8,128]{2,1,0:T(8,128)S(1)}) custom-call(s32[1]{0:T(128)S(6)} %copy.13.count_ref, f32[32,5,16,128]{3,2,1,0:T(8,128)S(1)} %get-tuple-element.46.field_ref, f32[5,16,128]{2,1,0:T(8,128)S(1)} %get-tuple-element.51.near_ref, f32[5,5,16,128]{3,2,1,0:T(8,128)S(1)} %get-tuple-element.52.reach_ref, ...), custom_call_target="tpu_custom_call" | custom-call | tf_op jit(solution)/shard_map/backward_and_faces/pallas_call | solution.py:360
  32.6 13.0 %all_to_all.5.got_ref = f32[32,8,128]{2,1,0:T(8,128)S(1)} all-to-all(f32[32,8,128]{2,1,0:T(8,128)S(1)} %get-tuple-element.57), channel_id=1, replica_groups=mesh['sweep'=4,'bulk'=8] {'sweep','bulk'}, dimensions={0} | all-to-all | bytes 262144 | tf_op jit(solution)/shard_map/all_to_all | solution.py:553
  45.6 3.6 %node_sums.1 = f32[128,128]{1,0:T(8,128)} custom-call(f32[32,8,128]{2,1,0:T(8,128)S(1)} %all_to_all.5.got_ref), custom_call_target="tpu_custom_call" | custom-call | tf_op jit(solution)/shard_map/node_sums/pallas_call | solution.py:417
Async XLA Ops:
  0.6 5.0 %copy-start.8 = (f32[32,5,5,16,128]{4,3,2,1,0:T(8,128)S(1)}, f32[32,5,5,16,128]{4,3,2,1,0:T(8,128)}, u32[]{:S(2)}) copy-start(f32[32,5,5,16,128]{4,3,2,1,0:T(8,128)} %coupled_ref) | copy-start | bytes 19660804
  0.6 5.0 %copy-start = (f32[32,5,5,16,128]{4,3,2,1,0:T(8,128)S(1)}, f32[32,5,5,16,128]{4,3,2,1,0:T(8,128)}, u32[]{:S(2)}) copy-start(f32[32,5,5,16,128]{4,3,2,1,0:T(8,128)} %inv_ref.5) | copy-start | bytes 19660804
  1.7 8.0 %copy-start.1 = (f32[32,5,16,128]{3,2,1,0:T(8,128)S(1)}, f32[32,5,16,128]{3,2,1,0:T(8,128)}, u32[]{:S(2)}) copy-start(f32[32,5,16,128]{3,2,1,0:T(8,128)} %source_ref.1) | copy-start | bytes 3932164
  1.8 8.0 %copy-start.2 = (f32[32,5,16,128]{3,2,1,0:T(8,128)S(1)}, f32[32,5,16,128]{3,2,1,0:T(8,128)}, u32[]{:S(2)}) copy-start(f32[32,5,16,128]{3,2,1,0:T(8,128)} %psi_ref.1) | copy-start | bytes 3932164
  1.8 8.0 %copy-start.3 = (f32[32,2,16,128]{3,2,1,0:T(8,128)S(1)}, f32[32,2,16,128]{3,2,1,0:T(8,128)}, u32[]{:S(2)}) copy-start(f32[32,2,16,128]{3,2,1,0:T(8,128)} %lateral_ref.1) | copy-start | bytes 1572868
  1.8 7.9 %collective-permute-start = (f32[160,128]{1,0:T(8,128)S(1)}, f32[160,128]{1,0:T(8,128)S(1)}, u32[]{:S(2)}, u32[]{:S(2)}) collective-permute-start(f32[160,128]{1,0:T(8,128)S(1)} %get-tuple-element.32), channel_id=1, source_target_pairs={{0,1},{1,0},{2,3},{3,2},{4,5},{5,4},{6,7},{7,6},{8,9},{9,8},{10,11... | collective-permute-start | bytes 245768 | tf_op jit(solution)/shard_map/ppermute | solution.py:535
  4.8 4.9 %collective-permute-start.1 = (f32[160,128]{1,0:T(8,128)S(1)}, f32[160,128]{1,0:T(8,128)S(1)}, u32[]{:S(2)}, u32[]{:S(2)}) collective-permute-start(f32[160,128]{1,0:T(8,128)S(1)} %get-tuple-element.33), channel_id=1, source_target_pairs={{1,2},{2,1},{3,4},{4,3},{5,6},{6,5},{9,10},{10,9},{11,12},{12,11},... | collective-permute-start | bytes 245768 | tf_op jit(solution)/shard_map/ppermute | solution.py:536
  9.8 6.1 %copy-start.9 = (f32[32,5,5,16,128]{4,3,2,1,0:T(8,128)S(1)}, f32[32,5,5,16,128]{4,3,2,1,0:T(8,128)}, u32[]{:S(2)}) copy-start(f32[32,5,5,16,128]{4,3,2,1,0:T(8,128)} %coupled_ref.1) | copy-start | bytes 19660804
  11.4 1.6 %collective-permute-start.3 = (f32[5,5,16,128]{3,2,1,0:T(8,128)S(1)}, f32[5,5,16,128]{3,2,1,0:T(8,128)S(1)}, u32[]{:S(2)}, u32[]{:S(2)}) collective-permute-start(f32[5,5,16,128]{3,2,1,0:T(8,128)S(1)} %get-tuple-element.40.refs_1_), channel_id=1, source_target_pairs={{0,8},{8,0},{16,24},{24,16},{1,9},{9,1},{17,25},{25,17},{2,10},{10... | collective-permute-start | bytes 614408 | tf_op jit(solution)/shard_map/ppermute | solution.py:519
  11.8 1.2 %collective-permute-start.2 = (f32[5,16,128]{2,1,0:T(8,128)S(1)}, f32[5,16,128]{2,1,0:T(8,128)S(1)}, u32[]{:S(2)}, u32[]{:S(2)}) collective-permute-start(f32[5,16,128]{2,1,0:T(8,128)S(1)} %get-tuple-element.39.refs_0_), channel_id=1, source_target_pairs={{0,8},{8,0},{16,24},{24,16},{1,9},{9,1},{17,25},{25,17},{2,10},{10... | collective-permute-start | bytes 122888 | tf_op jit(solution)/shard_map/ppermute | solution.py:516
  13.0 6.8 %collective-permute-start.4 = (f32[5,16,128]{2,1,0:T(8,128)S(1)}, f32[5,16,128]{2,1,0:T(8,128)S(1)}, u32[]{:S(2)}, u32[]{:S(2)}) collective-permute-start(f32[5,16,128]{2,1,0:T(8,128)S(1)} %get-tuple-element.43), channel_id=1, source_target_pairs={{0,16},{8,24},{16,0},{24,8},{1,17},{9,25},{17,1},{25,9},{2,18},{10... | collective-permute-start | bytes 122888 | tf_op jit(solution)/shard_map/ppermute | solution.py:516
  19.9 3.8 %copy-start.6 = (s32[2048,1]{0,1:T(1,128)S(1)}, s32[2048,1]{0,1:T(1,128)}, u32[]{:S(2)}) copy-start(s32[2048,1]{0,1:T(1,128)} %param.19) | copy-start | bytes 24580
  19.9 3.8 %copy-start.7 = (s32[2048]{0:T(1024)S(1)}, s32[2048]{0:T(1024)}, u32[]{:S(2)}) copy-start(s32[2048]{0:T(1024)} %param.20) | copy-start | bytes 24580
  19.9 7.1 %copy-start.4 = (f32[5,2048]{1,0:T(8,128)S(1)}, f32[5,2048]{1,0:T(8,128)}, u32[]{:S(2)}) copy-start(f32[5,2048]{1,0:T(8,128)} %weight_ref.1) | copy-start | bytes 122884
  19.9 7.1 %copy-start.5 = (s32[2048]{0:T(1024)S(1)}, s32[2048]{0:T(1024)}, u32[]{:S(2)}) copy-start(s32[2048]{0:T(1024)} %param.18) | copy-start | bytes 24580
  21.3 1.6 %collective-permute-start.6 = (f32[5,5,16,128]{3,2,1,0:T(8,128)S(1)}, f32[5,5,16,128]{3,2,1,0:T(8,128)S(1)}, u32[]{:S(2)}, u32[]{:S(2)}) collective-permute-start(f32[5,5,16,128]{3,2,1,0:T(8,128)S(1)} %get-tuple-element.50.refs_1_), channel_id=1, source_target_pairs={{0,8},{8,0},{16,24},{24,16},{1,9},{9,1},{17,25},{25,17},{2,10},{10... | collective-permute-start | bytes 614408 | tf_op jit(solution)/shard_map/ppermute | solution.py:519
  21.4 1.5 %collective-permute-start.5 = (f32[5,16,128]{2,1,0:T(8,128)S(1)}, f32[5,16,128]{2,1,0:T(8,128)S(1)}, u32[]{:S(2)}, u32[]{:S(2)}) collective-permute-start(f32[5,16,128]{2,1,0:T(8,128)S(1)} %get-tuple-element.49.refs_0_), channel_id=1, source_target_pairs={{0,8},{8,0},{16,24},{24,16},{1,9},{9,1},{17,25},{25,17},{2,10},{10... | collective-permute-start | bytes 122888 | tf_op jit(solution)/shard_map/ppermute | solution.py:516
  22.9 4.1 %collective-permute-start.7 = (f32[5,16,128]{2,1,0:T(8,128)S(1)}, f32[5,16,128]{2,1,0:T(8,128)S(1)}, u32[]{:S(2)}, u32[]{:S(2)}) collective-permute-start(f32[5,16,128]{2,1,0:T(8,128)S(1)} %get-tuple-element.53), channel_id=1, source_target_pairs={{0,16},{8,24},{16,0},{24,8},{1,17},{9,25},{17,1},{25,9},{2,18},{10... | collective-permute-start | bytes 122888 | tf_op jit(solution)/shard_map/ppermute | solution.py:516

commit v5 on v4

--- a/solution.py
+++ b/solution.py
@@ -123,7 +123,7 @@
             return [f for _, f in out]
 
         zero = [[jnp.zeros((8, LANES), F32)] * 5 for _ in halves(width)]
-        state = lax.fori_loop(0, planes, body, zero)
+        state = lax.fori_loop(0, planes, body, zero, unroll=2)
         for h, rows in enumerate(halves(width)):
             for c in range(5):
                 leaving_ref[c, rows, :] = state[h][c]
@@ -179,7 +179,7 @@
             return out
 
         start = last_join(near_ref, reach_ref, other_ref, False, width)
-        lax.fori_loop(0, planes, ahead, start)
+        lax.fori_loop(0, planes, ahead, start, unroll=4)
 
         def back(t, state):
             i = planes - 1 - t
@@ -190,7 +190,7 @@
             return out
 
         zero = [[jnp.zeros((8, LANES), F32)] * 5 for _ in halves(width)]
-        state = lax.fori_loop(0, planes, back, zero)
+        state = lax.fori_loop(0, planes, back, zero, unroll=4)
         for h, rows in enumerate(halves(width)):
             for c in range(5):
                 leaving_ref[c, rows, :] = state[h][c]
@@ -247,6 +247,11 @@
     )(in_vmem(owner), in_vmem(node))
 
 
+def spread(row, rows):
+    tile = jnp.broadcast_to(row, (16, LANES)).astype(BF16)
+    return jnp.concatenate([tile] * (rows // 16), axis=0)
+
+
 def split(value):
     high = value.astype(BF16)
     return high, (value - high.astype(F32)).astype(BF16)
@@ -254,22 +259,20 @@
 
 def place_in_slots(slot, parts, bucket_rows):
     face_rows = slot.shape[0]
-    high = (slot // LANES).astype(F32).astype(BF16)
-    low = (slot % LANES).astype(F32).astype(BF16)
-    parts = [p.astype(BF16) for p in parts]
+    high = (slot // LANES).astype(F32)
+    low = (slot % LANES).astype(F32)
+    parts = [p.astype(F32) for p in parts]
     high_iota = lax.broadcasted_iota(jnp.int32, (bucket_rows, LANES), 0).astype(F32).astype(BF16)
     low_iota = lax.broadcasted_iota(jnp.int32, (LANES, LANES), 0).astype(F32).astype(BF16)
+    ones, none = jnp.ones((LANES, LANES), BF16), jnp.zeros((LANES, LANES), BF16)
     zero = jnp.zeros((bucket_rows, LANES), BF16)
     lefts, rights = [], []
     for f in range(face_rows):
-
-        def spread(value, rows):
-            return jnp.broadcast_to(value[f:f + 1], (rows, LANES))
-
-        hot = high_iota == spread(high, bucket_rows)
-        lefts.append(jnp.concatenate([jnp.where(hot, spread(p, bucket_rows), zero) for p in parts], axis=0))
-        rights.append(jnp.where(low_iota == spread(low, LANES), jnp.ones((LANES, LANES), BF16),
-                                jnp.zeros((LANES, LANES), BF16)))
+        row = slice(f, f + 1)
+        hot = high_iota == spread(high[row], bucket_rows)
+        lefts.append(jnp.concatenate(
+            [jnp.where(hot, spread(p[row], bucket_rows), zero) for p in parts], axis=0))
+        rights.append(jnp.where(low_iota == spread(low[row], LANES), ones, none))
     out = lax.dot_general(jnp.concatenate(lefts, axis=1), jnp.concatenate(rights, axis=1),
                           (((1,), (1,)), ((), ())), preferred_element_type=F32)
     return [out[k * bucket_rows:(k + 1) * bucket_rows] for k in range(len(parts))]
@@ -309,7 +312,7 @@
         state = last_join(near_ref, reach_ref, other_ref, True, width)
         for k in reversed(range(planes // batch)):
             first = planes - (k + 1) * batch
-            state = lax.fori_loop(first, first + batch, back, state)
+            state = lax.fori_loop(first, first + batch, back, state, unroll=4)
             write(k).start()
 
         lane_iota = lax.broadcasted_iota(jnp.int32, (LANES, LANES), 0).astype(F32).astype(BF16)
@@ -319,7 +322,7 @@
             cells = [cell_ref[pl.ds(g * group + u, 1), :] for u in range(group)]
             hots, offs = [], []
             for at in cells:
-                lanes = jnp.broadcast_to((at % LANES).astype(F32), (LANES, LANES)).astype(BF16)
+                lanes = spread((at % LANES).astype(F32), LANES)
                 hots.append(jnp.where(lane_iota == lanes, jnp.ones((LANES, LANES), BF16),
                                       jnp.zeros((LANES, LANES), BF16)))
                 offs.append(jnp.broadcast_to(at // LANES, (8, LANES)) - sub8)
@@ -343,7 +346,7 @@
                 value_ref[pl.ds(g * group + u, 1), :] = jnp.sum(dot5(w, found[u]), axis=0, keepdims=True)
             return carry
 
-        lax.fori_loop(0, face_rows // group, gather, 0)
+        lax.fori_loop(0, face_rows // group, gather, 0, unroll=4)
         live = lax.broadcasted_iota(jnp.int32, (face_rows, LANES), 0) * LANES + lax.broadcasted_iota(
             jnp.int32, (face_rows, LANES), 1) < count_ref[0]
         high, low = split(jnp.where(live, value_ref[...], 0.0))
@@ -381,7 +384,7 @@
     devices, rows2, _ = got.shape
     rows_each = rows2 // 2
     side = NODES_DEV // LANES
-    batch = 32 // rows_each
+    batch = min(devices, 128 // rows_each)
 
     def kernel(got_ref, out_ref):
         iota = lax.broadcasted_iota(jnp.int32, (LANES, LANES), 0).astype(F32).astype(BF16)
@@ -393,25 +396,24 @@
             lefts, rights = [], []
             for u in range(batch):
                 d = t * batch + u
-                node = got_ref[d, rows_each:, :].astype(jnp.int32)
-                node_high = (node // LANES).astype(F32).astype(BF16)
-                node_low = (node % LANES).astype(F32).astype(BF16)
-                high, low = split(got_ref[d, :rows_each, :])
                 for r in range(rows_each):
-
-                    def spread(value, rows):
-                        return jnp.broadcast_to(value[r:r + 1], (rows, LANES))
-
-                    hot = side_iota == spread(node_high, side)
+                    value = got_ref[d, r:r + 1, :]
+                    node = got_ref[d, rows_each + r:rows_each + r + 1, :].astype(jnp.int32)
+                    high = value.astype(BF16).astype(F32)
+                    hot = side_iota == spread((node // LANES).astype(F32), side)
                     lefts.append(jnp.concatenate([
                         jnp.where(hot, spread(high, side), side_zero),
-                        jnp.where(hot, spread(low, side), side_zero)], axis=0))
-                    rights.append(jnp.where(iota == spread(node_low, LANES), ones, zero))
+                        jnp.where(hot, spread(value - high, side), side_zero)], axis=0))
+                    rights.append(jnp.where(iota == spread((node % LANES).astype(F32), LANES), ones, zero))
             return total + lax.dot_general(
                 jnp.concatenate(lefts, axis=1), jnp.concatenate(rights, axis=1),
                 (((1,), (1,)), ((), ())), preferred_element_type=F32)
 
-        total = lax.fori_loop(0, devices // batch, body, jnp.zeros((2 * side, LANES), F32))
+        total = jnp.zeros((2 * side, LANES), F32)
+        if batch == devices:
+            total = body(0, total)
+        else:
+            total = lax.fori_loop(0, devices // batch, body, total)
         out_ref[...] = total[:side] + total[side:]
 
     return pl.pallas_call(
@@ -419,7 +421,7 @@
         out_shape=jax.ShapeDtypeStruct((side, LANES), F32),
         in_specs=vmem_specs(1),
         out_specs=pl.BlockSpec(memory_space=VMEM),
-        compiler_params=pltpu.CompilerParams(vmem_limit_bytes=8 << 20),
+        compiler_params=pltpu.CompilerParams(vmem_limit_bytes=24 << 20),
         name="node_sums",
     )(in_vmem(got))
 

time: 49.3 us -> 46.9 us (0.951)
  Pallas kernels: 21.9 us -> 19.5 us
    pallas_call x1, Pallas kernels: 5.53 us -> 4.15 us  [backward_and_faces(): pl.pallas_call(kernel, out_shape=(jax.ShapeDtypeStruct(field.shape, F32),...]
    pallas_call x1, Pallas kernels: 3.56 us -> 2.97 us  [node_sums(): pl.pallas_call(kernel, out_shape=jax.ShapeDtypeStruct((side, LANES), F32)...]
where the time goes in v5:
time: 46.9 us; the launch traced here: 46.7 us
  Pallas kernels  19.5 us (42%)
  blocking collectives  13 us (28%)
  starting transfers between devices  7.89 us (17%)
  waiting for transfers between devices  4.75 us (10%)
  between operations  1.51 us (3%)
    all_to_all x1, blocking collectives, per_device(): got = lax.all_to_all(send, ('sweep', 'bulk'), 0, 0, tiled=True)  13 us
    pallas_call x2, Pallas kernels, matrices(): pl.pallas_call(kernel, out_shape=(VMEM(coupled.shape, F32), jax.ShapeDtyp...  8.03 us
    ppermute x4, waiting for transfers between devices, relay(): other = lax.ppermute(leaving, 'sweep', pairs)  4.74 us
    pallas_call x1, Pallas kernels, backward_and_faces(): pl.pallas_call(kernel, out_shape=(jax.ShapeDtypeStruct(field.shape, F32),...  4.15 us
    ppermute x4, starting transfers between devices, relay(): other = lax.ppermute(leaving, 'sweep', pairs)  3.62 us
    ppermute x1, starting transfers between devices, per_device(): first = lax.ppermute(low_edge, 'bulk', low_pairs)  3.03 us
    pallas_call x1, Pallas kernels, node_sums(): pl.pallas_call(kernel, out_shape=jax.ShapeDtypeStruct((side, LANES), F32)...  2.97 us
    pallas_call x1, Pallas kernels, forward_local(): pl.pallas_call(kernel, out_shape=(VMEM(source.shape, F32), jax.ShapeDtype...  1.48 us
  transfers between devices with their start and end apart: 8, of which 3 were waited for; matrix products, arithmetic and copies ran while one was open for 0% of the time, Pallas kernels for 18%

profile of v5, /device:TPU:0, one launch (start us, length us, event | category | flops | bytes accessed | tf_op | source)
XLA Modules:
  0.0 46.7 jit_solution(11939634733479694367)
XLA Ops:
  0.6 0.0 copy-start.8
  0.6 0.0 copy-start
  0.6 1.1 %edge_rows.1 = (f32[160,128]{1,0:T(8,128)S(1)}, f32[160,128]{1,0:T(8,128)S(1)}) custom-call(f32[32,5,16,128]{3,2,1,0:T(8,128)} %psi_ref.1), custom_call_target="tpu_custom_call" | custom-call | flops 10000000000 | bytes 20000000 | tf_op jit(solution)/shard_map/edge_rows/pallas_call | solution.py:84
  1.7 0.0 copy-start.1
  1.8 0.0 copy-start.2
  1.8 0.0 copy-start.3
  1.8 3.0 %collective-permute-start = (f32[160,128]{1,0:T(8,128)S(1)}, f32[160,128]{1,0:T(8,128)S(1)}, u32[]{:S(2)}, u32[]{:S(2)}) collective-permute-start(f32[160,128]{1,0:T(8,128)S(1)} %get-tuple-element.32), channel_id=1, source_target_pairs={{0,1},{1,0},{2,3},{3,2},{4,5},{5,4},{6,7},{7,6},{8,9},{9,8},{10,11... | collective-permute-start | bytes 245768 | tf_op jit(solution)/shard_map/ppermute | solution.py:537
  4.8 0.8 %collective-permute-start.1 = (f32[160,128]{1,0:T(8,128)S(1)}, f32[160,128]{1,0:T(8,128)S(1)}, u32[]{:S(2)}, u32[]{:S(2)}) collective-permute-start(f32[160,128]{1,0:T(8,128)S(1)} %get-tuple-element.33), channel_id=1, source_target_pairs={{1,2},{2,1},{3,4},{4,3},{5,6},{6,5},{9,10},{10,9},{11,12},{12,11},... | collective-permute-start | bytes 245768 | tf_op jit(solution)/shard_map/ppermute | solution.py:538
  5.6 0.0 copy-done.8
  5.6 0.0 copy-done
  5.6 4.1 %forward_matrices.1 = (f32[32,5,5,16,128]{4,3,2,1,0:T(8,128)S(1)}, f32[5,5,16,128]{3,2,1,0:T(8,128)S(1)}) custom-call(f32[32,5,5,16,128]{4,3,2,1,0:T(8,128)S(1)} %copy-done.8, f32[32,5,5,16,128]{4,3,2,1,0:T(8,128)S(1)} %copy-done), custom_call_target="tpu_custom_call" | custom-call | flops 5000000000 | bytes 20000000 | tf_op jit(solution)/shard_map/forward_matrices/pallas_call | solution.py:156
  9.7 0.0 collective-permute-done.first_ref
  9.7 0.0 collective-permute-done.1.second_ref
  9.7 0.0 copy-done.1
  9.7 0.0 copy-done.2
  9.7 0.0 copy-done.3
  9.8 0.0 copy-start.9
  9.8 1.5 %forward_local.1 = (f32[32,5,16,128]{3,2,1,0:T(8,128)S(1)}, f32[5,16,128]{2,1,0:T(8,128)S(1)}) custom-call(f32[32,5,16,128]{3,2,1,0:T(8,128)S(1)} %copy-done.1, f32[32,5,16,128]{3,2,1,0:T(8,128)S(1)} %copy-done.2, f32[32,2,16,128]{3,2,1,0:T(8,128)S(1)} %copy-done.3, f32[160,128]{1,0:T(8,128)S(1)} %collective-permute-done.first_ref, ...), custom_call_target="tpu_custom_call" | custom-call | tf_op jit(solution)/shard_map/forward_local/pallas_call | solution.py:131
  11.3 0.4 collective-permute-start.3
  11.6 0.2 collective-permute-start.2
  11.8 1.0 %collective-permute-done.2.refs_2_ = f32[5,16,128]{2,1,0:T(8,128)S(1)} collective-permute-done((f32[5,16,128]{2,1,0:T(8,128)S(1)}, f32[5,16,128]{2,1,0:T(8,128)S(1)}, u32[]{:S(2)}, u32[]{:S(2)}) %collective-permute-start.2) | collective-permute-done | bytes 40992 | tf_op jit(solution)/shard_map/ppermute | solution.py:518
  12.9 0.0 collective-permute-done.3.refs_3_
  12.9 0.1 join.2
  12.9 2.8 %collective-permute-start.4 = (f32[5,16,128]{2,1,0:T(8,128)S(1)}, f32[5,16,128]{2,1,0:T(8,128)S(1)}, u32[]{:S(2)}, u32[]{:S(2)}) collective-permute-start(f32[5,16,128]{2,1,0:T(8,128)S(1)} %get-tuple-element.43), channel_id=1, source_target_pairs={{0,16},{8,24},{16,0},{24,8},{1,17},{9,25},{17,1},{25,9},{2,18},{10... | collective-permute-start | bytes 122888 | tf_op jit(solution)/shard_map/ppermute | solution.py:518
  15.8 0.0 copy-done.9
  15.8 4.0 %backward_matrices.1 = (f32[32,5,5,16,128]{4,3,2,1,0:T(8,128)S(1)}, f32[5,5,16,128]{3,2,1,0:T(8,128)S(1)}) custom-call(f32[32,5,5,16,128]{4,3,2,1,0:T(8,128)S(1)} %copy-done.9, f32[32,5,5,16,128]{4,3,2,1,0:T(8,128)S(1)} %copy-done), custom_call_target="tpu_custom_call" | custom-call | flops 5000000000 | bytes 20000000 | tf_op jit(solution)/shard_map/backward_matrices/pallas_call | solution.py:156
  19.7 0.0 collective-permute-done.4.other_ref
  19.7 0.0 copy-start.6
  19.8 0.0 copy-start.7
  19.8 0.0 copy-start.4
  19.8 0.0 copy-start.5
  19.8 1.0 %forward_then_back.1 = (f32[32,5,16,128]{3,2,1,0:T(8,128)S(1)}, f32[5,16,128]{2,1,0:T(8,128)S(1)}) custom-call(f32[32,5,16,128]{3,2,1,0:T(8,128)S(1)} %get-tuple-element.36.scaled_ref, f32[5,16,128]{2,1,0:T(8,128)S(1)} %get-tuple-element.41.near_ref, f32[5,5,16,128]{3,2,1,0:T(8,128)S(1)} %get-tuple-element.42.reach_ref, ...), custom_call_target="tpu_custom_call" | custom-call | tf_op jit(solution)/shard_map/forward_then_back/pallas_call | solution.py:198
  20.8 0.1 collective-permute-start.6
  20.9 0.5 %collective-permute-start.5 = (f32[5,16,128]{2,1,0:T(8,128)S(1)}, f32[5,16,128]{2,1,0:T(8,128)S(1)}, u32[]{:S(2)}, u32[]{:S(2)}) collective-permute-start(f32[5,16,128]{2,1,0:T(8,128)S(1)} %get-tuple-element.49.refs_0_), channel_id=1, source_target_pairs={{0,8},{8,0},{16,24},{24,16},{1,9},{9,1},{17,25},{25,17},{2,10},{10... | collective-permute-start | bytes 122888 | tf_op jit(solution)/shard_map/ppermute | solution.py:518
  21.4 1.0 %collective-permute-done.5.refs_2_ = f32[5,16,128]{2,1,0:T(8,128)S(1)} collective-permute-done((f32[5,16,128]{2,1,0:T(8,128)S(1)}, f32[5,16,128]{2,1,0:T(8,128)S(1)}, u32[]{:S(2)}, u32[]{:S(2)}) %collective-permute-start.5) | collective-permute-done | bytes 40992 | tf_op jit(solution)/shard_map/ppermute | solution.py:518
  22.4 0.0 collective-permute-done.6.refs_3_
  22.4 0.1 join.3
  22.5 0.1 collective-permute-start.7
  23.2 0.0 copy-done.6
  23.2 0.0 copy-done.7
  23.2 0.6 %face_slots.1 = (s32[16,128]{1,0:T(8,128)S(1)}, f32[32,128]{1,0:T(8,128)S(1)}) custom-call(s32[16,128]{1,0:T(8,128)S(1)} %bitcast.5, s32[16,128]{1,0:T(8,128)S(1)} %bitcast.6), custom_call_target="tpu_custom_call" | custom-call | flops 4000000 | bytes 10000000 | tf_op jit(solution)/shard_map/face_slots/pallas_call | solution.py:239
  23.8 2.7 %collective-permute-done.7.other_ref = f32[5,16,128]{2,1,0:T(8,128)S(1)} collective-permute-done((f32[5,16,128]{2,1,0:T(8,128)S(1)}, f32[5,16,128]{2,1,0:T(8,128)S(1)}, u32[]{:S(2)}, u32[]{:S(2)}) %collective-permute-start.7) | collective-permute-done | bytes 40992 | tf_op jit(solution)/shard_map/ppermute | solution.py:518
  26.6 0.0 copy-done.4
  26.6 0.0 copy-done.5
  26.6 4.1 %backward_and_faces.1 = (f32[32,5,16,128]{3,2,1,0:T(8,128)}, f32[32,8,128]{2,1,0:T(8,128)S(1)}) custom-call(s32[1]{0:T(128)S(6)} %copy.13.count_ref, f32[32,5,16,128]{3,2,1,0:T(8,128)S(1)} %get-tuple-element.46.field_ref, f32[5,16,128]{2,1,0:T(8,128)S(1)} %get-tuple-element.51.near_ref, f32[5,5,16,128]{3,2,1,0:T(8,128)S(1)} %get-tuple-element.52.reach_ref, ...), custom_call_target="tpu_custom_call" | custom-call | tf_op jit(solution)/shard_map/backward_and_faces/pallas_call | solution.py:363
  30.7 13.0 %all_to_all.5.got_ref = f32[32,8,128]{2,1,0:T(8,128)S(1)} all-to-all(f32[32,8,128]{2,1,0:T(8,128)S(1)} %get-tuple-element.57), channel_id=1, replica_groups=mesh['sweep'=4,'bulk'=8] {'sweep','bulk'}, dimensions={0} | all-to-all | bytes 262144 | tf_op jit(solution)/shard_map/all_to_all | solution.py:555
  43.8 3.0 %node_sums.1 = f32[128,128]{1,0:T(8,128)} custom-call(f32[32,8,128]{2,1,0:T(8,128)S(1)} %all_to_all.5.got_ref), custom_call_target="tpu_custom_call" | custom-call | tf_op jit(solution)/shard_map/node_sums/pallas_call | solution.py:419
Async XLA Ops:
  0.6 5.0 %copy-start.8 = (f32[32,5,5,16,128]{4,3,2,1,0:T(8,128)S(1)}, f32[32,5,5,16,128]{4,3,2,1,0:T(8,128)}, u32[]{:S(2)}) copy-start(f32[32,5,5,16,128]{4,3,2,1,0:T(8,128)} %coupled_ref) | copy-start | bytes 19660804
  0.6 5.0 %copy-start = (f32[32,5,5,16,128]{4,3,2,1,0:T(8,128)S(1)}, f32[32,5,5,16,128]{4,3,2,1,0:T(8,128)}, u32[]{:S(2)}) copy-start(f32[32,5,5,16,128]{4,3,2,1,0:T(8,128)} %inv_ref.5) | copy-start | bytes 19660804
  1.7 8.0 %copy-start.1 = (f32[32,5,16,128]{3,2,1,0:T(8,128)S(1)}, f32[32,5,16,128]{3,2,1,0:T(8,128)}, u32[]{:S(2)}) copy-start(f32[32,5,16,128]{3,2,1,0:T(8,128)} %source_ref.1) | copy-start | bytes 3932164
  1.8 8.0 %copy-start.2 = (f32[32,5,16,128]{3,2,1,0:T(8,128)S(1)}, f32[32,5,16,128]{3,2,1,0:T(8,128)}, u32[]{:S(2)}) copy-start(f32[32,5,16,128]{3,2,1,0:T(8,128)} %psi_ref.1) | copy-start | bytes 3932164
  1.8 8.0 %copy-start.3 = (f32[32,2,16,128]{3,2,1,0:T(8,128)S(1)}, f32[32,2,16,128]{3,2,1,0:T(8,128)}, u32[]{:S(2)}) copy-start(f32[32,2,16,128]{3,2,1,0:T(8,128)} %lateral_ref.1) | copy-start | bytes 1572868
  1.8 7.9 %collective-permute-start = (f32[160,128]{1,0:T(8,128)S(1)}, f32[160,128]{1,0:T(8,128)S(1)}, u32[]{:S(2)}, u32[]{:S(2)}) collective-permute-start(f32[160,128]{1,0:T(8,128)S(1)} %get-tuple-element.32), channel_id=1, source_target_pairs={{0,1},{1,0},{2,3},{3,2},{4,5},{5,4},{6,7},{7,6},{8,9},{9,8},{10,11... | collective-permute-start | bytes 245768 | tf_op jit(solution)/shard_map/ppermute | solution.py:537
  4.8 4.9 %collective-permute-start.1 = (f32[160,128]{1,0:T(8,128)S(1)}, f32[160,128]{1,0:T(8,128)S(1)}, u32[]{:S(2)}, u32[]{:S(2)}) collective-permute-start(f32[160,128]{1,0:T(8,128)S(1)} %get-tuple-element.33), channel_id=1, source_target_pairs={{1,2},{2,1},{3,4},{4,3},{5,6},{6,5},{9,10},{10,9},{11,12},{12,11},... | collective-permute-start | bytes 245768 | tf_op jit(solution)/shard_map/ppermute | solution.py:538
  9.8 6.0 %copy-start.9 = (f32[32,5,5,16,128]{4,3,2,1,0:T(8,128)S(1)}, f32[32,5,5,16,128]{4,3,2,1,0:T(8,128)}, u32[]{:S(2)}) copy-start(f32[32,5,5,16,128]{4,3,2,1,0:T(8,128)} %coupled_ref.1) | copy-start | bytes 19660804
  11.3 1.6 %collective-permute-start.3 = (f32[5,5,16,128]{3,2,1,0:T(8,128)S(1)}, f32[5,5,16,128]{3,2,1,0:T(8,128)S(1)}, u32[]{:S(2)}, u32[]{:S(2)}) collective-permute-start(f32[5,5,16,128]{3,2,1,0:T(8,128)S(1)} %get-tuple-element.40.refs_1_), channel_id=1, source_target_pairs={{0,8},{8,0},{16,24},{24,16},{1,9},{9,1},{17,25},{25,17},{2,10},{10... | collective-permute-start | bytes 614408 | tf_op jit(solution)/shard_map/ppermute | solution.py:521
  11.6 1.2 %collective-permute-start.2 = (f32[5,16,128]{2,1,0:T(8,128)S(1)}, f32[5,16,128]{2,1,0:T(8,128)S(1)}, u32[]{:S(2)}, u32[]{:S(2)}) collective-permute-start(f32[5,16,128]{2,1,0:T(8,128)S(1)} %get-tuple-element.39.refs_0_), channel_id=1, source_target_pairs={{0,8},{8,0},{16,24},{24,16},{1,9},{9,1},{17,25},{25,17},{2,10},{10... | collective-permute-start | bytes 122888 | tf_op jit(solution)/shard_map/ppermute | solution.py:518
  12.9 6.8 %collective-permute-start.4 = (f32[5,16,128]{2,1,0:T(8,128)S(1)}, f32[5,16,128]{2,1,0:T(8,128)S(1)}, u32[]{:S(2)}, u32[]{:S(2)}) collective-permute-start(f32[5,16,128]{2,1,0:T(8,128)S(1)} %get-tuple-element.43), channel_id=1, source_target_pairs={{0,16},{8,24},{16,0},{24,8},{1,17},{9,25},{17,1},{25,9},{2,18},{10... | collective-permute-start | bytes 122888 | tf_op jit(solution)/shard_map/ppermute | solution.py:518
  19.7 3.5 %copy-start.6 = (s32[2048,1]{0,1:T(1,128)S(1)}, s32[2048,1]{0,1:T(1,128)}, u32[]{:S(2)}) copy-start(s32[2048,1]{0,1:T(1,128)} %param.19) | copy-start | bytes 24580
  19.8 3.5 %copy-start.7 = (s32[2048]{0:T(1024)S(1)}, s32[2048]{0:T(1024)}, u32[]{:S(2)}) copy-start(s32[2048]{0:T(1024)} %param.20) | copy-start | bytes 24580
  19.8 6.8 %copy-start.4 = (f32[5,2048]{1,0:T(8,128)S(1)}, f32[5,2048]{1,0:T(8,128)}, u32[]{:S(2)}) copy-start(f32[5,2048]{1,0:T(8,128)} %weight_ref.1) | copy-start | bytes 122884
  19.8 6.8 %copy-start.5 = (s32[2048]{0:T(1024)S(1)}, s32[2048]{0:T(1024)}, u32[]{:S(2)}) copy-start(s32[2048]{0:T(1024)} %param.18) | copy-start | bytes 24580
  20.8 1.6 %collective-permute-start.6 = (f32[5,5,16,128]{3,2,1,0:T(8,128)S(1)}, f32[5,5,16,128]{3,2,1,0:T(8,128)S(1)}, u32[]{:S(2)}, u32[]{:S(2)}) collective-permute-start(f32[5,5,16,128]{3,2,1,0:T(8,128)S(1)} %get-tuple-element.50.refs_1_), channel_id=1, source_target_pairs={{0,8},{8,0},{16,24},{24,16},{1,9},{9,1},{17,25},{25,17},{2,10},{10... | collective-permute-start | bytes 614408 | tf_op jit(solution)/shard_map/ppermute | solution.py:521
  20.9 1.5 %collective-permute-start.5 = (f32[5,16,128]{2,1,0:T(8,128)S(1)}, f32[5,16,128]{2,1,0:T(8,128)S(1)}, u32[]{:S(2)}, u32[]{:S(2)}) collective-permute-start(f32[5,16,128]{2,1,0:T(8,128)S(1)} %get-tuple-element.49.refs_0_), channel_id=1, source_target_pairs={{0,8},{8,0},{16,24},{24,16},{1,9},{9,1},{17,25},{25,17},{2,10},{10... | collective-permute-start | bytes 122888 | tf_op jit(solution)/shard_map/ppermute | solution.py:518
  22.5 4.1 %collective-permute-start.7 = (f32[5,16,128]{2,1,0:T(8,128)S(1)}, f32[5,16,128]{2,1,0:T(8,128)S(1)}, u32[]{:S(2)}, u32[]{:S(2)}) collective-permute-start(f32[5,16,128]{2,1,0:T(8,128)S(1)} %get-tuple-element.53), channel_id=1, source_target_pairs={{0,16},{8,24},{16,0},{24,8},{1,17},{9,25},{17,1},{25,9},{2,18},{10... | collective-permute-start | bytes 122888 | tf_op jit(solution)/shard_map/ppermute | solution.py:518

commit v6 on v5

--- a/solution.py
+++ b/solution.py
@@ -53,6 +53,13 @@
         for x in range(5):
             ratio_ref[at, c, x, rows, :] = ratio[c][x]
             total_ref[c, x, rows, :] = total[c][x]
+
+
+def keep_map(map_ref, total_ref, leaving, width):
+    map_ref[:5] = total_ref[...]
+    for h, rows in enumerate(halves(width)):
+        for c in range(5):
+            map_ref[5, c, rows, :] = leaving[h][c]
 
 
 def set_identity(total_ref, planes):
@@ -93,11 +100,11 @@
     )(in_hbm(psi))
 
 
-def forward_local(source, psi, lateral, first, second, ratio, inv):
+def forward_local(source, psi, lateral, first, second, ratio, inv, total):
     planes, width = source.shape[0], source.shape[2]
 
-    def kernel(source_ref, psi_ref, lateral_ref, first_ref, second_ref, ratio_ref, inv_ref,
-               scaled_ref, leaving_ref):
+    def kernel(source_ref, psi_ref, lateral_ref, first_ref, second_ref, ratio_ref, inv_ref, total_ref,
+               scaled_ref, map_ref):
         is_odd = lax.rem(lax.axis_index("bulk"), 2) == 1
 
         def body(i, state):
@@ -124,18 +131,16 @@
 
         zero = [[jnp.zeros((8, LANES), F32)] * 5 for _ in halves(width)]
         state = lax.fori_loop(0, planes, body, zero, unroll=2)
-        for h, rows in enumerate(halves(width)):
-            for c in range(5):
-                leaving_ref[c, rows, :] = state[h][c]
-
-    return pl.pallas_call(
-        kernel,
-        out_shape=(VMEM(source.shape, F32), jax.ShapeDtypeStruct(source.shape[1:], F32)),
-        in_specs=vmem_specs(7),
+        keep_map(map_ref, total_ref, state, width)
+
+    return pl.pallas_call(
+        kernel,
+        out_shape=(VMEM(source.shape, F32), jax.ShapeDtypeStruct((6,) + source.shape[1:], F32)),
+        in_specs=vmem_specs(8),
         out_specs=tuple(vmem_specs(2)),
         compiler_params=pltpu.CompilerParams(vmem_limit_bytes=4 << 20),
         name="forward_local",
-    )(*[in_vmem(v) for v in (source, psi, lateral, first, second, ratio, inv)])
+    )(*[in_vmem(v) for v in (source, psi, lateral, first, second, ratio, inv, total)])
 
 
 def matrices(coupled, inv, backward, name):
@@ -164,10 +169,11 @@
     )(in_vmem(coupled), in_vmem(inv))
 
 
-def forward_then_back(scaled, arriving, ratio, back_ratio):
+def forward_then_back(scaled, arriving, ratio, back_ratio, back_total):
     planes, width = scaled.shape[0], scaled.shape[2]
 
-    def kernel(scaled_ref, near_ref, reach_ref, other_ref, ratio_ref, back_ref, field_ref, leaving_ref):
+    def kernel(scaled_ref, near_ref, reach_ref, other_ref, ratio_ref, back_ref, total_ref,
+               field_ref, map_ref):
         def ahead(i, state):
             out = []
             for h, rows in enumerate(halves(width)):
@@ -191,18 +197,16 @@
 
         zero = [[jnp.zeros((8, LANES), F32)] * 5 for _ in halves(width)]
         state = lax.fori_loop(0, planes, back, zero, unroll=4)
-        for h, rows in enumerate(halves(width)):
-            for c in range(5):
-                leaving_ref[c, rows, :] = state[h][c]
-
-    return pl.pallas_call(
-        kernel,
-        out_shape=(VMEM(scaled.shape, F32), jax.ShapeDtypeStruct(scaled.shape[1:], F32)),
-        in_specs=vmem_specs(6),
+        keep_map(map_ref, total_ref, state, width)
+
+    return pl.pallas_call(
+        kernel,
+        out_shape=(VMEM(scaled.shape, F32), jax.ShapeDtypeStruct((6,) + scaled.shape[1:], F32)),
+        in_specs=vmem_specs(7),
         out_specs=tuple(vmem_specs(2)),
         compiler_params=pltpu.CompilerParams(vmem_limit_bytes=4 << 20),
         name="forward_then_back",
-    )(in_vmem(scaled), *[in_vmem(v) for v in arriving], in_vmem(ratio), in_vmem(back_ratio))
+    )(*[in_vmem(v) for v in (scaled, *arriving, ratio, back_ratio, back_total)])
 
 
 def face_slots(owner, node, owners):
@@ -463,67 +467,64 @@
     return start
 
 
-def join(stage, backward, near, reach, leaving, total, other, other_total, carry_total):
+def join(stage, backward, near, reach, own, other, whole):
     first = near is None
-    width = leaving.shape[1]
-    outs = [leaving.shape, total.shape, leaving.shape] + ([total.shape] if carry_total else [])
+    _, _, width, _ = own.shape
+    vector = own.shape[1:]
+    outs = [vector, (5,) + vector, own.shape if whole else vector]
+    operands = [own, other] + ([] if first else [near, reach])
 
     def kernel(*refs):
         ins, out = refs[:len(operands)], refs[len(operands):]
         after = comes_after(stage, backward)
         for rows in halves(width):
-            own, theirs = load_vector(ins[0], rows), load_vector(ins[2], rows)
-            own_total, their_total = load_matrix(ins[1], rows), load_matrix(ins[3], rows)
+            mine, theirs = load_vector(ins[0].at[5], rows), load_vector(ins[1].at[5], rows)
+            my_total, their_total = load_matrix(ins[0], rows), load_matrix(ins[1], rows)
             if first:
                 entering = theirs
                 through = their_total
                 before = [jnp.zeros((8, LANES), F32)] * 5
                 unit = [[jnp.full((8, LANES), 1.0 if c == d else 0.0, F32) for d in range(5)] for c in range(5)]
             else:
-                before, unit = load_vector(ins[4], rows), load_matrix(ins[5], rows)
+                before, unit = load_vector(ins[2], rows), load_matrix(ins[3], rows)
                 entering = [a + b for a, b in zip(before, matvec(unit, theirs))]
                 through = matmat(unit, their_total)
             entering, through = pick(after, entering, before), pick(after, through, unit)
-            downstream = pick(after, own_total, their_total)
-            sent = matvec(downstream, pick(after, theirs, own))
-            sent = [a + b for a, b in zip(pick(after, own, theirs), sent)]
+            downstream = pick(after, my_total, their_total)
+            sent = matvec(downstream, pick(after, theirs, mine))
+            sent = [a + b for a, b in zip(pick(after, mine, theirs), sent)]
+            sent_ref = out[2].at[5] if whole else out[2]
             for c in range(5):
                 out[0][c, rows, :] = entering[c]
-                out[2][c, rows, :] = sent[c]
+                sent_ref[c, rows, :] = sent[c]
                 for d in range(5):
                     out[1][c, d, rows, :] = through[c][d]
-            if carry_total:
-                whole = matmat(downstream, pick(after, their_total, own_total))
+            if whole:
+                product = matmat(downstream, pick(after, their_total, my_total))
                 for c in range(5):
                     for d in range(5):
-                        out[3][c, d, rows, :] = whole[c][d]
-
-    operands = [leaving, total, other, other_total] + ([] if first else [near, reach])
+                        out[2][c, d, rows, :] = product[c][d]
+
     return pl.pallas_call(
         kernel,
         out_shape=tuple(jax.ShapeDtypeStruct(shape, F32) for shape in outs),
         in_specs=vmem_specs(len(operands)),
-        out_specs=tuple(vmem_specs(len(outs))),
+        out_specs=tuple(vmem_specs(3)),
         compiler_params=pltpu.CompilerParams(vmem_limit_bytes=4 << 20),
         name="join",
     )(*[in_vmem(v) for v in operands])
 
 
-def relay(total, leaving, backward):
+def relay(own, backward):
     size = lax.axis_size("sweep")
     stages = size.bit_length() - 1
     near = reach = None
     for stage in range(stages):
         pairs = [(i, i ^ (1 << stage)) for i in range(size)]
-        other = lax.ppermute(leaving, "sweep", pairs)
+        other = lax.ppermute(own, "sweep", pairs)
         if stage == stages - 1:
-            return (near, reach, other), leaving
-        other_total = lax.ppermute(total, "sweep", pairs)
-        carry_total = stage + 2 < stages
-        joined = join(stage, backward, near, reach, leaving, total, other, other_total, carry_total)
-        near, reach, leaving = joined[:3]
-        if carry_total:
-            total = joined[3]
+            return (near, reach, other), own
+        near, reach, own = join(stage, backward, near, reach, own, other, stage + 2 < stages)
 
 
 def per_device(source, psi_old, lateral, lower_jac, upper_jac, diag_inv, face_weight, face_cell,
@@ -538,14 +539,12 @@
     second = lax.ppermute(high_edge, "bulk", high_pairs)
 
     ratio, total = matrices(lower_jac, diag_inv, False, "forward_matrices")
-    scaled, leaving = forward_local(source, psi_old, lateral, first, second, ratio, diag_inv)
-    total, leaving = lax.optimization_barrier((total, leaving))
-    arriving, joined = relay(total, leaving, False)
+    scaled, own = forward_local(source, psi_old, lateral, first, second, ratio, diag_inv, total)
+    arriving, joined = relay(own, False)
     upper_jac, joined = lax.optimization_barrier((upper_jac, joined))
     back_ratio, back_total = matrices(upper_jac, diag_inv, True, "backward_matrices")
-    field, leaving = forward_then_back(scaled, arriving, ratio, back_ratio)
-    back_total, leaving = lax.optimization_barrier((back_total, leaving))
-    arriving, _ = relay(back_total, leaving, True)
+    field, own = forward_then_back(scaled, arriving, ratio, back_ratio, back_total)
+    arriving, _ = relay(own, True)
 
     slots = face_cell.shape[0]
     rows = (slots // LANES, LANES)

time: 46.9 us -> 46.9 us (level)
  waiting for transfers between devices: 4.75 us -> 5.41 us
  starting transfers between devices: 7.89 us -> 7.23 us
    ppermute x6 -> x4, starting transfers between devices: 4.08 us -> 3.41 us  [relay(): other = lax.ppermute(own, 'sweep', pairs)]
    ppermute x6 -> x4, waiting for transfers between devices: 4.74 us -> 5.41 us  [relay(): other = lax.ppermute(own, 'sweep', pairs)]
  transfers between devices with their start and end apart: 8 -> 6, of which waited for: 3 -> 3; matrix products, arithmetic and copies ran while one was open for 0% -> 0% of each run, Pallas kernels for 18% -> 18%
where the time goes in v6:
time: 46.9 us; the launch traced here: 46.7 us
  Pallas kernels  19.4 us (41%)
  blocking collectives  13 us (28%)
  starting transfers between devices  7.23 us (15%)
  waiting for transfers between devices  5.41 us (12%)
  between operations  1.51 us (3%)
    all_to_all x1, blocking collectives, per_device(): got = lax.all_to_all(send, ('sweep', 'bulk'), 0, 0, tiled=True)  13 us
    pallas_call x2, Pallas kernels, matrices(): pl.pallas_call(kernel, out_shape=(VMEM(coupled.shape, F32), jax.ShapeDtyp...  7.9 us
    ppermute x4, waiting for transfers between devices, relay(): other = lax.ppermute(own, 'sweep', pairs)  5.41 us
    pallas_call x1, Pallas kernels, backward_and_faces(): pl.pallas_call(kernel, out_shape=(jax.ShapeDtypeStruct(field.shape, F32),...  4.17 us
    ppermute x4, starting transfers between devices, relay(): other = lax.ppermute(own, 'sweep', pairs)  3.41 us
    ppermute x1, starting transfers between devices, per_device(): first = lax.ppermute(low_edge, 'bulk', low_pairs)  3.03 us
    pallas_call x1, Pallas kernels, node_sums(): pl.pallas_call(kernel, out_shape=jax.ShapeDtypeStruct((side, LANES), F32)...  2.98 us
    pallas_call x1, Pallas kernels, forward_local(): pl.pallas_call(kernel, out_shape=(VMEM(source.shape, F32), jax.ShapeDtype...  1.49 us
  transfers between devices with their start and end apart: 6, of which 3 were waited for; matrix products, arithmetic and copies ran while one was open for 0% of the time, Pallas kernels for 18%

profile of v6, /device:TPU:0, one launch (start us, length us, event | category | flops | bytes accessed | tf_op | source)
XLA Modules:
  0.0 46.7 jit_solution(11709967764001430446)
XLA Ops:
  0.6 0.0 copy-start.8
  0.6 0.0 copy-start
  0.6 1.1 %edge_rows.1 = (f32[160,128]{1,0:T(8,128)S(1)}, f32[160,128]{1,0:T(8,128)S(1)}) custom-call(f32[32,5,16,128]{3,2,1,0:T(8,128)} %psi_ref.1), custom_call_target="tpu_custom_call" | custom-call | flops 10000000000 | bytes 20000000 | tf_op jit(solution)/shard_map/edge_rows/pallas_call | solution.py:91
  1.7 0.0 copy-start.1
  1.8 0.0 copy-start.2
  1.8 0.0 copy-start.3
  1.8 3.0 %collective-permute-start = (f32[160,128]{1,0:T(8,128)S(1)}, f32[160,128]{1,0:T(8,128)S(1)}, u32[]{:S(2)}, u32[]{:S(2)}) collective-permute-start(f32[160,128]{1,0:T(8,128)S(1)} %get-tuple-element.28), channel_id=1, source_target_pairs={{0,1},{1,0},{2,3},{3,2},{4,5},{5,4},{6,7},{7,6},{8,9},{9,8},{10,11... | collective-permute-start | bytes 245768 | tf_op jit(solution)/shard_map/ppermute | solution.py:538
  4.8 0.8 %collective-permute-start.1 = (f32[160,128]{1,0:T(8,128)S(1)}, f32[160,128]{1,0:T(8,128)S(1)}, u32[]{:S(2)}, u32[]{:S(2)}) collective-permute-start(f32[160,128]{1,0:T(8,128)S(1)} %get-tuple-element.29), channel_id=1, source_target_pairs={{1,2},{2,1},{3,4},{4,3},{5,6},{6,5},{9,10},{10,9},{11,12},{12,11},... | collective-permute-start | bytes 245768 | tf_op jit(solution)/shard_map/ppermute | solution.py:539
  5.6 0.0 copy-done.8
  5.6 0.0 copy-done
  5.6 3.9 %forward_matrices.1 = (f32[32,5,5,16,128]{4,3,2,1,0:T(8,128)S(1)}, f32[5,5,16,128]{3,2,1,0:T(8,128)S(1)}) custom-call(f32[32,5,5,16,128]{4,3,2,1,0:T(8,128)S(1)} %copy-done.8, f32[32,5,5,16,128]{4,3,2,1,0:T(8,128)S(1)} %copy-done), custom_call_target="tpu_custom_call" | custom-call | flops 5000000000 | bytes 20000000 | tf_op jit(solution)/shard_map/forward_matrices/pallas_call | solution.py:161
  9.6 0.0 collective-permute-done.first_ref
  9.6 0.0 collective-permute-done.1.second_ref
  9.6 0.0 copy-done.1
  9.6 0.0 copy-done.2
  9.6 0.0 copy-done.3
  9.6 0.0 copy-start.9
  9.6 1.5 %forward_local.1 = (f32[32,5,16,128]{3,2,1,0:T(8,128)S(1)}, f32[6,5,16,128]{3,2,1,0:T(8,128)S(1)}) custom-call(f32[32,5,16,128]{3,2,1,0:T(8,128)S(1)} %copy-done.1, f32[32,5,16,128]{3,2,1,0:T(8,128)S(1)} %copy-done.2, f32[32,2,16,128]{3,2,1,0:T(8,128)S(1)} %copy-done.3, f32[160,128]{1,0:T(8,128)S(1)} %collective-permute-done.first_ref, ...), custom_call_target="tpu_custom_call" | custom-call | tf_op jit(solution)/shard_map/forward_local/pallas_call | solution.py:136
  11.1 0.4 collective-permute-start.2
  11.5 1.2 %collective-permute-done.2.refs_1_ = f32[6,5,16,128]{3,2,1,0:T(8,128)S(1)} collective-permute-done((f32[6,5,16,128]{3,2,1,0:T(8,128)S(1)}, f32[6,5,16,128]{3,2,1,0:T(8,128)S(1)}, u32[]{:S(2)}, u32[]{:S(2)}) %collective-permute-start.2) | collective-permute-done | bytes 245792 | tf_op jit(solution)/shard_map/ppermute | solution.py:524
  12.7 0.1 join.2
  12.8 2.9 %collective-permute-start.3 = (f32[5,16,128]{2,1,0:T(8,128)S(1)}, f32[5,16,128]{2,1,0:T(8,128)S(1)}, u32[]{:S(2)}, u32[]{:S(2)}) collective-permute-start(f32[5,16,128]{2,1,0:T(8,128)S(1)} %get-tuple-element.37), channel_id=1, source_target_pairs={{0,16},{8,24},{16,0},{24,8},{1,17},{9,25},{17,1},{25,9},{2,18},{10... | collective-permute-start | bytes 122888 | tf_op jit(solution)/shard_map/ppermute | solution.py:524
  15.6 0.0 copy-done.9
  15.6 4.0 %backward_matrices.1 = (f32[32,5,5,16,128]{4,3,2,1,0:T(8,128)S(1)}, f32[5,5,16,128]{3,2,1,0:T(8,128)S(1)}) custom-call(f32[32,5,5,16,128]{4,3,2,1,0:T(8,128)S(1)} %copy-done.9, f32[32,5,5,16,128]{4,3,2,1,0:T(8,128)S(1)} %copy-done), custom_call_target="tpu_custom_call" | custom-call | flops 5000000000 | bytes 20000000 | tf_op jit(solution)/shard_map/backward_matrices/pallas_call | solution.py:161
  19.6 0.0 collective-permute-done.3.other_ref
  19.6 0.0 copy-start.6
  19.6 0.0 copy-start.7
  19.6 0.0 copy-start.4
  19.6 0.0 copy-start.5
  19.7 1.1 %forward_then_back.1 = (f32[32,5,16,128]{3,2,1,0:T(8,128)S(1)}, f32[6,5,16,128]{3,2,1,0:T(8,128)S(1)}) custom-call(f32[32,5,16,128]{3,2,1,0:T(8,128)S(1)} %get-tuple-element.33.scaled_ref, f32[5,16,128]{2,1,0:T(8,128)S(1)} %get-tuple-element.35.near_ref, f32[5,5,16,128]{3,2,1,0:T(8,128)S(1)} %get-tuple-element.36.reach_ref, ...), custom_call_target="tpu_custom_call" | custom-call | tf_op jit(solution)/shard_map/forward_then_back/pallas_call | solution.py:202
  20.8 0.1 collective-permute-start.4
  20.8 1.5 %collective-permute-done.4.refs_1_ = f32[6,5,16,128]{3,2,1,0:T(8,128)S(1)} collective-permute-done((f32[6,5,16,128]{3,2,1,0:T(8,128)S(1)}, f32[6,5,16,128]{3,2,1,0:T(8,128)S(1)}, u32[]{:S(2)}, u32[]{:S(2)}) %collective-permute-start.4) | collective-permute-done | bytes 245792 | tf_op jit(solution)/shard_map/ppermute | solution.py:524
  22.4 0.1 collective-permute-start.5
  23.1 0.0 copy-done.6
  23.2 0.0 copy-done.7
  23.2 0.6 %face_slots.1 = (s32[16,128]{1,0:T(8,128)S(1)}, f32[32,128]{1,0:T(8,128)S(1)}) custom-call(s32[16,128]{1,0:T(8,128)S(1)} %bitcast.5, s32[16,128]{1,0:T(8,128)S(1)} %bitcast.6), custom_call_target="tpu_custom_call" | custom-call | flops 4000000 | bytes 10000000 | tf_op jit(solution)/shard_map/face_slots/pallas_call | solution.py:243
  23.8 2.7 %collective-permute-done.5.other_ref = f32[5,16,128]{2,1,0:T(8,128)S(1)} collective-permute-done((f32[5,16,128]{2,1,0:T(8,128)S(1)}, f32[5,16,128]{2,1,0:T(8,128)S(1)}, u32[]{:S(2)}, u32[]{:S(2)}) %collective-permute-start.5) | collective-permute-done | bytes 40992 | tf_op jit(solution)/shard_map/ppermute | solution.py:524
  26.5 0.0 copy-done.4
  26.5 0.0 copy-done.5
  26.5 4.2 %backward_and_faces.1 = (f32[32,5,16,128]{3,2,1,0:T(8,128)}, f32[32,8,128]{2,1,0:T(8,128)S(1)}) custom-call(s32[1]{0:T(128)S(6)} %copy.13.count_ref, f32[32,5,16,128]{3,2,1,0:T(8,128)S(1)} %get-tuple-element.41.field_ref, f32[5,16,128]{2,1,0:T(8,128)S(1)} %get-tuple-element.43.near_ref, f32[5,5,16,128]{3,2,1,0:T(8,128)S(1)} %get-tuple-element.44.reach_ref, ...), custom_call_target="tpu_custom_call" | custom-call | tf_op jit(solution)/shard_map/backward_and_faces/pallas_call | solution.py:367
  30.6 13.0 %all_to_all.5.got_ref = f32[32,8,128]{2,1,0:T(8,128)S(1)} all-to-all(f32[32,8,128]{2,1,0:T(8,128)S(1)} %get-tuple-element.49), channel_id=1, replica_groups=mesh['sweep'=4,'bulk'=8] {'sweep','bulk'}, dimensions={0} | all-to-all | bytes 262144 | tf_op jit(solution)/shard_map/all_to_all | solution.py:554
  43.7 3.0 %node_sums.1 = f32[128,128]{1,0:T(8,128)} custom-call(f32[32,8,128]{2,1,0:T(8,128)S(1)} %all_to_all.5.got_ref), custom_call_target="tpu_custom_call" | custom-call | tf_op jit(solution)/shard_map/node_sums/pallas_call | solution.py:423
  (1 shorter events, 0.0 us)
Async XLA Ops:
  0.6 5.0 %copy-start.8 = (f32[32,5,5,16,128]{4,3,2,1,0:T(8,128)S(1)}, f32[32,5,5,16,128]{4,3,2,1,0:T(8,128)}, u32[]{:S(2)}) copy-start(f32[32,5,5,16,128]{4,3,2,1,0:T(8,128)} %coupled_ref) | copy-start | bytes 19660804
  0.6 5.0 %copy-start = (f32[32,5,5,16,128]{4,3,2,1,0:T(8,128)S(1)}, f32[32,5,5,16,128]{4,3,2,1,0:T(8,128)}, u32[]{:S(2)}) copy-start(f32[32,5,5,16,128]{4,3,2,1,0:T(8,128)} %inv_ref.5) | copy-start | bytes 19660804
  1.7 7.9 %copy-start.1 = (f32[32,5,16,128]{3,2,1,0:T(8,128)S(1)}, f32[32,5,16,128]{3,2,1,0:T(8,128)}, u32[]{:S(2)}) copy-start(f32[32,5,16,128]{3,2,1,0:T(8,128)} %source_ref.1) | copy-start | bytes 3932164
  1.8 7.9 %copy-start.2 = (f32[32,5,16,128]{3,2,1,0:T(8,128)S(1)}, f32[32,5,16,128]{3,2,1,0:T(8,128)}, u32[]{:S(2)}) copy-start(f32[32,5,16,128]{3,2,1,0:T(8,128)} %psi_ref.1) | copy-start | bytes 3932164
  1.8 7.9 %copy-start.3 = (f32[32,2,16,128]{3,2,1,0:T(8,128)S(1)}, f32[32,2,16,128]{3,2,1,0:T(8,128)}, u32[]{:S(2)}) copy-start(f32[32,2,16,128]{3,2,1,0:T(8,128)} %lateral_ref.1) | copy-start | bytes 1572868
  1.8 7.8 %collective-permute-start = (f32[160,128]{1,0:T(8,128)S(1)}, f32[160,128]{1,0:T(8,128)S(1)}, u32[]{:S(2)}, u32[]{:S(2)}) collective-permute-start(f32[160,128]{1,0:T(8,128)S(1)} %get-tuple-element.28), channel_id=1, source_target_pairs={{0,1},{1,0},{2,3},{3,2},{4,5},{5,4},{6,7},{7,6},{8,9},{9,8},{10,11... | collective-permute-start | bytes 245768 | tf_op jit(solution)/shard_map/ppermute | solution.py:538
  4.8 4.8 %collective-permute-start.1 = (f32[160,128]{1,0:T(8,128)S(1)}, f32[160,128]{1,0:T(8,128)S(1)}, u32[]{:S(2)}, u32[]{:S(2)}) collective-permute-start(f32[160,128]{1,0:T(8,128)S(1)} %get-tuple-element.29), channel_id=1, source_target_pairs={{1,2},{2,1},{3,4},{4,3},{5,6},{6,5},{9,10},{10,9},{11,12},{12,11},... | collective-permute-start | bytes 245768 | tf_op jit(solution)/shard_map/ppermute | solution.py:539
  9.6 6.0 %copy-start.9 = (f32[32,5,5,16,128]{4,3,2,1,0:T(8,128)S(1)}, f32[32,5,5,16,128]{4,3,2,1,0:T(8,128)}, u32[]{:S(2)}) copy-start(f32[32,5,5,16,128]{4,3,2,1,0:T(8,128)} %coupled_ref.1) | copy-start | bytes 19660804
  11.1 1.6 %collective-permute-start.2 = (f32[6,5,16,128]{3,2,1,0:T(8,128)S(1)}, f32[6,5,16,128]{3,2,1,0:T(8,128)S(1)}, u32[]{:S(2)}, u32[]{:S(2)}) collective-permute-start(f32[6,5,16,128]{3,2,1,0:T(8,128)S(1)} %get-tuple-element.34.refs_0_), channel_id=1, source_target_pairs={{0,8},{8,0},{16,24},{24,16},{1,9},{9,1},{17,25},{25,17},{2,10},{10... | collective-permute-start | bytes 737288 | tf_op jit(solution)/shard_map/ppermute | solution.py:524
  12.8 6.8 %collective-permute-start.3 = (f32[5,16,128]{2,1,0:T(8,128)S(1)}, f32[5,16,128]{2,1,0:T(8,128)S(1)}, u32[]{:S(2)}, u32[]{:S(2)}) collective-permute-start(f32[5,16,128]{2,1,0:T(8,128)S(1)} %get-tuple-element.37), channel_id=1, source_target_pairs={{0,16},{8,24},{16,0},{24,8},{1,17},{9,25},{17,1},{25,9},{2,18},{10... | collective-permute-start | bytes 122888 | tf_op jit(solution)/shard_map/ppermute | solution.py:524
  19.6 3.5 %copy-start.6 = (s32[2048,1]{0,1:T(1,128)S(1)}, s32[2048,1]{0,1:T(1,128)}, u32[]{:S(2)}) copy-start(s32[2048,1]{0,1:T(1,128)} %param.19) | copy-start | bytes 24580
  19.6 3.5 %copy-start.7 = (s32[2048]{0:T(1024)S(1)}, s32[2048]{0:T(1024)}, u32[]{:S(2)}) copy-start(s32[2048]{0:T(1024)} %param.20) | copy-start | bytes 24580
  19.6 6.8 %copy-start.4 = (f32[5,2048]{1,0:T(8,128)S(1)}, f32[5,2048]{1,0:T(8,128)}, u32[]{:S(2)}) copy-start(f32[5,2048]{1,0:T(8,128)} %weight_ref.1) | copy-start | bytes 122884
  19.6 6.8 %copy-start.5 = (s32[2048]{0:T(1024)S(1)}, s32[2048]{0:T(1024)}, u32[]{:S(2)}) copy-start(s32[2048]{0:T(1024)} %param.18) | copy-start | bytes 24580
  20.8 1.6 %collective-permute-start.4 = (f32[6,5,16,128]{3,2,1,0:T(8,128)S(1)}, f32[6,5,16,128]{3,2,1,0:T(8,128)S(1)}, u32[]{:S(2)}, u32[]{:S(2)}) collective-permute-start(f32[6,5,16,128]{3,2,1,0:T(8,128)S(1)} %get-tuple-element.42.refs_0_), channel_id=1, source_target_pairs={{0,8},{8,0},{16,24},{24,16},{1,9},{9,1},{17,25},{25,17},{2,10},{10... | collective-permute-start | bytes 737288 | tf_op jit(solution)/shard_map/ppermute | solution.py:524
  22.4 4.1 %collective-permute-start.5 = (f32[5,16,128]{2,1,0:T(8,128)S(1)}, f32[5,16,128]{2,1,0:T(8,128)S(1)}, u32[]{:S(2)}, u32[]{:S(2)}) collective-permute-start(f32[5,16,128]{2,1,0:T(8,128)S(1)} %get-tuple-element.45), channel_id=1, source_target_pairs={{0,16},{8,24},{16,0},{24,8},{1,17},{9,25},{17,1},{25,9},{2,18},{10... | collective-permute-start | bytes 122888 | tf_op jit(solution)/shard_map/ppermute | solution.py:524

commit v7 on v6

--- a/solution.py
+++ b/solution.py
@@ -100,10 +100,10 @@
     )(in_hbm(psi))
 
 
-def forward_local(source, psi, lateral, first, second, ratio, inv, total):
+def forward_local(source, psi, lateral, second, first, ratio, inv, total):
     planes, width = source.shape[0], source.shape[2]
 
-    def kernel(source_ref, psi_ref, lateral_ref, first_ref, second_ref, ratio_ref, inv_ref, total_ref,
+    def kernel(source_ref, psi_ref, lateral_ref, second_ref, first_ref, ratio_ref, inv_ref, total_ref,
                scaled_ref, map_ref):
         is_odd = lax.rem(lax.axis_index("bulk"), 2) == 1
 
@@ -140,7 +140,7 @@
         out_specs=tuple(vmem_specs(2)),
         compiler_params=pltpu.CompilerParams(vmem_limit_bytes=4 << 20),
         name="forward_local",
-    )(*[in_vmem(v) for v in (source, psi, lateral, first, second, ratio, inv, total)])
+    )(*[in_vmem(v) for v in (source, psi, lateral, second, first, ratio, inv, total)])
 
 
 def matrices(coupled, inv, backward, name):
@@ -535,11 +535,11 @@
     high_pairs = [(i, j) for i in range(bulk) for j in [i + 1 if i % 2 else i - 1] if 0 <= j < bulk]
     low_edge, high_edge = edge_rows(psi_old)
     low_edge, high_edge, lower_jac = lax.optimization_barrier((low_edge, high_edge, lower_jac))
+    second = lax.ppermute(high_edge, "bulk", high_pairs)
     first = lax.ppermute(low_edge, "bulk", low_pairs)
-    second = lax.ppermute(high_edge, "bulk", high_pairs)
 
     ratio, total = matrices(lower_jac, diag_inv, False, "forward_matrices")
-    scaled, own = forward_local(source, psi_old, lateral, first, second, ratio, diag_inv, total)
+    scaled, own = forward_local(source, psi_old, lateral, second, first, ratio, diag_inv, total)
     arriving, joined = relay(own, False)
     upper_jac, joined = lax.optimization_barrier((upper_jac, joined))
     back_ratio, back_total = matrices(upper_jac, diag_inv, True, "backward_matrices")

time: 46.9 us -> 46.9 us (level)
  starting transfers between devices: 7.23 us -> 9.15 us
  blocking collectives: 13 us -> 11.3 us
    ppermute x1, starting transfers between devices: 3.03 us -> 6.06 us  [per_device(): first = lax.ppermute(low_edge, 'bulk', low_pairs)]
    all_to_all x1, blocking collectives: 13 us -> 11.3 us  [per_device(): got = lax.all_to_all(send, ('sweep', 'bulk'), 0, 0, tiled=True)]
    ppermute x4, starting transfers between devices: 3.41 us -> 2.3 us  [relay(): other = lax.ppermute(own, 'sweep', pairs)]
where the time goes in v7:
time: 46.9 us; the launch traced here: 46.7 us
  Pallas kernels  19.4 us (41%)
  blocking collectives  11.3 us (24%)
  starting transfers between devices  9.15 us (20%)
  waiting for transfers between devices  5.21 us (11%)
  between operations  1.51 us (3%)
    all_to_all x1, blocking collectives, per_device(): got = lax.all_to_all(send, ('sweep', 'bulk'), 0, 0, tiled=True)  11.3 us
    pallas_call x2, Pallas kernels, matrices(): pl.pallas_call(kernel, out_shape=(VMEM(coupled.shape, F32), jax.ShapeDtyp...  7.9 us
    ppermute x1, starting transfers between devices, per_device(): first = lax.ppermute(low_edge, 'bulk', low_pairs)  6.06 us
    ppermute x4, waiting for transfers between devices, relay(): other = lax.ppermute(own, 'sweep', pairs)  5.2 us
    pallas_call x1, Pallas kernels, backward_and_faces(): pl.pallas_call(kernel, out_shape=(jax.ShapeDtypeStruct(field.shape, F32),...  4.17 us
    pallas_call x1, Pallas kernels, node_sums(): pl.pallas_call(kernel, out_shape=jax.ShapeDtypeStruct((side, LANES), F32)...  2.98 us
    ppermute x4, starting transfers between devices, relay(): other = lax.ppermute(own, 'sweep', pairs)  2.3 us
    pallas_call x1, Pallas kernels, forward_local(): pl.pallas_call(kernel, out_shape=(VMEM(source.shape, F32), jax.ShapeDtype...  1.49 us
  transfers between devices with their start and end apart: 6, of which 3 were waited for; matrix products, arithmetic and copies ran while one was open for 0% of the time, Pallas kernels for 18%

profile of v7, /device:TPU:0, one launch (start us, length us, event | category | flops | bytes accessed | tf_op | source)
XLA Modules:
  0.0 46.7 jit_solution(9449234057260605044)
XLA Ops:
  0.6 0.0 copy-start.8
  0.6 0.0 copy-start
  0.6 1.1 %edge_rows.1 = (f32[160,128]{1,0:T(8,128)S(1)}, f32[160,128]{1,0:T(8,128)S(1)}) custom-call(f32[32,5,16,128]{3,2,1,0:T(8,128)} %psi_ref.1), custom_call_target="tpu_custom_call" | custom-call | flops 10000000000 | bytes 20000000 | tf_op jit(solution)/shard_map/edge_rows/pallas_call | solution.py:91
  1.7 0.0 copy-start.1
  1.8 0.0 copy-start.2
  1.8 0.0 copy-start.3
  1.8 0.8 %collective-permute-start = (f32[160,128]{1,0:T(8,128)S(1)}, f32[160,128]{1,0:T(8,128)S(1)}, u32[]{:S(2)}, u32[]{:S(2)}) collective-permute-start(f32[160,128]{1,0:T(8,128)S(1)} %get-tuple-element.28), channel_id=1, source_target_pairs={{1,2},{2,1},{3,4},{4,3},{5,6},{6,5},{9,10},{10,9},{11,12},{12,11},... | collective-permute-start | bytes 245768 | tf_op jit(solution)/shard_map/ppermute | solution.py:538
  2.6 6.1 %collective-permute-start.1 = (f32[160,128]{1,0:T(8,128)S(1)}, f32[160,128]{1,0:T(8,128)S(1)}, u32[]{:S(2)}, u32[]{:S(2)}) collective-permute-start(f32[160,128]{1,0:T(8,128)S(1)} %get-tuple-element.29), channel_id=1, source_target_pairs={{0,1},{1,0},{2,3},{3,2},{4,5},{5,4},{6,7},{7,6},{8,9},{9,8},{10,11... | collective-permute-start | bytes 245768 | tf_op jit(solution)/shard_map/ppermute | solution.py:539
  8.6 0.0 copy-done.8
  8.6 0.0 copy-done
  8.7 3.9 %forward_matrices.1 = (f32[32,5,5,16,128]{4,3,2,1,0:T(8,128)S(1)}, f32[5,5,16,128]{3,2,1,0:T(8,128)S(1)}) custom-call(f32[32,5,5,16,128]{4,3,2,1,0:T(8,128)S(1)} %copy-done.8, f32[32,5,5,16,128]{4,3,2,1,0:T(8,128)S(1)} %copy-done), custom_call_target="tpu_custom_call" | custom-call | flops 5000000000 | bytes 20000000 | tf_op jit(solution)/shard_map/forward_matrices/pallas_call | solution.py:161
  12.6 0.0 collective-permute-done.second_ref
  12.6 0.0 collective-permute-done.1.first_ref
  12.6 0.0 copy-done.1
  12.6 0.0 copy-done.2
  12.6 0.0 copy-done.3
  12.7 0.0 copy-start.9
  12.7 1.5 %forward_local.1 = (f32[32,5,16,128]{3,2,1,0:T(8,128)S(1)}, f32[6,5,16,128]{3,2,1,0:T(8,128)S(1)}) custom-call(f32[32,5,16,128]{3,2,1,0:T(8,128)S(1)} %copy-done.1, f32[32,5,16,128]{3,2,1,0:T(8,128)S(1)} %copy-done.2, f32[32,2,16,128]{3,2,1,0:T(8,128)S(1)} %copy-done.3, f32[160,128]{1,0:T(8,128)S(1)} %collective-permute-done.second_ref, ...), custom_call_target="tpu_custom_call" | custom-call | tf_op jit(solution)/shard_map/forward_local/pallas_call | solution.py:136
  14.2 0.1 collective-permute-start.2
  14.2 1.5 %collective-permute-done.2.refs_1_ = f32[6,5,16,128]{3,2,1,0:T(8,128)S(1)} collective-permute-done((f32[6,5,16,128]{3,2,1,0:T(8,128)S(1)}, f32[6,5,16,128]{3,2,1,0:T(8,128)S(1)}, u32[]{:S(2)}, u32[]{:S(2)}) %collective-permute-start.2) | collective-permute-done | bytes 245792 | tf_op jit(solution)/shard_map/ppermute | solution.py:524
  15.7 0.1 join.2
  15.8 1.6 %collective-permute-start.3 = (f32[5,16,128]{2,1,0:T(8,128)S(1)}, f32[5,16,128]{2,1,0:T(8,128)S(1)}, u32[]{:S(2)}, u32[]{:S(2)}) collective-permute-start(f32[5,16,128]{2,1,0:T(8,128)S(1)} %get-tuple-element.37), channel_id=1, source_target_pairs={{0,16},{8,24},{16,0},{24,8},{1,17},{9,25},{17,1},{25,9},{2,18},{10... | collective-permute-start | bytes 122888 | tf_op jit(solution)/shard_map/ppermute | solution.py:524
  17.3 0.0 copy-done.9
  17.4 4.0 %backward_matrices.1 = (f32[32,5,5,16,128]{4,3,2,1,0:T(8,128)S(1)}, f32[5,5,16,128]{3,2,1,0:T(8,128)S(1)}) custom-call(f32[32,5,5,16,128]{4,3,2,1,0:T(8,128)S(1)} %copy-done.9, f32[32,5,5,16,128]{4,3,2,1,0:T(8,128)S(1)} %copy-done), custom_call_target="tpu_custom_call" | custom-call | flops 5000000000 | bytes 20000000 | tf_op jit(solution)/shard_map/backward_matrices/pallas_call | solution.py:161
  21.3 0.0 collective-permute-done.3.other_ref
  21.3 0.0 copy-start.6
  21.3 0.0 copy-start.7
  21.3 0.0 copy-start.4
  21.4 0.0 copy-start.5
  21.4 1.1 %forward_then_back.1 = (f32[32,5,16,128]{3,2,1,0:T(8,128)S(1)}, f32[6,5,16,128]{3,2,1,0:T(8,128)S(1)}) custom-call(f32[32,5,16,128]{3,2,1,0:T(8,128)S(1)} %get-tuple-element.33.scaled_ref, f32[5,16,128]{2,1,0:T(8,128)S(1)} %get-tuple-element.35.near_ref, f32[5,5,16,128]{3,2,1,0:T(8,128)S(1)} %get-tuple-element.36.reach_ref, ...), custom_call_target="tpu_custom_call" | custom-call | tf_op jit(solution)/shard_map/forward_then_back/pallas_call | solution.py:202
  22.5 0.1 collective-permute-start.4
  22.6 1.5 %collective-permute-done.4.refs_1_ = f32[6,5,16,128]{3,2,1,0:T(8,128)S(1)} collective-permute-done((f32[6,5,16,128]{3,2,1,0:T(8,128)S(1)}, f32[6,5,16,128]{3,2,1,0:T(8,128)S(1)}, u32[]{:S(2)}, u32[]{:S(2)}) %collective-permute-start.4) | collective-permute-done | bytes 245792 | tf_op jit(solution)/shard_map/ppermute | solution.py:524
  24.1 0.6 %collective-permute-start.5 = (f32[5,16,128]{2,1,0:T(8,128)S(1)}, f32[5,16,128]{2,1,0:T(8,128)S(1)}, u32[]{:S(2)}, u32[]{:S(2)}) collective-permute-start(f32[5,16,128]{2,1,0:T(8,128)S(1)} %get-tuple-element.45), channel_id=1, source_target_pairs={{0,16},{8,24},{16,0},{24,8},{1,17},{9,25},{17,1},{25,9},{2,18},{10... | collective-permute-start | bytes 122888 | tf_op jit(solution)/shard_map/ppermute | solution.py:524
  25.4 0.0 copy-done.6
  25.4 0.0 copy-done.7
  25.4 0.6 %face_slots.1 = (s32[16,128]{1,0:T(8,128)S(1)}, f32[32,128]{1,0:T(8,128)S(1)}) custom-call(s32[16,128]{1,0:T(8,128)S(1)} %bitcast.5, s32[16,128]{1,0:T(8,128)S(1)} %bitcast.6), custom_call_target="tpu_custom_call" | custom-call | flops 4000000 | bytes 10000000 | tf_op jit(solution)/shard_map/face_slots/pallas_call | solution.py:243
  26.0 2.2 %collective-permute-done.5.other_ref = f32[5,16,128]{2,1,0:T(8,128)S(1)} collective-permute-done((f32[5,16,128]{2,1,0:T(8,128)S(1)}, f32[5,16,128]{2,1,0:T(8,128)S(1)}, u32[]{:S(2)}, u32[]{:S(2)}) %collective-permute-start.5) | collective-permute-done | bytes 40992 | tf_op jit(solution)/shard_map/ppermute | solution.py:524
  28.2 0.0 copy-done.4
  28.2 0.0 copy-done.5
  28.2 4.2 %backward_and_faces.1 = (f32[32,5,16,128]{3,2,1,0:T(8,128)}, f32[32,8,128]{2,1,0:T(8,128)S(1)}) custom-call(s32[1]{0:T(128)S(6)} %copy.13.count_ref, f32[32,5,16,128]{3,2,1,0:T(8,128)S(1)} %get-tuple-element.41.field_ref, f32[5,16,128]{2,1,0:T(8,128)S(1)} %get-tuple-element.43.near_ref, f32[5,5,16,128]{3,2,1,0:T(8,128)S(1)} %get-tuple-element.44.reach_ref, ...), custom_call_target="tpu_custom_call" | custom-call | tf_op jit(solution)/shard_map/backward_and_faces/pallas_call | solution.py:367
  32.4 11.3 %all_to_all.5.got_ref = f32[32,8,128]{2,1,0:T(8,128)S(1)} all-to-all(f32[32,8,128]{2,1,0:T(8,128)S(1)} %get-tuple-element.49), channel_id=1, replica_groups=mesh['sweep'=4,'bulk'=8] {'sweep','bulk'}, dimensions={0} | all-to-all | bytes 262144 | tf_op jit(solution)/shard_map/all_to_all | solution.py:554
  43.7 3.0 %node_sums.1 = f32[128,128]{1,0:T(8,128)} custom-call(f32[32,8,128]{2,1,0:T(8,128)S(1)} %all_to_all.5.got_ref), custom_call_target="tpu_custom_call" | custom-call | tf_op jit(solution)/shard_map/node_sums/pallas_call | solution.py:423
  (1 shorter events, 0.0 us)
Async XLA Ops:
  0.6 8.0 %copy-start.8 = (f32[32,5,5,16,128]{4,3,2,1,0:T(8,128)S(1)}, f32[32,5,5,16,128]{4,3,2,1,0:T(8,128)}, u32[]{:S(2)}) copy-start(f32[32,5,5,16,128]{4,3,2,1,0:T(8,128)} %coupled_ref) | copy-start | bytes 19660804
  0.6 8.0 %copy-start = (f32[32,5,5,16,128]{4,3,2,1,0:T(8,128)S(1)}, f32[32,5,5,16,128]{4,3,2,1,0:T(8,128)}, u32[]{:S(2)}) copy-start(f32[32,5,5,16,128]{4,3,2,1,0:T(8,128)} %inv_ref.5) | copy-start | bytes 19660804
  1.7 10.9 %copy-start.1 = (f32[32,5,16,128]{3,2,1,0:T(8,128)S(1)}, f32[32,5,16,128]{3,2,1,0:T(8,128)}, u32[]{:S(2)}) copy-start(f32[32,5,16,128]{3,2,1,0:T(8,128)} %source_ref.1) | copy-start | bytes 3932164
  1.8 10.9 %copy-start.2 = (f32[32,5,16,128]{3,2,1,0:T(8,128)S(1)}, f32[32,5,16,128]{3,2,1,0:T(8,128)}, u32[]{:S(2)}) copy-start(f32[32,5,16,128]{3,2,1,0:T(8,128)} %psi_ref.1) | copy-start | bytes 3932164
  1.8 10.9 %copy-start.3 = (f32[32,2,16,128]{3,2,1,0:T(8,128)S(1)}, f32[32,2,16,128]{3,2,1,0:T(8,128)}, u32[]{:S(2)}) copy-start(f32[32,2,16,128]{3,2,1,0:T(8,128)} %lateral_ref.1) | copy-start | bytes 1572868
  1.8 10.8 %collective-permute-start = (f32[160,128]{1,0:T(8,128)S(1)}, f32[160,128]{1,0:T(8,128)S(1)}, u32[]{:S(2)}, u32[]{:S(2)}) collective-permute-start(f32[160,128]{1,0:T(8,128)S(1)} %get-tuple-element.28), channel_id=1, source_target_pairs={{1,2},{2,1},{3,4},{4,3},{5,6},{6,5},{9,10},{10,9},{11,12},{12,11},... | collective-permute-start | bytes 245768 | tf_op jit(solution)/shard_map/ppermute | solution.py:538
  2.6 10.0 %collective-permute-start.1 = (f32[160,128]{1,0:T(8,128)S(1)}, f32[160,128]{1,0:T(8,128)S(1)}, u32[]{:S(2)}, u32[]{:S(2)}) collective-permute-start(f32[160,128]{1,0:T(8,128)S(1)} %get-tuple-element.29), channel_id=1, source_target_pairs={{0,1},{1,0},{2,3},{3,2},{4,5},{5,4},{6,7},{7,6},{8,9},{9,8},{10,11... | collective-permute-start | bytes 245768 | tf_op jit(solution)/shard_map/ppermute | solution.py:539
  12.7 4.7 %copy-start.9 = (f32[32,5,5,16,128]{4,3,2,1,0:T(8,128)S(1)}, f32[32,5,5,16,128]{4,3,2,1,0:T(8,128)}, u32[]{:S(2)}) copy-start(f32[32,5,5,16,128]{4,3,2,1,0:T(8,128)} %coupled_ref.1) | copy-start | bytes 19660804
  14.2 1.6 %collective-permute-start.2 = (f32[6,5,16,128]{3,2,1,0:T(8,128)S(1)}, f32[6,5,16,128]{3,2,1,0:T(8,128)S(1)}, u32[]{:S(2)}, u32[]{:S(2)}) collective-permute-start(f32[6,5,16,128]{3,2,1,0:T(8,128)S(1)} %get-tuple-element.34.refs_0_), channel_id=1, source_target_pairs={{0,8},{8,0},{16,24},{24,16},{1,9},{9,1},{17,25},{25,17},{2,10},{10... | collective-permute-start | bytes 737288 | tf_op jit(solution)/shard_map/ppermute | solution.py:524
  15.8 5.5 %collective-permute-start.3 = (f32[5,16,128]{2,1,0:T(8,128)S(1)}, f32[5,16,128]{2,1,0:T(8,128)S(1)}, u32[]{:S(2)}, u32[]{:S(2)}) collective-permute-start(f32[5,16,128]{2,1,0:T(8,128)S(1)} %get-tuple-element.37), channel_id=1, source_target_pairs={{0,16},{8,24},{16,0},{24,8},{1,17},{9,25},{17,1},{25,9},{2,18},{10... | collective-permute-start | bytes 122888 | tf_op jit(solution)/shard_map/ppermute | solution.py:524
  21.3 4.0 %copy-start.6 = (s32[2048,1]{0,1:T(1,128)S(1)}, s32[2048,1]{0,1:T(1,128)}, u32[]{:S(2)}) copy-start(s32[2048,1]{0,1:T(1,128)} %param.19) | copy-start | bytes 24580
  21.3 4.0 %copy-start.7 = (s32[2048]{0:T(1024)S(1)}, s32[2048]{0:T(1024)}, u32[]{:S(2)}) copy-start(s32[2048]{0:T(1024)} %param.20) | copy-start | bytes 24580
  21.3 6.8 %copy-start.4 = (f32[5,2048]{1,0:T(8,128)S(1)}, f32[5,2048]{1,0:T(8,128)}, u32[]{:S(2)}) copy-start(f32[5,2048]{1,0:T(8,128)} %weight_ref.1) | copy-start | bytes 122884
  21.4 6.8 %copy-start.5 = (s32[2048]{0:T(1024)S(1)}, s32[2048]{0:T(1024)}, u32[]{:S(2)}) copy-start(s32[2048]{0:T(1024)} %param.18) | copy-start | bytes 24580
  22.5 1.6 %collective-permute-start.4 = (f32[6,5,16,128]{3,2,1,0:T(8,128)S(1)}, f32[6,5,16,128]{3,2,1,0:T(8,128)S(1)}, u32[]{:S(2)}, u32[]{:S(2)}) collective-permute-start(f32[6,5,16,128]{3,2,1,0:T(8,128)S(1)} %get-tuple-element.42.refs_0_), channel_id=1, source_target_pairs={{0,8},{8,0},{16,24},{24,16},{1,9},{9,1},{17,25},{25,17},{2,10},{10... | collective-permute-start | bytes 737288 | tf_op jit(solution)/shard_map/ppermute | solution.py:524
  24.1 4.1 %collective-permute-start.5 = (f32[5,16,128]{2,1,0:T(8,128)S(1)}, f32[5,16,128]{2,1,0:T(8,128)S(1)}, u32[]{:S(2)}, u32[]{:S(2)}) collective-permute-start(f32[5,16,128]{2,1,0:T(8,128)S(1)} %get-tuple-element.45), channel_id=1, source_target_pairs={{0,16},{8,24},{16,0},{24,8},{1,17},{9,25},{17,1},{25,9},{2,18},{10... | collective-permute-start | bytes 122888 | tf_op jit(solution)/shard_map/ppermute | solution.py:524

commit v8 on v7

--- a/solution.py
+++ b/solution.py
@@ -143,30 +143,68 @@
     )(*[in_vmem(v) for v in (source, psi, lateral, second, first, ratio, inv, total)])
 
 
-def matrices(coupled, inv, backward, name):
+def some_ratios(coupled, inv, count):
     planes, width = coupled.shape[0], coupled.shape[3]
 
-    def kernel(coupled_ref, inv_ref, ratio_ref, total_ref):
+    def kernel(coupled_ref, inv_ref, ratio_ref):
+        def body(t, carry):
+            at = planes - 1 - t
+            for rows in halves(width):
+                ratio = ratio_of(coupled_ref, inv_ref, at, rows)
+                for c in range(5):
+                    for x in range(5):
+                        ratio_ref[at, c, x, rows, :] = ratio[c][x]
+            return carry
+
+        lax.fori_loop(0, count, body, 0, unroll=2)
+
+    return pl.pallas_call(
+        kernel,
+        out_shape=VMEM(coupled.shape, F32),
+        in_specs=vmem_specs(2),
+        out_specs=pl.BlockSpec(memory_space=VMEM),
+        compiler_params=pltpu.CompilerParams(vmem_limit_bytes=4 << 20),
+        cost_estimate=pl.CostEstimate(flops=100_000_000, bytes_accessed=8_000, transcendentals=0),
+        name="some_ratios",
+    )(in_vmem(coupled), in_vmem(inv))
+
+
+def matrices(coupled, inv, backward, name, started=None, count=0):
+    planes, width = coupled.shape[0], coupled.shape[3]
+
+    def kernel(coupled_ref, inv_ref, *refs):
+        ratio_ref, total_ref = refs[-2:]
         set_identity(total_ref, planes)
 
-        def body(t, carry):
+        def body(t, carry, known):
             at = planes - 1 - t if backward else t
             for rows in halves(width):
-                ratio = ratio_of(coupled_ref, inv_ref, at, rows)
-                keep_matrices(ratio, next_total(ratio, total_ref, rows), ratio_ref, total_ref, at, rows)
+                if known:
+                    ratio = block(ratio_ref, at, rows)
+                    total = next_total(ratio, total_ref, rows)
+                    for c in range(5):
+                        for x in range(5):
+                            total_ref[c, x, rows, :] = total[c][x]
+                else:
+                    ratio = ratio_of(coupled_ref, inv_ref, at, rows)
+                    keep_matrices(ratio, next_total(ratio, total_ref, rows), ratio_ref, total_ref, at, rows)
             return carry
 
-        lax.fori_loop(0, planes, body, 0, unroll=2)
-
+        if count:
+            lax.fori_loop(0, count, lambda t, carry: body(t, carry, True), 0, unroll=2)
+        lax.fori_loop(count, planes, lambda t, carry: body(t, carry, False), 0, unroll=2)
+
+    operands = [coupled, inv] + ([] if started is None else [started])
     return pl.pallas_call(
         kernel,
         out_shape=(VMEM(coupled.shape, F32), jax.ShapeDtypeStruct(coupled.shape[1:], F32)),
-        in_specs=vmem_specs(2),
+        in_specs=vmem_specs(len(operands)),
         out_specs=tuple(vmem_specs(2)),
+        input_output_aliases={} if started is None else {2: 0},
         compiler_params=pltpu.CompilerParams(vmem_limit_bytes=4 << 20),
         cost_estimate=pl.CostEstimate(flops=5_000_000_000, bytes_accessed=20_000_000, transcendentals=0),
         name=name,
-    )(in_vmem(coupled), in_vmem(inv))
+    )(*[in_vmem(v) for v in operands])
 
 
 def forward_then_back(scaled, arriving, ratio, back_ratio, back_total):
@@ -534,15 +572,19 @@
     low_pairs = [(i, i ^ 1) for i in range(bulk) if i ^ 1 < bulk]
     high_pairs = [(i, j) for i in range(bulk) for j in [i + 1 if i % 2 else i - 1] if 0 <= j < bulk]
     low_edge, high_edge = edge_rows(psi_old)
-    low_edge, high_edge, lower_jac = lax.optimization_barrier((low_edge, high_edge, lower_jac))
+    low_edge, high_edge, lower_jac, upper_jac = lax.optimization_barrier(
+        (low_edge, high_edge, lower_jac, upper_jac))
     second = lax.ppermute(high_edge, "bulk", high_pairs)
     first = lax.ppermute(low_edge, "bulk", low_pairs)
 
     ratio, total = matrices(lower_jac, diag_inv, False, "forward_matrices")
+    count = 14 * upper_jac.shape[0] // 32
+    started = some_ratios(upper_jac, diag_inv, count)
+    ratio, started = lax.optimization_barrier((ratio, started))
     scaled, own = forward_local(source, psi_old, lateral, second, first, ratio, diag_inv, total)
     arriving, joined = relay(own, False)
-    upper_jac, joined = lax.optimization_barrier((upper_jac, joined))
-    back_ratio, back_total = matrices(upper_jac, diag_inv, True, "backward_matrices")
+    started, joined = lax.optimization_barrier((started, joined))
+    back_ratio, back_total = matrices(upper_jac, diag_inv, True, "backward_matrices", started, count)
     field, own = forward_then_back(scaled, arriving, ratio, back_ratio, back_total)
     arriving, _ = relay(own, True)
 

time: 46.9 us -> 48.1 us (1.026)
  local copies, waits for them, and re-layouts: 0.06 us -> 0.93 us
    pallas_call x0 -> x1, Pallas kernels: none -> 0.89 us  [some_ratios(): pl.pallas_call(kernel, out_shape=VMEM(coupled.shape, F32), in_specs=vmem_...]
    unnamed x20 -> x22, local copies, waits for them, and re-layouts: 0.06 us -> 0.93 us
    pallas_call x2, Pallas kernels: 7.9 us -> 7.19 us  [matrices(): pl.pallas_call(kernel, out_shape=(VMEM(coupled.shape, F32), jax.ShapeDtyp...]
where the time goes in v8:
time: 48.1 us; the launch traced here: 47.9 us
  Pallas kernels  19.5 us (41%)
  blocking collectives  11.6 us (24%)
  starting transfers between devices  9.45 us (20%)
  waiting for transfers between devices  4.91 us (10%)
  between operations  1.52 us (3%)
  local copies, waits for them, and re-layouts  0.93 us (2%)
    all_to_all x1, blocking collectives, per_device(): got = lax.all_to_all(send, ('sweep', 'bulk'), 0, 0, tiled=True)  11.6 us
    pallas_call x2, Pallas kernels, matrices(): pl.pallas_call(kernel, out_shape=(VMEM(coupled.shape, F32), jax.ShapeDtyp...  7.19 us
    ppermute x1, starting transfers between devices, per_device(): first = lax.ppermute(low_edge, 'bulk', low_pairs)  6.06 us
    ppermute x4, waiting for transfers between devices, relay(): other = lax.ppermute(own, 'sweep', pairs)  4.91 us
    pallas_call x1, Pallas kernels, backward_and_faces(): pl.pallas_call(kernel, out_shape=(jax.ShapeDtypeStruct(field.shape, F32),...  4.17 us
    pallas_call x1, Pallas kernels, node_sums(): pl.pallas_call(kernel, out_shape=jax.ShapeDtypeStruct((side, LANES), F32)...  2.98 us
    ppermute x4, starting transfers between devices, relay(): other = lax.ppermute(own, 'sweep', pairs)  2.59 us
    pallas_call x1, Pallas kernels, forward_local(): pl.pallas_call(kernel, out_shape=(VMEM(source.shape, F32), jax.ShapeDtype...  1.48 us
  transfers between devices with their start and end apart: 6, of which 3 were waited for; matrix products, arithmetic and copies ran while one was open for 0% of the time, Pallas kernels for 18%

profile of v8, /device:TPU:0, one launch (start us, length us, event | category | flops | bytes accessed | tf_op | source)
XLA Modules:
  0.0 47.9 jit_solution(11754441307367325567)
XLA Ops:
  0.6 0.0 copy-start.8
  0.6 0.0 copy-start
  0.6 1.1 %edge_rows.1 = (f32[160,128]{1,0:T(8,128)S(1)}, f32[160,128]{1,0:T(8,128)S(1)}) custom-call(f32[32,5,16,128]{3,2,1,0:T(8,128)} %psi_ref.1), custom_call_target="tpu_custom_call" | custom-call | flops 10000000000 | bytes 20000000 | tf_op jit(solution)/shard_map/edge_rows/pallas_call | solution.py:91
  1.7 0.0 slice-start
  1.8 0.0 slice-start.1
  1.8 0.8 %collective-permute-start = (f32[160,128]{1,0:T(8,128)S(1)}, f32[160,128]{1,0:T(8,128)S(1)}, u32[]{:S(2)}, u32[]{:S(2)}) collective-permute-start(f32[160,128]{1,0:T(8,128)S(1)} %get-tuple-element.31), channel_id=1, source_target_pairs={{1,2},{2,1},{3,4},{4,3},{5,6},{6,5},{9,10},{10,9},{11,12},{12,11},... | collective-permute-start | bytes 245768 | tf_op jit(solution)/shard_map/ppermute | solution.py:577
  2.6 6.1 %collective-permute-start.1 = (f32[160,128]{1,0:T(8,128)S(1)}, f32[160,128]{1,0:T(8,128)S(1)}, u32[]{:S(2)}, u32[]{:S(2)}) collective-permute-start(f32[160,128]{1,0:T(8,128)S(1)} %get-tuple-element.32), channel_id=1, source_target_pairs={{0,1},{1,0},{2,3},{3,2},{4,5},{5,4},{6,7},{7,6},{8,9},{9,8},{10,11... | collective-permute-start | bytes 245768 | tf_op jit(solution)/shard_map/ppermute | solution.py:578
  8.6 0.0 copy-done.8
  8.6 0.0 copy-done
  8.6 4.1 %forward_matrices.1 = (f32[32,5,5,16,128]{4,3,2,1,0:T(8,128)S(1)}, f32[5,5,16,128]{3,2,1,0:T(8,128)S(1)}) custom-call(f32[32,5,5,16,128]{4,3,2,1,0:T(8,128)S(1)} %copy-done.8, f32[32,5,5,16,128]{4,3,2,1,0:T(8,128)S(1)} %copy-done), custom_call_target="tpu_custom_call" | custom-call | flops 5000000000 | bytes 20000000 | tf_op jit(solution)/shard_map/forward_matrices/pallas_call | solution.py:198
  12.7 0.0 slice-done
  12.7 0.0 slice-done.1
  12.7 0.0 copy-start.1
  12.8 0.0 copy-start.2
  12.8 0.0 copy-start.3
  12.8 0.9 %some_ratios.1.refs_0_ = f32[32,5,5,16,128]{4,3,2,1,0:T(8,128)S(1)} custom-call(f32[32,5,5,16,128]{4,3,2,1,0:T(8,128)S(1)} %bitcast.5, f32[32,5,5,16,128]{4,3,2,1,0:T(8,128)S(1)} %copy-done), custom_call_target="tpu_custom_call" | custom-call | flops 100000000 | bytes 8000 | tf_op jit(solution)/shard_map/some_ratios/pallas_call | solution.py:161
  13.7 0.0 collective-permute-done.second_ref
  13.7 0.0 collective-permute-done.1.first_ref
  13.7 0.4 copy-done.1
  14.1 0.4 copy-done.2
  14.5 0.1 copy-done.3
  14.6 1.5 %forward_local.1 = (f32[32,5,16,128]{3,2,1,0:T(8,128)S(1)}, f32[6,5,16,128]{3,2,1,0:T(8,128)S(1)}) custom-call(f32[32,5,16,128]{3,2,1,0:T(8,128)S(1)} %copy-done.1, f32[32,5,16,128]{3,2,1,0:T(8,128)S(1)} %copy-done.2, f32[32,2,16,128]{3,2,1,0:T(8,128)S(1)} %copy-done.3, f32[160,128]{1,0:T(8,128)S(1)} %collective-permute-done.second_ref, ...), custom_call_target="tpu_custom_call" | custom-call | tf_op jit(solution)/shard_map/forward_local/pallas_call | solution.py:136
  16.1 0.1 collective-permute-start.2
  16.1 1.5 %collective-permute-done.2.refs_1_ = f32[6,5,16,128]{3,2,1,0:T(8,128)S(1)} collective-permute-done((f32[6,5,16,128]{3,2,1,0:T(8,128)S(1)}, f32[6,5,16,128]{3,2,1,0:T(8,128)S(1)}, u32[]{:S(2)}, u32[]{:S(2)}) %collective-permute-start.2) | collective-permute-done | bytes 245792 | tf_op jit(solution)/shard_map/ppermute | solution.py:562
  17.6 0.1 join.2
  17.7 1.6 %collective-permute-start.3 = (f32[5,16,128]{2,1,0:T(8,128)S(1)}, f32[5,16,128]{2,1,0:T(8,128)S(1)}, u32[]{:S(2)}, u32[]{:S(2)}) collective-permute-start(f32[5,16,128]{2,1,0:T(8,128)S(1)} %get-tuple-element.42), channel_id=1, source_target_pairs={{0,16},{8,24},{16,0},{24,8},{1,17},{9,25},{17,1},{25,9},{2,18},{10... | collective-permute-start | bytes 122888 | tf_op jit(solution)/shard_map/ppermute | solution.py:562
  19.2 3.1 %backward_matrices.1 = (f32[32,5,5,16,128]{4,3,2,1,0:T(8,128)S(1)}, f32[5,5,16,128]{3,2,1,0:T(8,128)S(1)}) custom-call(f32[32,5,5,16,128]{4,3,2,1,0:T(8,128)S(1)} %bitcast.5, f32[32,5,5,16,128]{4,3,2,1,0:T(8,128)S(1)} %copy-done, f32[32,5,5,16,128]{4,3,2,1,0:T(8,128)S(1)} %some_ratios.1.refs_0_), custom_call_target="tpu_custom_call", output_to_operand_aliasing={{0}: (2, {})} | custom-call | flops 5000000000 | bytes 20000000 | tf_op jit(solution)/shard_map/backward_matrices/pallas_call | solution.py:198
  22.4 0.0 collective-permute-done.3.other_ref
  22.4 0.0 copy-start.6
  22.4 0.0 copy-start.7
  22.4 0.0 copy-start.4
  22.4 0.0 copy-start.5
  22.4 1.0 %forward_then_back.1 = (f32[32,5,16,128]{3,2,1,0:T(8,128)S(1)}, f32[6,5,16,128]{3,2,1,0:T(8,128)S(1)}) custom-call(f32[32,5,16,128]{3,2,1,0:T(8,128)S(1)} %get-tuple-element.38.scaled_ref, f32[5,16,128]{2,1,0:T(8,128)S(1)} %get-tuple-element.40.near_ref, f32[5,5,16,128]{3,2,1,0:T(8,128)S(1)} %get-tuple-element.41.reach_ref, ...), custom_call_target="tpu_custom_call" | custom-call | tf_op jit(solution)/shard_map/forward_then_back/pallas_call | solution.py:240
  23.5 0.1 collective-permute-start.4
  23.6 1.5 %collective-permute-done.4.refs_1_ = f32[6,5,16,128]{3,2,1,0:T(8,128)S(1)} collective-permute-done((f32[6,5,16,128]{3,2,1,0:T(8,128)S(1)}, f32[6,5,16,128]{3,2,1,0:T(8,128)S(1)}, u32[]{:S(2)}, u32[]{:S(2)}) %collective-permute-start.4) | collective-permute-done | bytes 245792 | tf_op jit(solution)/shard_map/ppermute | solution.py:562
  25.1 0.9 %collective-permute-start.5 = (f32[5,16,128]{2,1,0:T(8,128)S(1)}, f32[5,16,128]{2,1,0:T(8,128)S(1)}, u32[]{:S(2)}, u32[]{:S(2)}) collective-permute-start(f32[5,16,128]{2,1,0:T(8,128)S(1)} %get-tuple-element.51), channel_id=1, source_target_pairs={{0,16},{8,24},{16,0},{24,8},{1,17},{9,25},{17,1},{25,9},{2,18},{10... | collective-permute-start | bytes 122888 | tf_op jit(solution)/shard_map/ppermute | solution.py:562
  26.7 0.0 copy-done.6
  26.7 0.0 copy-done.7
  26.7 0.6 %face_slots.1 = (s32[16,128]{1,0:T(8,128)S(1)}, f32[32,128]{1,0:T(8,128)S(1)}) custom-call(s32[16,128]{1,0:T(8,128)S(1)} %bitcast.7, s32[16,128]{1,0:T(8,128)S(1)} %bitcast.8), custom_call_target="tpu_custom_call" | custom-call | flops 4000000 | bytes 10000000 | tf_op jit(solution)/shard_map/face_slots/pallas_call | solution.py:281
  27.3 1.9 %collective-permute-done.5.other_ref = f32[5,16,128]{2,1,0:T(8,128)S(1)} collective-permute-done((f32[5,16,128]{2,1,0:T(8,128)S(1)}, f32[5,16,128]{2,1,0:T(8,128)S(1)}, u32[]{:S(2)}, u32[]{:S(2)}) %collective-permute-start.5) | collective-permute-done | bytes 40992 | tf_op jit(solution)/shard_map/ppermute | solution.py:562
  29.2 0.0 copy-done.4
  29.2 0.0 copy-done.5
  29.2 4.2 %backward_and_faces.1 = (f32[32,5,16,128]{3,2,1,0:T(8,128)}, f32[32,8,128]{2,1,0:T(8,128)S(1)}) custom-call(s32[1]{0:T(128)S(6)} %copy.15.count_ref, f32[32,5,16,128]{3,2,1,0:T(8,128)S(1)} %get-tuple-element.47.field_ref, f32[5,16,128]{2,1,0:T(8,128)S(1)} %get-tuple-element.49.near_ref, f32[5,5,16,128]{3,2,1,0:T(8,128)S(1)} %get-tuple-element.50.reach_ref, ...), custom_call_target="tpu_custom_call" | custom-call | tf_op jit(solution)/shard_map/backward_and_faces/pallas_call | solution.py:405
  33.4 11.6 %all_to_all.5.got_ref = f32[32,8,128]{2,1,0:T(8,128)S(1)} all-to-all(f32[32,8,128]{2,1,0:T(8,128)S(1)} %get-tuple-element.55), channel_id=1, replica_groups=mesh['sweep'=4,'bulk'=8] {'sweep','bulk'}, dimensions={0} | all-to-all | bytes 262144 | tf_op jit(solution)/shard_map/all_to_all | solution.py:596
  45.0 3.0 %node_sums.1 = f32[128,128]{1,0:T(8,128)} custom-call(f32[32,8,128]{2,1,0:T(8,128)S(1)} %all_to_all.5.got_ref), custom_call_target="tpu_custom_call" | custom-call | tf_op jit(solution)/shard_map/node_sums/pallas_call | solution.py:461
  (2 shorter events, 0.0 us)
Async XLA Ops:
  0.6 8.0 %copy-start.8 = (f32[32,5,5,16,128]{4,3,2,1,0:T(8,128)S(1)}, f32[32,5,5,16,128]{4,3,2,1,0:T(8,128)}, u32[]{:S(2)}) copy-start(f32[32,5,5,16,128]{4,3,2,1,0:T(8,128)} %coupled_ref) | copy-start | bytes 19660804
  0.6 8.0 %copy-start = (f32[32,5,5,16,128]{4,3,2,1,0:T(8,128)S(1)}, f32[32,5,5,16,128]{4,3,2,1,0:T(8,128)}, u32[]{:S(2)}) copy-start(f32[32,5,5,16,128]{4,3,2,1,0:T(8,128)} %inv_ref.7) | copy-start | bytes 19660804
  1.7 11.0 %slice-start = ((s8[6553600]{0:T(1024)(128)(4,1)}), s8[4194304]{0:T(1024)(128)(4,1)S(1)}, s32[]{:S(2)}) async-start(s8[6553600]{0:T(1024)(128)(4,1)} %bitcast.4), calls=%async_computation.1 | async-start | bytes 8388608
  1.8 11.0 %slice-start.1 = ((s8[6553600]{0:T(1024)(128)(4,1)}), s8[2359296]{0:T(1024)(128)(4,1)S(1)}, s32[]{:S(2)}) async-start(s8[6553600]{0:T(1024)(128)(4,1)} %bitcast.4), calls=%async_computation.2 | async-start | bytes 4718592
  1.8 11.9 %collective-permute-start = (f32[160,128]{1,0:T(8,128)S(1)}, f32[160,128]{1,0:T(8,128)S(1)}, u32[]{:S(2)}, u32[]{:S(2)}) collective-permute-start(f32[160,128]{1,0:T(8,128)S(1)} %get-tuple-element.31), channel_id=1, source_target_pairs={{1,2},{2,1},{3,4},{4,3},{5,6},{6,5},{9,10},{10,9},{11,12},{12,11},... | collective-permute-start | bytes 245768 | tf_op jit(solution)/shard_map/ppermute | solution.py:577
  2.6 11.1 %collective-permute-start.1 = (f32[160,128]{1,0:T(8,128)S(1)}, f32[160,128]{1,0:T(8,128)S(1)}, u32[]{:S(2)}, u32[]{:S(2)}) collective-permute-start(f32[160,128]{1,0:T(8,128)S(1)} %get-tuple-element.32), channel_id=1, source_target_pairs={{0,1},{1,0},{2,3},{3,2},{4,5},{5,4},{6,7},{7,6},{8,9},{9,8},{10,11... | collective-permute-start | bytes 245768 | tf_op jit(solution)/shard_map/ppermute | solution.py:578
  12.7 1.3 %copy-start.1 = (f32[32,5,16,128]{3,2,1,0:T(8,128)S(1)}, f32[32,5,16,128]{3,2,1,0:T(8,128)}, u32[]{:S(2)}) copy-start(f32[32,5,16,128]{3,2,1,0:T(8,128)} %source_ref.1) | copy-start | bytes 3932164
  12.8 1.7 %copy-start.2 = (f32[32,5,16,128]{3,2,1,0:T(8,128)S(1)}, f32[32,5,16,128]{3,2,1,0:T(8,128)}, u32[]{:S(2)}) copy-start(f32[32,5,16,128]{3,2,1,0:T(8,128)} %psi_ref.1) | copy-start | bytes 3932164
  12.8 1.8 %copy-start.3 = (f32[32,2,16,128]{3,2,1,0:T(8,128)S(1)}, f32[32,2,16,128]{3,2,1,0:T(8,128)}, u32[]{:S(2)}) copy-start(f32[32,2,16,128]{3,2,1,0:T(8,128)} %lateral_ref.1) | copy-start | bytes 1572868
  16.1 1.6 %collective-permute-start.2 = (f32[6,5,16,128]{3,2,1,0:T(8,128)S(1)}, f32[6,5,16,128]{3,2,1,0:T(8,128)S(1)}, u32[]{:S(2)}, u32[]{:S(2)}) collective-permute-start(f32[6,5,16,128]{3,2,1,0:T(8,128)S(1)} %get-tuple-element.39.refs_0_), channel_id=1, source_target_pairs={{0,8},{8,0},{16,24},{24,16},{1,9},{9,1},{17,25},{25,17},{2,10},{10... | collective-permute-start | bytes 737288 | tf_op jit(solution)/shard_map/ppermute | solution.py:562
  17.7 4.7 %collective-permute-start.3 = (f32[5,16,128]{2,1,0:T(8,128)S(1)}, f32[5,16,128]{2,1,0:T(8,128)S(1)}, u32[]{:S(2)}, u32[]{:S(2)}) collective-permute-start(f32[5,16,128]{2,1,0:T(8,128)S(1)} %get-tuple-element.42), channel_id=1, source_target_pairs={{0,16},{8,24},{16,0},{24,8},{1,17},{9,25},{17,1},{25,9},{2,18},{10... | collective-permute-start | bytes 122888 | tf_op jit(solution)/shard_map/ppermute | solution.py:562
  22.4 4.3 %copy-start.6 = (s32[2048,1]{0,1:T(1,128)S(1)}, s32[2048,1]{0,1:T(1,128)}, u32[]{:S(2)}) copy-start(s32[2048,1]{0,1:T(1,128)} %param.19) | copy-start | bytes 24580
  22.4 4.3 %copy-start.7 = (s32[2048]{0:T(1024)S(1)}, s32[2048]{0:T(1024)}, u32[]{:S(2)}) copy-start(s32[2048]{0:T(1024)} %param.20) | copy-start | bytes 24580
  22.4 6.8 %copy-start.4 = (f32[5,2048]{1,0:T(8,128)S(1)}, f32[5,2048]{1,0:T(8,128)}, u32[]{:S(2)}) copy-start(f32[5,2048]{1,0:T(8,128)} %weight_ref.1) | copy-start | bytes 122884
  22.4 6.8 %copy-start.5 = (s32[2048]{0:T(1024)S(1)}, s32[2048]{0:T(1024)}, u32[]{:S(2)}) copy-start(s32[2048]{0:T(1024)} %param.18) | copy-start | bytes 24580
  23.5 1.6 %collective-permute-start.4 = (f32[6,5,16,128]{3,2,1,0:T(8,128)S(1)}, f32[6,5,16,128]{3,2,1,0:T(8,128)S(1)}, u32[]{:S(2)}, u32[]{:S(2)}) collective-permute-start(f32[6,5,16,128]{3,2,1,0:T(8,128)S(1)} %get-tuple-element.48.refs_0_), channel_id=1, source_target_pairs={{0,8},{8,0},{16,24},{24,16},{1,9},{9,1},{17,25},{25,17},{2,10},{10... | collective-permute-start | bytes 737288 | tf_op jit(solution)/shard_map/ppermute | solution.py:562
  25.1 4.1 %collective-permute-start.5 = (f32[5,16,128]{2,1,0:T(8,128)S(1)}, f32[5,16,128]{2,1,0:T(8,128)S(1)}, u32[]{:S(2)}, u32[]{:S(2)}) collective-permute-start(f32[5,16,128]{2,1,0:T(8,128)S(1)} %get-tuple-element.51), channel_id=1, source_target_pairs={{0,16},{8,24},{16,0},{24,8},{1,17},{9,25},{17,1},{25,9},{2,18},{10... | collective-permute-start | bytes 122888 | tf_op jit(solution)/shard_map/ppermute | solution.py:562

commit v9 on v7

--- a/solution.py
+++ b/solution.py
@@ -287,6 +287,7 @@
     face_rows = cell.shape[0]
     bucket_rows = nodes.shape[0]
     rows_each = bucket_rows // owners
+    half = rows_each // 2
     group = 2
     piece = 4
     batch = 8
@@ -357,10 +358,12 @@
         placed = place_in_slots(slot_ref[...], [high, low], bucket_rows)
         values = placed[0] + placed[1]
         for o in range(owners):
-            here = slice(o * rows_each, (o + 1) * rows_each)
-            both = jnp.concatenate([values[here], nodes_ref[here, :]], axis=0)
-            for d in range(o, devices, owners):
-                send_ref[d] = both
+            for core in range(2):
+                start = o * rows_each + core * half
+                here = slice(start, start + half)
+                both = jnp.concatenate([values[here], nodes_ref[here, :]], axis=0)
+                for d in range(core * owners + o, devices, 2 * owners):
+                    send_ref[d] = both
         for k in range(planes // batch):
             write(k).wait()
 
@@ -368,7 +371,7 @@
         kernel,
         out_shape=(
             jax.ShapeDtypeStruct(field.shape, F32),
-            jax.ShapeDtypeStruct((devices, 2 * rows_each, LANES), F32),
+            jax.ShapeDtypeStruct((devices, 2 * half, LANES), F32),
         ),
         in_specs=[pl.BlockSpec(memory_space=pltpu.SMEM)] + vmem_specs(9),
         out_specs=(pl.BlockSpec(memory_space=pltpu.HBM), pl.BlockSpec(memory_space=VMEM)),
@@ -552,7 +555,9 @@
     adjoint, send = backward_and_faces(field, arriving, back_ratio, face_count, face_cell.reshape(rows),
                                        face_weight, slot, nodes, devices, bulk)
     got = lax.all_to_all(send, ("sweep", "bulk"), 0, 0, tiled=True)
-    return adjoint, node_sums(got).reshape(NODES_DEV)
+    mine = node_sums(got)
+    pairs = [(i, i ^ 1) for i in range(lax.axis_size("sweep"))]
+    return adjoint, (mine + lax.ppermute(mine, "sweep", pairs)).reshape(NODES_DEV)
 
 
 def solution(mesh):

time: 46.9 us -> 46.7 us (level)
  Pallas kernels: 19.4 us -> 17.7 us
  waiting for transfers between devices: 5.21 us -> 6.35 us
  other arithmetic: 0 us -> 0.64 us
    pallas_call x1, Pallas kernels: 2.98 us -> 1.26 us  [node_sums(): pl.pallas_call(kernel, out_shape=jax.ShapeDtypeStruct((side, LANES), F32)...]
    ppermute x0 -> x1, waiting for transfers between devices: none -> 1.14 us  [per_device(): lax.ppermute(mine, 'sweep', pairs)]
    reshape x0 -> x1, other arithmetic: none -> 0.64 us  [per_device(): (mine + lax.ppermute(mine, 'sweep', pairs)).reshape(NODES_DEV)]
  transfers between devices with their start and end apart: 6 -> 7, of which waited for: 3 -> 4; matrix products, arithmetic and copies ran while one was open for 0% -> 0% of each run, Pallas kernels for 18% -> 18%
where the time goes in v9:
time: 46.7 us; the launch traced here: 46.5 us
  Pallas kernels  17.7 us (38%)
  blocking collectives  10.9 us (23%)
  starting transfers between devices  9.33 us (20%)
  waiting for transfers between devices  6.35 us (14%)
  between operations  1.52 us (3%)
  other arithmetic  0.64 us (1%)
    all_to_all x1, blocking collectives, per_device(): got = lax.all_to_all(send, ('sweep', 'bulk'), 0, 0, tiled=True)  10.9 us
    pallas_call x2, Pallas kernels, matrices(): pl.pallas_call(kernel, out_shape=(VMEM(coupled.shape, F32), jax.ShapeDtyp...  7.9 us
    ppermute x1, starting transfers between devices, per_device(): first = lax.ppermute(low_edge, 'bulk', low_pairs)  6.06 us
    ppermute x4, waiting for transfers between devices, relay(): other = lax.ppermute(own, 'sweep', pairs)  5.2 us
    pallas_call x1, Pallas kernels, backward_and_faces(): pl.pallas_call(kernel, out_shape=(jax.ShapeDtypeStruct(field.shape, F32),...  4.17 us
    ppermute x4, starting transfers between devices, relay(): other = lax.ppermute(own, 'sweep', pairs)  2.3 us
    pallas_call x1, Pallas kernels, forward_local(): pl.pallas_call(kernel, out_shape=(VMEM(source.shape, F32), jax.ShapeDtype...  1.49 us
    pallas_call x1, Pallas kernels, node_sums(): pl.pallas_call(kernel, out_shape=jax.ShapeDtypeStruct((side, LANES), F32)...  1.26 us
  transfers between devices with their start and end apart: 7, of which 4 were waited for; matrix products, arithmetic and copies ran while one was open for 0% of the time, Pallas kernels for 18%

profile of v9, /device:TPU:0, one launch (start us, length us, event | category | flops | bytes accessed | tf_op | source)
XLA Modules:
  0.0 46.5 jit_solution(4316705934834092359)
XLA Ops:
  0.6 0.0 copy-start.8
  0.6 0.0 copy-start
  0.6 1.1 %edge_rows.1 = (f32[160,128]{1,0:T(8,128)S(1)}, f32[160,128]{1,0:T(8,128)S(1)}) custom-call(f32[32,5,16,128]{3,2,1,0:T(8,128)} %psi_ref.1), custom_call_target="tpu_custom_call" | custom-call | flops 10000000000 | bytes 20000000 | tf_op jit(solution)/shard_map/edge_rows/pallas_call | solution.py:91
  1.7 0.0 copy-start.1
  1.8 0.0 copy-start.2
  1.8 0.0 copy-start.3
  1.8 0.8 %collective-permute-start = (f32[160,128]{1,0:T(8,128)S(1)}, f32[160,128]{1,0:T(8,128)S(1)}, u32[]{:S(2)}, u32[]{:S(2)}) collective-permute-start(f32[160,128]{1,0:T(8,128)S(1)} %get-tuple-element.28), channel_id=1, source_target_pairs={{1,2},{2,1},{3,4},{4,3},{5,6},{6,5},{9,10},{10,9},{11,12},{12,11},... | collective-permute-start | bytes 245768 | tf_op jit(solution)/shard_map/ppermute | solution.py:541
  2.6 6.1 %collective-permute-start.1 = (f32[160,128]{1,0:T(8,128)S(1)}, f32[160,128]{1,0:T(8,128)S(1)}, u32[]{:S(2)}, u32[]{:S(2)}) collective-permute-start(f32[160,128]{1,0:T(8,128)S(1)} %get-tuple-element.29), channel_id=1, source_target_pairs={{0,1},{1,0},{2,3},{3,2},{4,5},{5,4},{6,7},{7,6},{8,9},{9,8},{10,11... | collective-permute-start | bytes 245768 | tf_op jit(solution)/shard_map/ppermute | solution.py:542
  8.6 0.0 copy-done.8
  8.6 0.0 copy-done
  8.7 3.9 %forward_matrices.1 = (f32[32,5,5,16,128]{4,3,2,1,0:T(8,128)S(1)}, f32[5,5,16,128]{3,2,1,0:T(8,128)S(1)}) custom-call(f32[32,5,5,16,128]{4,3,2,1,0:T(8,128)S(1)} %copy-done.8, f32[32,5,5,16,128]{4,3,2,1,0:T(8,128)S(1)} %copy-done), custom_call_target="tpu_custom_call" | custom-call | flops 5000000000 | bytes 20000000 | tf_op jit(solution)/shard_map/forward_matrices/pallas_call | solution.py:161
  12.6 0.0 collective-permute-done.second_ref
  12.6 0.0 collective-permute-done.1.first_ref
  12.6 0.0 copy-done.1
  12.6 0.0 copy-done.2
  12.6 0.0 copy-done.3
  12.7 0.0 copy-start.9
  12.7 1.5 %forward_local.1 = (f32[32,5,16,128]{3,2,1,0:T(8,128)S(1)}, f32[6,5,16,128]{3,2,1,0:T(8,128)S(1)}) custom-call(f32[32,5,16,128]{3,2,1,0:T(8,128)S(1)} %copy-done.1, f32[32,5,16,128]{3,2,1,0:T(8,128)S(1)} %copy-done.2, f32[32,2,16,128]{3,2,1,0:T(8,128)S(1)} %copy-done.3, f32[160,128]{1,0:T(8,128)S(1)} %collective-permute-done.second_ref, ...), custom_call_target="tpu_custom_call" | custom-call | tf_op jit(solution)/shard_map/forward_local/pallas_call | solution.py:136
  14.2 0.1 collective-permute-start.2
  14.2 1.5 %collective-permute-done.2.refs_1_ = f32[6,5,16,128]{3,2,1,0:T(8,128)S(1)} collective-permute-done((f32[6,5,16,128]{3,2,1,0:T(8,128)S(1)}, f32[6,5,16,128]{3,2,1,0:T(8,128)S(1)}, u32[]{:S(2)}, u32[]{:S(2)}) %collective-permute-start.2) | collective-permute-done | bytes 245792 | tf_op jit(solution)/shard_map/ppermute | solution.py:527
  15.7 0.1 join.2
  15.8 1.6 %collective-permute-start.3 = (f32[5,16,128]{2,1,0:T(8,128)S(1)}, f32[5,16,128]{2,1,0:T(8,128)S(1)}, u32[]{:S(2)}, u32[]{:S(2)}) collective-permute-start(f32[5,16,128]{2,1,0:T(8,128)S(1)} %get-tuple-element.37), channel_id=1, source_target_pairs={{0,16},{8,24},{16,0},{24,8},{1,17},{9,25},{17,1},{25,9},{2,18},{10... | collective-permute-start | bytes 122888 | tf_op jit(solution)/shard_map/ppermute | solution.py:527
  17.3 0.0 copy-done.9
  17.4 4.0 %backward_matrices.1 = (f32[32,5,5,16,128]{4,3,2,1,0:T(8,128)S(1)}, f32[5,5,16,128]{3,2,1,0:T(8,128)S(1)}) custom-call(f32[32,5,5,16,128]{4,3,2,1,0:T(8,128)S(1)} %copy-done.9, f32[32,5,5,16,128]{4,3,2,1,0:T(8,128)S(1)} %copy-done), custom_call_target="tpu_custom_call" | custom-call | flops 5000000000 | bytes 20000000 | tf_op jit(solution)/shard_map/backward_matrices/pallas_call | solution.py:161
  21.3 0.0 collective-permute-done.3.other_ref
  21.3 0.0 copy-start.6
  21.3 0.0 copy-start.7
  21.3 0.0 copy-start.4
  21.4 0.0 copy-start.5
  21.4 1.1 %forward_then_back.1 = (f32[32,5,16,128]{3,2,1,0:T(8,128)S(1)}, f32[6,5,16,128]{3,2,1,0:T(8,128)S(1)}) custom-call(f32[32,5,16,128]{3,2,1,0:T(8,128)S(1)} %get-tuple-element.33.scaled_ref, f32[5,16,128]{2,1,0:T(8,128)S(1)} %get-tuple-element.35.near_ref, f32[5,5,16,128]{3,2,1,0:T(8,128)S(1)} %get-tuple-element.36.reach_ref, ...), custom_call_target="tpu_custom_call" | custom-call | tf_op jit(solution)/shard_map/forward_then_back/pallas_call | solution.py:202
  22.5 0.1 collective-permute-start.4
  22.6 1.5 %collective-permute-done.4.refs_1_ = f32[6,5,16,128]{3,2,1,0:T(8,128)S(1)} collective-permute-done((f32[6,5,16,128]{3,2,1,0:T(8,128)S(1)}, f32[6,5,16,128]{3,2,1,0:T(8,128)S(1)}, u32[]{:S(2)}, u32[]{:S(2)}) %collective-permute-start.4) | collective-permute-done | bytes 245792 | tf_op jit(solution)/shard_map/ppermute | solution.py:527
  24.1 0.6 %collective-permute-start.5 = (f32[5,16,128]{2,1,0:T(8,128)S(1)}, f32[5,16,128]{2,1,0:T(8,128)S(1)}, u32[]{:S(2)}, u32[]{:S(2)}) collective-permute-start(f32[5,16,128]{2,1,0:T(8,128)S(1)} %get-tuple-element.45), channel_id=1, source_target_pairs={{0,16},{8,24},{16,0},{24,8},{1,17},{9,25},{17,1},{25,9},{2,18},{10... | collective-permute-start | bytes 122888 | tf_op jit(solution)/shard_map/ppermute | solution.py:527
  25.4 0.0 copy-done.6
  25.4 0.0 copy-done.7
  25.4 0.6 %face_slots.1 = (s32[16,128]{1,0:T(8,128)S(1)}, f32[32,128]{1,0:T(8,128)S(1)}) custom-call(s32[16,128]{1,0:T(8,128)S(1)} %bitcast.6, s32[16,128]{1,0:T(8,128)S(1)} %bitcast.7), custom_call_target="tpu_custom_call" | custom-call | flops 4000000 | bytes 10000000 | tf_op jit(solution)/shard_map/face_slots/pallas_call | solution.py:243
  26.0 2.2 %collective-permute-done.5.other_ref = f32[5,16,128]{2,1,0:T(8,128)S(1)} collective-permute-done((f32[5,16,128]{2,1,0:T(8,128)S(1)}, f32[5,16,128]{2,1,0:T(8,128)S(1)}, u32[]{:S(2)}, u32[]{:S(2)}) %collective-permute-start.5) | collective-permute-done | bytes 40992 | tf_op jit(solution)/shard_map/ppermute | solution.py:527
  28.2 0.0 copy-done.4
  28.2 0.0 copy-done.5
  28.2 4.2 %backward_and_faces.1 = (f32[32,5,16,128]{3,2,1,0:T(8,128)}, f32[32,4,128]{2,1,0:T(4,128)S(1)}) custom-call(s32[1]{0:T(128)S(6)} %copy.13.count_ref, f32[32,5,16,128]{3,2,1,0:T(8,128)S(1)} %get-tuple-element.41.field_ref, f32[5,16,128]{2,1,0:T(8,128)S(1)} %get-tuple-element.43.near_ref, f32[5,5,16,128]{3,2,1,0:T(8,128)S(1)} %get-tuple-element.44.reach_ref, ...), custom_call_target="tpu_custom_call" | custom-call | tf_op jit(solution)/shard_map/backward_and_faces/pallas_call | solution.py:370
  32.4 10.9 %all_to_all.5.got_ref = f32[32,4,128]{2,1,0:T(4,128)S(1)} all-to-all(f32[32,4,128]{2,1,0:T(4,128)S(1)} %get-tuple-element.49), channel_id=1, replica_groups=mesh['sweep'=4,'bulk'=8] {'sweep','bulk'}, dimensions={0} | all-to-all | bytes 131072 | tf_op jit(solution)/shard_map/all_to_all | solution.py:557
  43.2 1.3 %node_sums.1 = f32[128,128]{1,0:T(8,128)S(1)} custom-call(f32[32,4,128]{2,1,0:T(4,128)S(1)} %all_to_all.5.got_ref), custom_call_target="tpu_custom_call" | custom-call | tf_op jit(solution)/shard_map/node_sums/pallas_call | solution.py:426
  44.5 0.2 collective-permute-start.6
  44.7 1.1 %collective-permute-done.6 = f32[128,128]{1,0:T(8,128)S(1)} collective-permute-done((f32[128,128]{1,0:T(8,128)S(1)}, f32[128,128]{1,0:T(8,128)S(1)}, u32[]{:S(2)}, u32[]{:S(2)}) %collective-permute-start.6) | collective-permute-done | bytes 65568 | tf_op jit(solution)/shard_map/ppermute | solution.py:560
  45.8 0.6 %add_bitcast_fusion = f32[16384]{0:T(1024)} fusion(f32[128,128]{1,0:T(8,128)S(1)} %node_sums.1, f32[128,128]{1,0:T(8,128)S(1)} %collective-permute-done.6), kind=kLoop, calls=%fused_computation | loop fusion | flops 16384 | bytes 196608 | tf_op jit(solution)/shard_map/reshape | solution.py:560
  (1 shorter events, 0.0 us)
Async XLA Ops:
  0.6 8.0 %copy-start.8 = (f32[32,5,5,16,128]{4,3,2,1,0:T(8,128)S(1)}, f32[32,5,5,16,128]{4,3,2,1,0:T(8,128)}, u32[]{:S(2)}) copy-start(f32[32,5,5,16,128]{4,3,2,1,0:T(8,128)} %coupled_ref) | copy-start | bytes 19660804
  0.6 8.0 %copy-start = (f32[32,5,5,16,128]{4,3,2,1,0:T(8,128)S(1)}, f32[32,5,5,16,128]{4,3,2,1,0:T(8,128)}, u32[]{:S(2)}) copy-start(f32[32,5,5,16,128]{4,3,2,1,0:T(8,128)} %inv_ref.5) | copy-start | bytes 19660804
  1.7 10.9 %copy-start.1 = (f32[32,5,16,128]{3,2,1,0:T(8,128)S(1)}, f32[32,5,16,128]{3,2,1,0:T(8,128)}, u32[]{:S(2)}) copy-start(f32[32,5,16,128]{3,2,1,0:T(8,128)} %source_ref.1) | copy-start | bytes 3932164
  1.8 10.9 %copy-start.2 = (f32[32,5,16,128]{3,2,1,0:T(8,128)S(1)}, f32[32,5,16,128]{3,2,1,0:T(8,128)}, u32[]{:S(2)}) copy-start(f32[32,5,16,128]{3,2,1,0:T(8,128)} %psi_ref.1) | copy-start | bytes 3932164
  1.8 10.9 %copy-start.3 = (f32[32,2,16,128]{3,2,1,0:T(8,128)S(1)}, f32[32,2,16,128]{3,2,1,0:T(8,128)}, u32[]{:S(2)}) copy-start(f32[32,2,16,128]{3,2,1,0:T(8,128)} %lateral_ref.1) | copy-start | bytes 1572868
  1.8 10.8 %collective-permute-start = (f32[160,128]{1,0:T(8,128)S(1)}, f32[160,128]{1,0:T(8,128)S(1)}, u32[]{:S(2)}, u32[]{:S(2)}) collective-permute-start(f32[160,128]{1,0:T(8,128)S(1)} %get-tuple-element.28), channel_id=1, source_target_pairs={{1,2},{2,1},{3,4},{4,3},{5,6},{6,5},{9,10},{10,9},{11,12},{12,11},... | collective-permute-start | bytes 245768 | tf_op jit(solution)/shard_map/ppermute | solution.py:541
  2.6 10.0 %collective-permute-start.1 = (f32[160,128]{1,0:T(8,128)S(1)}, f32[160,128]{1,0:T(8,128)S(1)}, u32[]{:S(2)}, u32[]{:S(2)}) collective-permute-start(f32[160,128]{1,0:T(8,128)S(1)} %get-tuple-element.29), channel_id=1, source_target_pairs={{0,1},{1,0},{2,3},{3,2},{4,5},{5,4},{6,7},{7,6},{8,9},{9,8},{10,11... | collective-permute-start | bytes 245768 | tf_op jit(solution)/shard_map/ppermute | solution.py:542
  12.7 4.7 %copy-start.9 = (f32[32,5,5,16,128]{4,3,2,1,0:T(8,128)S(1)}, f32[32,5,5,16,128]{4,3,2,1,0:T(8,128)}, u32[]{:S(2)}) copy-start(f32[32,5,5,16,128]{4,3,2,1,0:T(8,128)} %coupled_ref.1) | copy-start | bytes 19660804
  14.2 1.6 %collective-permute-start.2 = (f32[6,5,16,128]{3,2,1,0:T(8,128)S(1)}, f32[6,5,16,128]{3,2,1,0:T(8,128)S(1)}, u32[]{:S(2)}, u32[]{:S(2)}) collective-permute-start(f32[6,5,16,128]{3,2,1,0:T(8,128)S(1)} %get-tuple-element.34.refs_0_), channel_id=1, source_target_pairs={{0,8},{8,0},{16,24},{24,16},{1,9},{9,1},{17,25},{25,17},{2,10},{10... | collective-permute-start | bytes 737288 | tf_op jit(solution)/shard_map/ppermute | solution.py:527
  15.8 5.5 %collective-permute-start.3 = (f32[5,16,128]{2,1,0:T(8,128)S(1)}, f32[5,16,128]{2,1,0:T(8,128)S(1)}, u32[]{:S(2)}, u32[]{:S(2)}) collective-permute-start(f32[5,16,128]{2,1,0:T(8,128)S(1)} %get-tuple-element.37), channel_id=1, source_target_pairs={{0,16},{8,24},{16,0},{24,8},{1,17},{9,25},{17,1},{25,9},{2,18},{10... | collective-permute-start | bytes 122888 | tf_op jit(solution)/shard_map/ppermute | solution.py:527
  21.3 4.0 %copy-start.6 = (s32[2048,1]{0,1:T(1,128)S(1)}, s32[2048,1]{0,1:T(1,128)}, u32[]{:S(2)}) copy-start(s32[2048,1]{0,1:T(1,128)} %param.19) | copy-start | bytes 24580
  21.3 4.0 %copy-start.7 = (s32[2048]{0:T(1024)S(1)}, s32[2048]{0:T(1024)}, u32[]{:S(2)}) copy-start(s32[2048]{0:T(1024)} %param.20) | copy-start | bytes 24580
  21.3 6.8 %copy-start.4 = (f32[5,2048]{1,0:T(8,128)S(1)}, f32[5,2048]{1,0:T(8,128)}, u32[]{:S(2)}) copy-start(f32[5,2048]{1,0:T(8,128)} %weight_ref.1) | copy-start | bytes 122884
  21.4 6.8 %copy-start.5 = (s32[2048]{0:T(1024)S(1)}, s32[2048]{0:T(1024)}, u32[]{:S(2)}) copy-start(s32[2048]{0:T(1024)} %param.18) | copy-start | bytes 24580
  22.5 1.6 %collective-permute-start.4 = (f32[6,5,16,128]{3,2,1,0:T(8,128)S(1)}, f32[6,5,16,128]{3,2,1,0:T(8,128)S(1)}, u32[]{:S(2)}, u32[]{:S(2)}) collective-permute-start(f32[6,5,16,128]{3,2,1,0:T(8,128)S(1)} %get-tuple-element.42.refs_0_), channel_id=1, source_target_pairs={{0,8},{8,0},{16,24},{24,16},{1,9},{9,1},{17,25},{25,17},{2,10},{10... | collective-permute-start | bytes 737288 | tf_op jit(solution)/shard_map/ppermute | solution.py:527
  24.1 4.1 %collective-permute-start.5 = (f32[5,16,128]{2,1,0:T(8,128)S(1)}, f32[5,16,128]{2,1,0:T(8,128)S(1)}, u32[]{:S(2)}, u32[]{:S(2)}) collective-permute-start(f32[5,16,128]{2,1,0:T(8,128)S(1)} %get-tuple-element.45), channel_id=1, source_target_pairs={{0,16},{8,24},{16,0},{24,8},{1,17},{9,25},{17,1},{25,9},{2,18},{10... | collective-permute-start | bytes 122888 | tf_op jit(solution)/shard_map/ppermute | solution.py:527
  44.5 1.3 %collective-permute-start.6 = (f32[128,128]{1,0:T(8,128)S(1)}, f32[128,128]{1,0:T(8,128)S(1)}, u32[]{:S(2)}, u32[]{:S(2)}) collective-permute-start(f32[128,128]{1,0:T(8,128)S(1)} %node_sums.1), channel_id=1, source_target_pairs={{0,8},{8,0},{16,24},{24,16},{1,9},{9,1},{17,25},{25,17},{2,10},{10... | collective-permute-start | bytes 196616 | tf_op jit(solution)/shard_map/ppermute | solution.py:560

commit v10 on v9

--- a/solution.py
+++ b/solution.py
@@ -100,47 +100,80 @@
     )(in_hbm(psi))
 
 
-def forward_local(source, psi, lateral, second, first, ratio, inv, total):
+def inner_right_side(source, psi, lateral):
     planes, width = source.shape[0], source.shape[2]
 
-    def kernel(source_ref, psi_ref, lateral_ref, second_ref, first_ref, ratio_ref, inv_ref, total_ref,
-               scaled_ref, map_ref):
-        is_odd = lax.rem(lax.axis_index("bulk"), 2) == 1
-
-        def body(i, state):
+    def kernel(source_ref, psi_ref, lateral_ref, right_ref, edge_ref):
+        row = lax.broadcasted_iota(jnp.int32, (width, LANES), 0)
+        none = jnp.zeros((1, LANES), F32)
+
+        def body(i, carry):
             below, above = lateral_ref[i, 0], lateral_ref[i, 1]
+            edge_ref[i, 0] = jnp.where(row == 0, below, 0.0)[:8]
+            edge_ref[i, 1] = jnp.where(row == width - 1, above, 0.0)[width - 8:]
             right = []
             for c in range(5):
-                one = first_ref[pl.ds(c * planes + i, 1), :]
-                two = second_ref[pl.ds(c * planes + i, 1), :]
                 here = psi_ref[i, c]
-                down = jnp.concatenate([jnp.where(is_odd, one, two), here[:width - 1]], axis=0)
-                up = jnp.concatenate([here[1:], jnp.where(is_odd, two, one)], axis=0)
+                down = jnp.concatenate([none, here[:width - 1]], axis=0)
+                up = jnp.concatenate([here[1:], none], axis=0)
                 right.append(source_ref[i, c] - below * down - above * up)
+            for c in range(5):
+                right_ref[i, c] = right[c]
+            return carry
+
+        lax.fori_loop(0, planes, body, 0, unroll=2)
+
+    return pl.pallas_call(
+        kernel,
+        out_shape=(VMEM(source.shape, F32), VMEM((planes, 2, 8, LANES), F32)),
+        in_specs=vmem_specs(3),
+        out_specs=tuple(vmem_specs(2)),
+        compiler_params=pltpu.CompilerParams(vmem_limit_bytes=4 << 20),
+        name="inner_right_side",
+    )(*[in_vmem(v) for v in (source, psi, lateral)])
+
+
+def forward_local(right, edge, second, first, ratio, inv, total):
+    planes, width = right.shape[0], right.shape[2]
+    parts = halves(width)
+
+    def kernel(right_ref, edge_ref, second_ref, first_ref, ratio_ref, inv_ref, total_ref,
+               scaled_ref, map_ref, low_ref, high_ref):
+        is_odd = lax.rem(lax.axis_index("bulk"), 2) == 1
+        one, two = first_ref[...], second_ref[...]
+        low_ref[...] = jnp.where(is_odd, one, two)
+        high_ref[...] = jnp.where(is_odd, two, one)
+
+        def body(i, state):
             out = []
-            for h, rows in enumerate(halves(width)):
-                r = [v[8 * h:8 * h + 8] for v in right]
+            for h, rows in enumerate(parts):
+                r = [right_ref[i, c, rows, :] for c in range(5)]
+                for last, halo_ref in ((0, low_ref), (len(parts) - 1, high_ref)):
+                    if h == last:
+                        k = 0 if halo_ref is low_ref else 1
+                        r = [r[c] - edge_ref[i, k] * halo_ref[pl.ds(c * planes + i, 1), :] for c in range(5)]
                 d = block(inv_ref, i, rows)
                 e = block(ratio_ref, i, rows)
                 g = [dot5(d[c], r) for c in range(5)]
                 out.append((g, [g[c] - dot5(e[c], state[h]) for c in range(5)]))
-            for h, rows in enumerate(halves(width)):
+            for h, rows in enumerate(parts):
                 for c in range(5):
                     scaled_ref[i, c, rows, :] = out[h][0][c]
             return [f for _, f in out]
 
-        zero = [[jnp.zeros((8, LANES), F32)] * 5 for _ in halves(width)]
+        zero = [[jnp.zeros((8, LANES), F32)] * 5 for _ in parts]
         state = lax.fori_loop(0, planes, body, zero, unroll=2)
         keep_map(map_ref, total_ref, state, width)
 
     return pl.pallas_call(
         kernel,
-        out_shape=(VMEM(source.shape, F32), jax.ShapeDtypeStruct((6,) + source.shape[1:], F32)),
-        in_specs=vmem_specs(8),
+        out_shape=(VMEM(right.shape, F32), jax.ShapeDtypeStruct((6,) + right.shape[1:], F32)),
+        in_specs=vmem_specs(7),
         out_specs=tuple(vmem_specs(2)),
+        scratch_shapes=[VMEM(first.shape, F32), VMEM(first.shape, F32)],
         compiler_params=pltpu.CompilerParams(vmem_limit_bytes=4 << 20),
         name="forward_local",
-    )(*[in_vmem(v) for v in (source, psi, lateral, second, first, ratio, inv, total)])
+    )(*[in_vmem(v) for v in (right, edge, second, first, ratio, inv, total)])
 
 
 def matrices(coupled, inv, backward, name):
@@ -542,7 +575,9 @@
     first = lax.ppermute(low_edge, "bulk", low_pairs)
 
     ratio, total = matrices(lower_jac, diag_inv, False, "forward_matrices")
-    scaled, own = forward_local(source, psi_old, lateral, second, first, ratio, diag_inv, total)
+    right, edge = inner_right_side(source, psi_old, lateral)
+    right, edge, ratio = lax.optimization_barrier((right, edge, ratio))
+    scaled, own = forward_local(right, edge, second, first, ratio, diag_inv, total)
     arriving, joined = relay(own, False)
     upper_jac, joined = lax.optimization_barrier((upper_jac, joined))
     back_ratio, back_total = matrices(upper_jac, diag_inv, True, "backward_matrices")

time: 46.7 us -> 47.1 us (level)
    pallas_call x1 -> x2, Pallas kernels: 1.49 us -> 1.67 us  [the longest x1 1.22 us: forward_local(): pl.pallas_call(kernel, out_shape=(VMEM(right.shape, F32), jax.ShapeDtypeS...]
  transfers between devices with their start and end apart: 7 -> 7, of which waited for: 4 -> 4; matrix products, arithmetic and copies ran while one was open for 0% -> 0% of each run, Pallas kernels for 18% -> 20%
where the time goes in v10:
time: 47.1 us; the launch traced here: 46.9 us
  Pallas kernels  18.1 us (38%)
  blocking collectives  10.9 us (23%)
  starting transfers between devices  9.33 us (20%)
  waiting for transfers between devices  6.35 us (13%)
  between operations  1.53 us (3%)
  other arithmetic  0.64 us (1%)
    all_to_all x1, blocking collectives, per_device(): got = lax.all_to_all(send, ('sweep', 'bulk'), 0, 0, tiled=True)  10.9 us
    pallas_call x2, Pallas kernels, matrices(): pl.pallas_call(kernel, out_shape=(VMEM(coupled.shape, F32), jax.ShapeDtyp...  8.15 us
    ppermute x1, starting transfers between devices, per_device(): first = lax.ppermute(low_edge, 'bulk', low_pairs)  6.06 us
    ppermute x4, waiting for transfers between devices, relay(): other = lax.ppermute(own, 'sweep', pairs)  5.2 us
    pallas_call x1, Pallas kernels, backward_and_faces(): pl.pallas_call(kernel, out_shape=(jax.ShapeDtypeStruct(field.shape, F32),...  4.17 us
    ppermute x4, starting transfers between devices, relay(): other = lax.ppermute(own, 'sweep', pairs)  2.3 us
    pallas_call x1, Pallas kernels, node_sums(): pl.pallas_call(kernel, out_shape=jax.ShapeDtypeStruct((side, LANES), F32)...  1.26 us
    pallas_call x1, Pallas kernels, forward_local(): pl.pallas_call(kernel, out_shape=(VMEM(right.shape, F32), jax.ShapeDtypeS...  1.22 us
  transfers between devices with their start and end apart: 7, of which 4 were waited for; matrix products, arithmetic and copies ran while one was open for 0% of the time, Pallas kernels for 20%

profile of v10, /device:TPU:0, one launch (start us, length us, event | category | flops | bytes accessed | tf_op | source)
XLA Modules:
  0.0 46.9 jit_solution(14987783176172831010)
XLA Ops:
  0.6 0.0 copy-start.8
  0.6 0.0 copy-start
  0.6 1.1 %edge_rows.1 = (f32[160,128]{1,0:T(8,128)S(1)}, f32[160,128]{1,0:T(8,128)S(1)}) custom-call(f32[32,5,16,128]{3,2,1,0:T(8,128)} %psi_hbm.1), custom_call_target="tpu_custom_call" | custom-call | flops 10000000000 | bytes 20000000 | tf_op jit(solution)/shard_map/edge_rows/pallas_call | solution.py:91
  1.7 0.0 copy-start.1
  1.8 0.0 copy-start.2
  1.8 0.0 copy-start.3
  1.8 0.8 %collective-permute-start = (f32[160,128]{1,0:T(8,128)S(1)}, f32[160,128]{1,0:T(8,128)S(1)}, u32[]{:S(2)}, u32[]{:S(2)}) collective-permute-start(f32[160,128]{1,0:T(8,128)S(1)} %get-tuple-element.39), channel_id=1, source_target_pairs={{1,2},{2,1},{3,4},{4,3},{5,6},{6,5},{9,10},{10,9},{11,12},{12,11},... | collective-permute-start | bytes 245768 | tf_op jit(solution)/shard_map/ppermute | solution.py:574
  2.6 6.1 %collective-permute-start.1 = (f32[160,128]{1,0:T(8,128)S(1)}, f32[160,128]{1,0:T(8,128)S(1)}, u32[]{:S(2)}, u32[]{:S(2)}) collective-permute-start(f32[160,128]{1,0:T(8,128)S(1)} %get-tuple-element.40), channel_id=1, source_target_pairs={{0,1},{1,0},{2,3},{3,2},{4,5},{5,4},{6,7},{7,6},{8,9},{9,8},{10,11... | collective-permute-start | bytes 245768 | tf_op jit(solution)/shard_map/ppermute | solution.py:575
  8.6 0.0 copy-done.8
  8.6 0.0 copy-done
  8.7 4.1 %forward_matrices.1 = (f32[32,5,5,16,128]{4,3,2,1,0:T(8,128)S(1)}, f32[5,5,16,128]{3,2,1,0:T(8,128)S(1)}) custom-call(f32[32,5,5,16,128]{4,3,2,1,0:T(8,128)S(1)} %copy-done.8, f32[32,5,5,16,128]{4,3,2,1,0:T(8,128)S(1)} %copy-done), custom_call_target="tpu_custom_call" | custom-call | flops 5000000000 | bytes 20000000 | tf_op jit(solution)/shard_map/forward_matrices/pallas_call | solution.py:194
  12.7 0.0 copy-done.1
  12.7 0.0 copy-done.2
  12.7 0.0 copy-done.3
  12.8 0.0 slice-start
  12.8 0.5 inner_right_side.1
  13.2 0.0 collective-permute-done.second_ref
  13.2 0.0 collective-permute-done.1.first_ref
  13.3 0.0 slice-start.1
  13.3 1.2 %forward_local.1 = (f32[32,5,16,128]{3,2,1,0:T(8,128)S(1)}, f32[6,5,16,128]{3,2,1,0:T(8,128)S(1)}) custom-call(f32[32,5,16,128]{3,2,1,0:T(8,128)S(1)} %get-tuple-element.37.right_ref, f32[32,2,8,128]{3,2,1,0:T(8,128)S(1)} %get-tuple-element.38.edge_ref, f32[160,128]{1,0:T(8,128)S(1)} %collective-permute-done.second_ref, ...), custom_call_target="tpu_custom_call" | custom-call | tf_op jit(solution)/shard_map/forward_local/pallas_call | solution.py:168
  14.5 0.1 collective-permute-start.2
  14.6 1.5 %collective-permute-done.2.refs_1_ = f32[6,5,16,128]{3,2,1,0:T(8,128)S(1)} collective-permute-done((f32[6,5,16,128]{3,2,1,0:T(8,128)S(1)}, f32[6,5,16,128]{3,2,1,0:T(8,128)S(1)}, u32[]{:S(2)}, u32[]{:S(2)}) %collective-permute-start.2) | collective-permute-done | bytes 245792 | tf_op jit(solution)/shard_map/ppermute | solution.py:560
  16.1 0.1 join.2
  16.1 1.6 %collective-permute-start.3 = (f32[5,16,128]{2,1,0:T(8,128)S(1)}, f32[5,16,128]{2,1,0:T(8,128)S(1)}, u32[]{:S(2)}, u32[]{:S(2)}) collective-permute-start(f32[5,16,128]{2,1,0:T(8,128)S(1)} %get-tuple-element.47), channel_id=1, source_target_pairs={{0,16},{8,24},{16,0},{24,8},{1,17},{9,25},{17,1},{25,9},{2,18},{10... | collective-permute-start | bytes 122888 | tf_op jit(solution)/shard_map/ppermute | solution.py:560
  17.7 0.0 slice-done
  17.7 0.0 slice-done.1
  17.7 4.1 %backward_matrices.1 = (f32[32,5,5,16,128]{4,3,2,1,0:T(8,128)S(1)}, f32[5,5,16,128]{3,2,1,0:T(8,128)S(1)}) custom-call(f32[32,5,5,16,128]{4,3,2,1,0:T(8,128)S(1)} %bitcast.9, f32[32,5,5,16,128]{4,3,2,1,0:T(8,128)S(1)} %copy-done), custom_call_target="tpu_custom_call" | custom-call | flops 5000000000 | bytes 20000000 | tf_op jit(solution)/shard_map/backward_matrices/pallas_call | solution.py:194
  21.8 0.0 collective-permute-done.3.other_ref
  21.8 0.0 copy-start.6
  21.8 0.0 copy-start.7
  21.8 0.0 copy-start.4
  21.8 0.0 copy-start.5
  21.8 1.1 %forward_then_back.1 = (f32[32,5,16,128]{3,2,1,0:T(8,128)S(1)}, f32[6,5,16,128]{3,2,1,0:T(8,128)S(1)}) custom-call(f32[32,5,16,128]{3,2,1,0:T(8,128)S(1)} %get-tuple-element.43.scaled_ref, f32[5,16,128]{2,1,0:T(8,128)S(1)} %get-tuple-element.45.near_ref, f32[5,5,16,128]{3,2,1,0:T(8,128)S(1)} %get-tuple-element.46.reach_ref, ...), custom_call_target="tpu_custom_call" | custom-call | tf_op jit(solution)/shard_map/forward_then_back/pallas_call | solution.py:235
  22.9 0.1 collective-permute-start.4
  23.0 1.5 %collective-permute-done.4.refs_1_ = f32[6,5,16,128]{3,2,1,0:T(8,128)S(1)} collective-permute-done((f32[6,5,16,128]{3,2,1,0:T(8,128)S(1)}, f32[6,5,16,128]{3,2,1,0:T(8,128)S(1)}, u32[]{:S(2)}, u32[]{:S(2)}) %collective-permute-start.4) | collective-permute-done | bytes 245792 | tf_op jit(solution)/shard_map/ppermute | solution.py:560
  24.6 0.6 %collective-permute-start.5 = (f32[5,16,128]{2,1,0:T(8,128)S(1)}, f32[5,16,128]{2,1,0:T(8,128)S(1)}, u32[]{:S(2)}, u32[]{:S(2)}) collective-permute-start(f32[5,16,128]{2,1,0:T(8,128)S(1)} %get-tuple-element.55), channel_id=1, source_target_pairs={{0,16},{8,24},{16,0},{24,8},{1,17},{9,25},{17,1},{25,9},{2,18},{10... | collective-permute-start | bytes 122888 | tf_op jit(solution)/shard_map/ppermute | solution.py:560
  25.8 0.0 copy-done.6
  25.8 0.0 copy-done.7
  25.8 0.6 %face_slots.1 = (s32[16,128]{1,0:T(8,128)S(1)}, f32[32,128]{1,0:T(8,128)S(1)}) custom-call(s32[16,128]{1,0:T(8,128)S(1)} %bitcast.6, s32[16,128]{1,0:T(8,128)S(1)} %bitcast.7), custom_call_target="tpu_custom_call" | custom-call | flops 4000000 | bytes 10000000 | tf_op jit(solution)/shard_map/face_slots/pallas_call | solution.py:276
  26.4 2.2 %collective-permute-done.5.other_ref = f32[5,16,128]{2,1,0:T(8,128)S(1)} collective-permute-done((f32[5,16,128]{2,1,0:T(8,128)S(1)}, f32[5,16,128]{2,1,0:T(8,128)S(1)}, u32[]{:S(2)}, u32[]{:S(2)}) %collective-permute-start.5) | collective-permute-done | bytes 40992 | tf_op jit(solution)/shard_map/ppermute | solution.py:560
  28.6 0.0 copy-done.4
  28.6 0.0 copy-done.5
  28.6 4.2 %backward_and_faces.1 = (f32[32,5,16,128]{3,2,1,0:T(8,128)}, f32[32,4,128]{2,1,0:T(4,128)S(1)}) custom-call(s32[1]{0:T(128)S(6)} %copy.13.count_ref, f32[32,5,16,128]{3,2,1,0:T(8,128)S(1)} %get-tuple-element.51.field_ref, f32[5,16,128]{2,1,0:T(8,128)S(1)} %get-tuple-element.53.near_ref, f32[5,5,16,128]{3,2,1,0:T(8,128)S(1)} %get-tuple-element.54.reach_ref, ...), custom_call_target="tpu_custom_call" | custom-call | tf_op jit(solution)/shard_map/backward_and_faces/pallas_call | solution.py:403
  32.8 10.9 %all_to_all.5.got_ref = f32[32,4,128]{2,1,0:T(4,128)S(1)} all-to-all(f32[32,4,128]{2,1,0:T(4,128)S(1)} %get-tuple-element.59), channel_id=1, replica_groups=mesh['sweep'=4,'bulk'=8] {'sweep','bulk'}, dimensions={0} | all-to-all | bytes 131072 | tf_op jit(solution)/shard_map/all_to_all | solution.py:592
  43.7 1.3 %node_sums.1 = f32[128,128]{1,0:T(8,128)S(1)} custom-call(f32[32,4,128]{2,1,0:T(4,128)S(1)} %all_to_all.5.got_ref), custom_call_target="tpu_custom_call" | custom-call | tf_op jit(solution)/shard_map/node_sums/pallas_call | solution.py:459
  45.0 0.2 collective-permute-start.6
  45.1 1.1 %collective-permute-done.6 = f32[128,128]{1,0:T(8,128)S(1)} collective-permute-done((f32[128,128]{1,0:T(8,128)S(1)}, f32[128,128]{1,0:T(8,128)S(1)}, u32[]{:S(2)}, u32[]{:S(2)}) %collective-permute-start.6) | collective-permute-done | bytes 65568 | tf_op jit(solution)/shard_map/ppermute | solution.py:595
  46.3 0.6 %add_bitcast_fusion = f32[16384]{0:T(1024)} fusion(f32[128,128]{1,0:T(8,128)S(1)} %node_sums.1, f32[128,128]{1,0:T(8,128)S(1)} %collective-permute-done.6), kind=kLoop, calls=%fused_computation | loop fusion | flops 16384 | bytes 196608 | tf_op jit(solution)/shard_map/reshape | solution.py:595
  (2 shorter events, 0.0 us)
Async XLA Ops:
  0.6 8.0 %copy-start.8 = (f32[32,5,5,16,128]{4,3,2,1,0:T(8,128)S(1)}, f32[32,5,5,16,128]{4,3,2,1,0:T(8,128)}, u32[]{:S(2)}) copy-start(f32[32,5,5,16,128]{4,3,2,1,0:T(8,128)} %coupled_ref) | copy-start | bytes 19660804
  0.6 8.0 %copy-start = (f32[32,5,5,16,128]{4,3,2,1,0:T(8,128)S(1)}, f32[32,5,5,16,128]{4,3,2,1,0:T(8,128)}, u32[]{:S(2)}) copy-start(f32[32,5,5,16,128]{4,3,2,1,0:T(8,128)} %inv_ref.5) | copy-start | bytes 19660804
  1.7 11.0 %copy-start.1 = (f32[32,5,16,128]{3,2,1,0:T(8,128)S(1)}, f32[32,5,16,128]{3,2,1,0:T(8,128)}, u32[]{:S(2)}) copy-start(f32[32,5,16,128]{3,2,1,0:T(8,128)} %source_ref.1) | copy-start | bytes 3932164
  1.8 11.0 %copy-start.2 = (f32[32,5,16,128]{3,2,1,0:T(8,128)S(1)}, f32[32,5,16,128]{3,2,1,0:T(8,128)}, u32[]{:S(2)}) copy-start(f32[32,5,16,128]{3,2,1,0:T(8,128)} %psi_hbm.1) | copy-start | bytes 3932164
  1.8 11.0 %copy-start.3 = (f32[32,2,16,128]{3,2,1,0:T(8,128)S(1)}, f32[32,2,16,128]{3,2,1,0:T(8,128)}, u32[]{:S(2)}) copy-start(f32[32,2,16,128]{3,2,1,0:T(8,128)} %lateral_ref.1) | copy-start | bytes 1572868
  1.8 11.5 %collective-permute-start = (f32[160,128]{1,0:T(8,128)S(1)}, f32[160,128]{1,0:T(8,128)S(1)}, u32[]{:S(2)}, u32[]{:S(2)}) collective-permute-start(f32[160,128]{1,0:T(8,128)S(1)} %get-tuple-element.39), channel_id=1, source_target_pairs={{1,2},{2,1},{3,4},{4,3},{5,6},{6,5},{9,10},{10,9},{11,12},{12,11},... | collective-permute-start | bytes 245768 | tf_op jit(solution)/shard_map/ppermute | solution.py:574
  2.6 10.7 %collective-permute-start.1 = (f32[160,128]{1,0:T(8,128)S(1)}, f32[160,128]{1,0:T(8,128)S(1)}, u32[]{:S(2)}, u32[]{:S(2)}) collective-permute-start(f32[160,128]{1,0:T(8,128)S(1)} %get-tuple-element.40), channel_id=1, source_target_pairs={{0,1},{1,0},{2,3},{3,2},{4,5},{5,4},{6,7},{7,6},{8,9},{9,8},{10,11... | collective-permute-start | bytes 245768 | tf_op jit(solution)/shard_map/ppermute | solution.py:575
  12.8 4.9 %slice-start = ((s8[6553600]{0:T(1024)(128)(4,1)}), s8[4194304]{0:T(1024)(128)(4,1)S(1)}, s32[]{:S(2)}) async-start(s8[6553600]{0:T(1024)(128)(4,1)} %bitcast.8), calls=%async_computation.1 | async-start | bytes 8388608
  13.3 4.4 %slice-start.1 = ((s8[6553600]{0:T(1024)(128)(4,1)}), s8[2359296]{0:T(1024)(128)(4,1)S(1)}, s32[]{:S(2)}) async-start(s8[6553600]{0:T(1024)(128)(4,1)} %bitcast.8), calls=%async_computation.2 | async-start | bytes 4718592
  14.5 1.6 %collective-permute-start.2 = (f32[6,5,16,128]{3,2,1,0:T(8,128)S(1)}, f32[6,5,16,128]{3,2,1,0:T(8,128)S(1)}, u32[]{:S(2)}, u32[]{:S(2)}) collective-permute-start(f32[6,5,16,128]{3,2,1,0:T(8,128)S(1)} %get-tuple-element.44.refs_0_), channel_id=1, source_target_pairs={{0,8},{8,0},{16,24},{24,16},{1,9},{9,1},{17,25},{25,17},{2,10},{10... | collective-permute-start | bytes 737288 | tf_op jit(solution)/shard_map/ppermute | solution.py:560
  16.1 5.6 %collective-permute-start.3 = (f32[5,16,128]{2,1,0:T(8,128)S(1)}, f32[5,16,128]{2,1,0:T(8,128)S(1)}, u32[]{:S(2)}, u32[]{:S(2)}) collective-permute-start(f32[5,16,128]{2,1,0:T(8,128)S(1)} %get-tuple-element.47), channel_id=1, source_target_pairs={{0,16},{8,24},{16,0},{24,8},{1,17},{9,25},{17,1},{25,9},{2,18},{10... | collective-permute-start | bytes 122888 | tf_op jit(solution)/shard_map/ppermute | solution.py:560
  21.8 4.0 %copy-start.6 = (s32[2048,1]{0,1:T(1,128)S(1)}, s32[2048,1]{0,1:T(1,128)}, u32[]{:S(2)}) copy-start(s32[2048,1]{0,1:T(1,128)} %param.19) | copy-start | bytes 24580
  21.8 4.0 %copy-start.7 = (s32[2048]{0:T(1024)S(1)}, s32[2048]{0:T(1024)}, u32[]{:S(2)}) copy-start(s32[2048]{0:T(1024)} %param.20) | copy-start | bytes 24580
  21.8 6.8 %copy-start.4 = (f32[5,2048]{1,0:T(8,128)S(1)}, f32[5,2048]{1,0:T(8,128)}, u32[]{:S(2)}) copy-start(f32[5,2048]{1,0:T(8,128)} %weight_ref.1) | copy-start | bytes 122884
  21.8 6.8 %copy-start.5 = (s32[2048]{0:T(1024)S(1)}, s32[2048]{0:T(1024)}, u32[]{:S(2)}) copy-start(s32[2048]{0:T(1024)} %param.18) | copy-start | bytes 24580
  22.9 1.6 %collective-permute-start.4 = (f32[6,5,16,128]{3,2,1,0:T(8,128)S(1)}, f32[6,5,16,128]{3,2,1,0:T(8,128)S(1)}, u32[]{:S(2)}, u32[]{:S(2)}) collective-permute-start(f32[6,5,16,128]{3,2,1,0:T(8,128)S(1)} %get-tuple-element.52.refs_0_), channel_id=1, source_target_pairs={{0,8},{8,0},{16,24},{24,16},{1,9},{9,1},{17,25},{25,17},{2,10},{10... | collective-permute-start | bytes 737288 | tf_op jit(solution)/shard_map/ppermute | solution.py:560
  24.6 4.1 %collective-permute-start.5 = (f32[5,16,128]{2,1,0:T(8,128)S(1)}, f32[5,16,128]{2,1,0:T(8,128)S(1)}, u32[]{:S(2)}, u32[]{:S(2)}) collective-permute-start(f32[5,16,128]{2,1,0:T(8,128)S(1)} %get-tuple-element.55), channel_id=1, source_target_pairs={{0,16},{8,24},{16,0},{24,8},{1,17},{9,25},{17,1},{25,9},{2,18},{10... | collective-permute-start | bytes 122888 | tf_op jit(solution)/shard_map/ppermute | solution.py:560
  45.0 1.3 %collective-permute-start.6 = (f32[128,128]{1,0:T(8,128)S(1)}, f32[128,128]{1,0:T(8,128)S(1)}, u32[]{:S(2)}, u32[]{:S(2)}) collective-permute-start(f32[128,128]{1,0:T(8,128)S(1)} %node_sums.1), channel_id=1, source_target_pairs={{0,8},{8,0},{16,24},{24,16},{1,9},{9,1},{17,25},{25,17},{2,10},{10... | collective-permute-start | bytes 196616 | tf_op jit(solution)/shard_map/ppermute | solution.py:595

commit v11 on v9

--- a/solution.py
+++ b/solution.py
@@ -130,7 +130,7 @@
             return [f for _, f in out]
 
         zero = [[jnp.zeros((8, LANES), F32)] * 5 for _ in halves(width)]
-        state = lax.fori_loop(0, planes, body, zero, unroll=2)
+        state = lax.fori_loop(0, planes, body, zero, unroll=4)
         keep_map(map_ref, total_ref, state, width)
 
     return pl.pallas_call(
@@ -156,7 +156,7 @@
                 keep_matrices(ratio, next_total(ratio, total_ref, rows), ratio_ref, total_ref, at, rows)
             return carry
 
-        lax.fori_loop(0, planes, body, 0, unroll=2)
+        lax.fori_loop(0, planes, body, 0, unroll=4)
 
     return pl.pallas_call(
         kernel,

time: 46.7 us -> 46.4 us (level)
  no operation moved by 1% of the time
where the time goes in v11:
time: 46.4 us; the launch traced here: 46.3 us
  Pallas kernels  17.5 us (38%)
  blocking collectives  10.9 us (23%)
  starting transfers between devices  9.33 us (20%)
  waiting for transfers between devices  6.34 us (14%)
  between operations  1.52 us (3%)
  other arithmetic  0.64 us (1%)
    all_to_all x1, blocking collectives, per_device(): got = lax.all_to_all(send, ('sweep', 'bulk'), 0, 0, tiled=True)  10.9 us
    pallas_call x2, Pallas kernels, matrices(): pl.pallas_call(kernel, out_shape=(VMEM(coupled.shape, F32), jax.ShapeDtyp...  7.75 us
    ppermute x1, starting transfers between devices, per_device(): first = lax.ppermute(low_edge, 'bulk', low_pairs)  6.06 us
    ppermute x4, waiting for transfers between devices, relay(): other = lax.ppermute(own, 'sweep', pairs)  5.2 us
    pallas_call x1, Pallas kernels, backward_and_faces(): pl.pallas_call(kernel, out_shape=(jax.ShapeDtypeStruct(field.shape, F32),...  4.17 us
    ppermute x4, starting transfers between devices, relay(): other = lax.ppermute(own, 'sweep', pairs)  2.3 us
    pallas_call x1, Pallas kernels, forward_local(): pl.pallas_call(kernel, out_shape=(VMEM(source.shape, F32), jax.ShapeDtype...  1.42 us
    pallas_call x1, Pallas kernels, node_sums(): pl.pallas_call(kernel, out_shape=jax.ShapeDtypeStruct((side, LANES), F32)...  1.26 us
  transfers between devices with their start and end apart: 7, of which 4 were waited for; matrix products, arithmetic and copies ran while one was open for 0% of the time, Pallas kernels for 18%

profile of v11, /device:TPU:0, one launch (start us, length us, event | category | flops | bytes accessed | tf_op | source)
XLA Modules:
  0.0 46.3 jit_solution(13394496066355359390)
XLA Ops:
  0.6 0.0 copy-start.8
  0.6 0.0 copy-start
  0.6 1.1 %edge_rows.1 = (f32[160,128]{1,0:T(8,128)S(1)}, f32[160,128]{1,0:T(8,128)S(1)}) custom-call(f32[32,5,16,128]{3,2,1,0:T(8,128)} %psi_ref.1), custom_call_target="tpu_custom_call" | custom-call | flops 10000000000 | bytes 20000000 | tf_op jit(solution)/shard_map/edge_rows/pallas_call | solution.py:91
  1.7 0.0 copy-start.1
  1.8 0.0 copy-start.2
  1.8 0.0 copy-start.3
  1.8 0.8 %collective-permute-start = (f32[160,128]{1,0:T(8,128)S(1)}, f32[160,128]{1,0:T(8,128)S(1)}, u32[]{:S(2)}, u32[]{:S(2)}) collective-permute-start(f32[160,128]{1,0:T(8,128)S(1)} %get-tuple-element.28), channel_id=1, source_target_pairs={{1,2},{2,1},{3,4},{4,3},{5,6},{6,5},{9,10},{10,9},{11,12},{12,11},... | collective-permute-start | bytes 245768 | tf_op jit(solution)/shard_map/ppermute | solution.py:541
  2.6 6.1 %collective-permute-start.1 = (f32[160,128]{1,0:T(8,128)S(1)}, f32[160,128]{1,0:T(8,128)S(1)}, u32[]{:S(2)}, u32[]{:S(2)}) collective-permute-start(f32[160,128]{1,0:T(8,128)S(1)} %get-tuple-element.29), channel_id=1, source_target_pairs={{0,1},{1,0},{2,3},{3,2},{4,5},{5,4},{6,7},{7,6},{8,9},{9,8},{10,11... | collective-permute-start | bytes 245768 | tf_op jit(solution)/shard_map/ppermute | solution.py:542
  8.6 0.0 copy-done.8
  8.6 0.0 copy-done
  8.7 3.9 %forward_matrices.1 = (f32[32,5,5,16,128]{4,3,2,1,0:T(8,128)S(1)}, f32[5,5,16,128]{3,2,1,0:T(8,128)S(1)}) custom-call(f32[32,5,5,16,128]{4,3,2,1,0:T(8,128)S(1)} %copy-done.8, f32[32,5,5,16,128]{4,3,2,1,0:T(8,128)S(1)} %copy-done), custom_call_target="tpu_custom_call" | custom-call | flops 5000000000 | bytes 20000000 | tf_op jit(solution)/shard_map/forward_matrices/pallas_call | solution.py:161
  12.5 0.0 collective-permute-done.second_ref
  12.5 0.0 collective-permute-done.1.first_ref
  12.6 0.0 copy-done.1
  12.6 0.0 copy-done.2
  12.6 0.0 copy-done.3
  12.6 0.0 copy-start.9
  12.6 1.4 %forward_local.1 = (f32[32,5,16,128]{3,2,1,0:T(8,128)S(1)}, f32[6,5,16,128]{3,2,1,0:T(8,128)S(1)}) custom-call(f32[32,5,16,128]{3,2,1,0:T(8,128)S(1)} %copy-done.1, f32[32,5,16,128]{3,2,1,0:T(8,128)S(1)} %copy-done.2, f32[32,2,16,128]{3,2,1,0:T(8,128)S(1)} %copy-done.3, f32[160,128]{1,0:T(8,128)S(1)} %collective-permute-done.second_ref, ...), custom_call_target="tpu_custom_call" | custom-call | tf_op jit(solution)/shard_map/forward_local/pallas_call | solution.py:136
  14.0 0.1 collective-permute-start.2
  14.1 1.5 %collective-permute-done.2.refs_1_ = f32[6,5,16,128]{3,2,1,0:T(8,128)S(1)} collective-permute-done((f32[6,5,16,128]{3,2,1,0:T(8,128)S(1)}, f32[6,5,16,128]{3,2,1,0:T(8,128)S(1)}, u32[]{:S(2)}, u32[]{:S(2)}) %collective-permute-start.2) | collective-permute-done | bytes 245792 | tf_op jit(solution)/shard_map/ppermute | solution.py:527
  15.6 0.1 join.2
  15.7 1.6 %collective-permute-start.3 = (f32[5,16,128]{2,1,0:T(8,128)S(1)}, f32[5,16,128]{2,1,0:T(8,128)S(1)}, u32[]{:S(2)}, u32[]{:S(2)}) collective-permute-start(f32[5,16,128]{2,1,0:T(8,128)S(1)} %get-tuple-element.37), channel_id=1, source_target_pairs={{0,16},{8,24},{16,0},{24,8},{1,17},{9,25},{17,1},{25,9},{2,18},{10... | collective-permute-start | bytes 122888 | tf_op jit(solution)/shard_map/ppermute | solution.py:527
  17.2 0.0 copy-done.9
  17.2 3.9 %backward_matrices.1 = (f32[32,5,5,16,128]{4,3,2,1,0:T(8,128)S(1)}, f32[5,5,16,128]{3,2,1,0:T(8,128)S(1)}) custom-call(f32[32,5,5,16,128]{4,3,2,1,0:T(8,128)S(1)} %copy-done.9, f32[32,5,5,16,128]{4,3,2,1,0:T(8,128)S(1)} %copy-done), custom_call_target="tpu_custom_call" | custom-call | flops 5000000000 | bytes 20000000 | tf_op jit(solution)/shard_map/backward_matrices/pallas_call | solution.py:161
  21.1 0.0 collective-permute-done.3.other_ref
  21.1 0.0 copy-start.6
  21.1 0.0 copy-start.7
  21.1 0.0 copy-start.4
  21.1 0.0 copy-start.5
  21.2 1.1 %forward_then_back.1 = (f32[32,5,16,128]{3,2,1,0:T(8,128)S(1)}, f32[6,5,16,128]{3,2,1,0:T(8,128)S(1)}) custom-call(f32[32,5,16,128]{3,2,1,0:T(8,128)S(1)} %get-tuple-element.33.scaled_ref, f32[5,16,128]{2,1,0:T(8,128)S(1)} %get-tuple-element.35.near_ref, f32[5,5,16,128]{3,2,1,0:T(8,128)S(1)} %get-tuple-element.36.reach_ref, ...), custom_call_target="tpu_custom_call" | custom-call | tf_op jit(solution)/shard_map/forward_then_back/pallas_call | solution.py:202
  22.3 0.1 collective-permute-start.4
  22.3 1.5 %collective-permute-done.4.refs_1_ = f32[6,5,16,128]{3,2,1,0:T(8,128)S(1)} collective-permute-done((f32[6,5,16,128]{3,2,1,0:T(8,128)S(1)}, f32[6,5,16,128]{3,2,1,0:T(8,128)S(1)}, u32[]{:S(2)}, u32[]{:S(2)}) %collective-permute-start.4) | collective-permute-done | bytes 245792 | tf_op jit(solution)/shard_map/ppermute | solution.py:527
  23.9 0.6 %collective-permute-start.5 = (f32[5,16,128]{2,1,0:T(8,128)S(1)}, f32[5,16,128]{2,1,0:T(8,128)S(1)}, u32[]{:S(2)}, u32[]{:S(2)}) collective-permute-start(f32[5,16,128]{2,1,0:T(8,128)S(1)} %get-tuple-element.45), channel_id=1, source_target_pairs={{0,16},{8,24},{16,0},{24,8},{1,17},{9,25},{17,1},{25,9},{2,18},{10... | collective-permute-start | bytes 122888 | tf_op jit(solution)/shard_map/ppermute | solution.py:527
  25.1 0.0 copy-done.6
  25.2 0.0 copy-done.7
  25.2 0.6 %face_slots.1 = (s32[16,128]{1,0:T(8,128)S(1)}, f32[32,128]{1,0:T(8,128)S(1)}) custom-call(s32[16,128]{1,0:T(8,128)S(1)} %bitcast.6, s32[16,128]{1,0:T(8,128)S(1)} %bitcast.7), custom_call_target="tpu_custom_call" | custom-call | flops 4000000 | bytes 10000000 | tf_op jit(solution)/shard_map/face_slots/pallas_call | solution.py:243
  25.8 2.2 %collective-permute-done.5.other_ref = f32[5,16,128]{2,1,0:T(8,128)S(1)} collective-permute-done((f32[5,16,128]{2,1,0:T(8,128)S(1)}, f32[5,16,128]{2,1,0:T(8,128)S(1)}, u32[]{:S(2)}, u32[]{:S(2)}) %collective-permute-start.5) | collective-permute-done | bytes 40992 | tf_op jit(solution)/shard_map/ppermute | solution.py:527
  28.0 0.0 copy-done.4
  28.0 0.0 copy-done.5
  28.0 4.2 %backward_and_faces.1 = (f32[32,5,16,128]{3,2,1,0:T(8,128)}, f32[32,4,128]{2,1,0:T(4,128)S(1)}) custom-call(s32[1]{0:T(128)S(6)} %copy.13.count_ref, f32[32,5,16,128]{3,2,1,0:T(8,128)S(1)} %get-tuple-element.41.field_ref, f32[5,16,128]{2,1,0:T(8,128)S(1)} %get-tuple-element.43.near_ref, f32[5,5,16,128]{3,2,1,0:T(8,128)S(1)} %get-tuple-element.44.reach_ref, ...), custom_call_target="tpu_custom_call" | custom-call | tf_op jit(solution)/shard_map/backward_and_faces/pallas_call | solution.py:370
  32.1 10.9 %all_to_all.5.got_ref = f32[32,4,128]{2,1,0:T(4,128)S(1)} all-to-all(f32[32,4,128]{2,1,0:T(4,128)S(1)} %get-tuple-element.49), channel_id=1, replica_groups=mesh['sweep'=4,'bulk'=8] {'sweep','bulk'}, dimensions={0} | all-to-all | bytes 131072 | tf_op jit(solution)/shard_map/all_to_all | solution.py:557
  43.0 1.3 %node_sums.1 = f32[128,128]{1,0:T(8,128)S(1)} custom-call(f32[32,4,128]{2,1,0:T(4,128)S(1)} %all_to_all.5.got_ref), custom_call_target="tpu_custom_call" | custom-call | tf_op jit(solution)/shard_map/node_sums/pallas_call | solution.py:426
  44.3 0.2 collective-permute-start.6
  44.5 1.1 %collective-permute-done.6 = f32[128,128]{1,0:T(8,128)S(1)} collective-permute-done((f32[128,128]{1,0:T(8,128)S(1)}, f32[128,128]{1,0:T(8,128)S(1)}, u32[]{:S(2)}, u32[]{:S(2)}) %collective-permute-start.6) | collective-permute-done | bytes 65568 | tf_op jit(solution)/shard_map/ppermute | solution.py:560
  45.6 0.6 %add_bitcast_fusion = f32[16384]{0:T(1024)} fusion(f32[128,128]{1,0:T(8,128)S(1)} %node_sums.1, f32[128,128]{1,0:T(8,128)S(1)} %collective-permute-done.6), kind=kLoop, calls=%fused_computation | loop fusion | flops 16384 | bytes 196608 | tf_op jit(solution)/shard_map/reshape | solution.py:560
  (1 shorter events, 0.0 us)
Async XLA Ops:
  0.6 8.0 %copy-start.8 = (f32[32,5,5,16,128]{4,3,2,1,0:T(8,128)S(1)}, f32[32,5,5,16,128]{4,3,2,1,0:T(8,128)}, u32[]{:S(2)}) copy-start(f32[32,5,5,16,128]{4,3,2,1,0:T(8,128)} %coupled_ref) | copy-start | bytes 19660804
  0.6 8.0 %copy-start = (f32[32,5,5,16,128]{4,3,2,1,0:T(8,128)S(1)}, f32[32,5,5,16,128]{4,3,2,1,0:T(8,128)}, u32[]{:S(2)}) copy-start(f32[32,5,5,16,128]{4,3,2,1,0:T(8,128)} %inv_ref.5) | copy-start | bytes 19660804
  1.7 10.8 %copy-start.1 = (f32[32,5,16,128]{3,2,1,0:T(8,128)S(1)}, f32[32,5,16,128]{3,2,1,0:T(8,128)}, u32[]{:S(2)}) copy-start(f32[32,5,16,128]{3,2,1,0:T(8,128)} %source_ref.1) | copy-start | bytes 3932164
  1.8 10.8 %copy-start.2 = (f32[32,5,16,128]{3,2,1,0:T(8,128)S(1)}, f32[32,5,16,128]{3,2,1,0:T(8,128)}, u32[]{:S(2)}) copy-start(f32[32,5,16,128]{3,2,1,0:T(8,128)} %psi_ref.1) | copy-start | bytes 3932164
  1.8 10.8 %copy-start.3 = (f32[32,2,16,128]{3,2,1,0:T(8,128)S(1)}, f32[32,2,16,128]{3,2,1,0:T(8,128)}, u32[]{:S(2)}) copy-start(f32[32,2,16,128]{3,2,1,0:T(8,128)} %lateral_ref.1) | copy-start | bytes 1572868
  1.8 10.8 %collective-permute-start = (f32[160,128]{1,0:T(8,128)S(1)}, f32[160,128]{1,0:T(8,128)S(1)}, u32[]{:S(2)}, u32[]{:S(2)}) collective-permute-start(f32[160,128]{1,0:T(8,128)S(1)} %get-tuple-element.28), channel_id=1, source_target_pairs={{1,2},{2,1},{3,4},{4,3},{5,6},{6,5},{9,10},{10,9},{11,12},{12,11},... | collective-permute-start | bytes 245768 | tf_op jit(solution)/shard_map/ppermute | solution.py:541
  2.6 10.0 %collective-permute-start.1 = (f32[160,128]{1,0:T(8,128)S(1)}, f32[160,128]{1,0:T(8,128)S(1)}, u32[]{:S(2)}, u32[]{:S(2)}) collective-permute-start(f32[160,128]{1,0:T(8,128)S(1)} %get-tuple-element.29), channel_id=1, source_target_pairs={{0,1},{1,0},{2,3},{3,2},{4,5},{5,4},{6,7},{7,6},{8,9},{9,8},{10,11... | collective-permute-start | bytes 245768 | tf_op jit(solution)/shard_map/ppermute | solution.py:542
  12.6 4.6 %copy-start.9 = (f32[32,5,5,16,128]{4,3,2,1,0:T(8,128)S(1)}, f32[32,5,5,16,128]{4,3,2,1,0:T(8,128)}, u32[]{:S(2)}) copy-start(f32[32,5,5,16,128]{4,3,2,1,0:T(8,128)} %coupled_ref.1) | copy-start | bytes 19660804
  14.0 1.6 %collective-permute-start.2 = (f32[6,5,16,128]{3,2,1,0:T(8,128)S(1)}, f32[6,5,16,128]{3,2,1,0:T(8,128)S(1)}, u32[]{:S(2)}, u32[]{:S(2)}) collective-permute-start(f32[6,5,16,128]{3,2,1,0:T(8,128)S(1)} %get-tuple-element.34.refs_0_), channel_id=1, source_target_pairs={{0,8},{8,0},{16,24},{24,16},{1,9},{9,1},{17,25},{25,17},{2,10},{10... | collective-permute-start | bytes 737288 | tf_op jit(solution)/shard_map/ppermute | solution.py:527
  15.7 5.4 %collective-permute-start.3 = (f32[5,16,128]{2,1,0:T(8,128)S(1)}, f32[5,16,128]{2,1,0:T(8,128)S(1)}, u32[]{:S(2)}, u32[]{:S(2)}) collective-permute-start(f32[5,16,128]{2,1,0:T(8,128)S(1)} %get-tuple-element.37), channel_id=1, source_target_pairs={{0,16},{8,24},{16,0},{24,8},{1,17},{9,25},{17,1},{25,9},{2,18},{10... | collective-permute-start | bytes 122888 | tf_op jit(solution)/shard_map/ppermute | solution.py:527
  21.1 4.0 %copy-start.6 = (s32[2048,1]{0,1:T(1,128)S(1)}, s32[2048,1]{0,1:T(1,128)}, u32[]{:S(2)}) copy-start(s32[2048,1]{0,1:T(1,128)} %param.19) | copy-start | bytes 24580
  21.1 4.0 %copy-start.7 = (s32[2048]{0:T(1024)S(1)}, s32[2048]{0:T(1024)}, u32[]{:S(2)}) copy-start(s32[2048]{0:T(1024)} %param.20) | copy-start | bytes 24580
  21.1 6.8 %copy-start.4 = (f32[5,2048]{1,0:T(8,128)S(1)}, f32[5,2048]{1,0:T(8,128)}, u32[]{:S(2)}) copy-start(f32[5,2048]{1,0:T(8,128)} %weight_ref.1) | copy-start | bytes 122884
  21.1 6.8 %copy-start.5 = (s32[2048]{0:T(1024)S(1)}, s32[2048]{0:T(1024)}, u32[]{:S(2)}) copy-start(s32[2048]{0:T(1024)} %param.18) | copy-start | bytes 24580
  22.3 1.6 %collective-permute-start.4 = (f32[6,5,16,128]{3,2,1,0:T(8,128)S(1)}, f32[6,5,16,128]{3,2,1,0:T(8,128)S(1)}, u32[]{:S(2)}, u32[]{:S(2)}) collective-permute-start(f32[6,5,16,128]{3,2,1,0:T(8,128)S(1)} %get-tuple-element.42.refs_0_), channel_id=1, source_target_pairs={{0,8},{8,0},{16,24},{24,16},{1,9},{9,1},{17,25},{25,17},{2,10},{10... | collective-permute-start | bytes 737288 | tf_op jit(solution)/shard_map/ppermute | solution.py:527
  23.9 4.1 %collective-permute-start.5 = (f32[5,16,128]{2,1,0:T(8,128)S(1)}, f32[5,16,128]{2,1,0:T(8,128)S(1)}, u32[]{:S(2)}, u32[]{:S(2)}) collective-permute-start(f32[5,16,128]{2,1,0:T(8,128)S(1)} %get-tuple-element.45), channel_id=1, source_target_pairs={{0,16},{8,24},{16,0},{24,8},{1,17},{9,25},{17,1},{25,9},{2,18},{10... | collective-permute-start | bytes 122888 | tf_op jit(solution)/shard_map/ppermute | solution.py:527
  44.3 1.3 %collective-permute-start.6 = (f32[128,128]{1,0:T(8,128)S(1)}, f32[128,128]{1,0:T(8,128)S(1)}, u32[]{:S(2)}, u32[]{:S(2)}) collective-permute-start(f32[128,128]{1,0:T(8,128)S(1)} %node_sums.1), channel_id=1, source_target_pairs={{0,8},{8,0},{16,24},{24,16},{1,9},{9,1},{17,25},{25,17},{2,10},{10... | collective-permute-start | bytes 196616 | tf_op jit(solution)/shard_map/ppermute | solution.py:560
